TPU v7x, 32 devices: a whole 2x2x4 slice. The times are simulated.
32 devices in a mesh: wide: 8 (over y, x, core), narrow: 4 (over z).
Axes of the slice: x: 2, y: 2, z: 4, core: 2. Of those that a mesh axis runs over, the one named last changes fastest.
Arguments:
- tokens: bfloat16 [64, 208, 768], P('wide'), may hold values from -6 to 6
- grid_shape: int32 [64, 2], P('wide'), may hold values from 8 to 24, as said below
- first_gain: bfloat16 [768], replicated, may hold values from 0.5 to 1.5
- first_shift: bfloat16 [768], replicated, may hold values from -1.1953125 to 1.1953125
- qkv_weight: bfloat16 [3, 768, 768], P(None, None, 'narrow'), may hold values from -0.21875 to 0.21875
- query_bias: bfloat16 [768], P('narrow'), may hold values from -1.796875 to 1.796875
- value_bias: bfloat16 [768], P('narrow'), may hold values from -0.59765625 to 0.59765625
- rel_table: bfloat16 [12, 2212], P('narrow'), may hold values from -5 to 5
- proj_weight: bfloat16 [768, 768], P('narrow'), may hold values from -1.25 to 1.25
- proj_bias: bfloat16 [768], replicated, may hold values from -1.796875 to 1.796875
- attn_scale: bfloat16 [768], replicated, may hold values from 0.25 to 1.75
- second_gain: bfloat16 [768], replicated, may hold values from 0.5 to 1.5
- second_shift: bfloat16 [768], replicated, may hold values from -1.1953125 to 1.1953125
- up_weight: bfloat16 [768, 3072], P(None, 'narrow'), may hold values from -0.21875 to 0.21875
- up_bias: bfloat16 [3072], P('narrow'), may hold values from -3 to 3
- down_weight: bfloat16 [3072, 768], P('narrow'), may hold values from -0.15625 to 0.15625
- down_bias: bfloat16 [768], replicated, may hold values from -1.796875 to 1.796875
- mlp_scale: bfloat16 [768], replicated, may hold values from 0.25 to 1.75
- cotangent: bfloat16 [64, 208, 768], P('wide'), may hold values from -6 to 6
Outputs:
- layer_out: bfloat16 [64, 208, 768], P('wide')
- tokens_grad: float32 [64, 208, 768], P('wide')
- first_gain_grad: float32 [768], replicated
- first_shift_grad: float32 [768], replicated
- qkv_weight_grad: float32 [3, 768, 768], P(None, None, 'narrow')
- query_bias_grad: float32 [768], P('narrow')
- value_bias_grad: float32 [768], P('narrow')
- rel_table_grad: float32 [12, 2212], P('narrow')
- proj_weight_grad: float32 [768, 768], P('narrow')
- proj_bias_grad: float32 [768], replicated
- attn_scale_grad: float32 [768], replicated
- second_gain_grad: float32 [768], replicated
- second_shift_grad: float32 [768], replicated
- up_weight_grad: float32 [768, 3072], P(None, 'narrow')
- up_bias_grad: float32 [3072], P('narrow')
- down_weight_grad: float32 [3072, 768], P('narrow')
- down_bias_grad: float32 [768], replicated
- mlp_scale_grad: float32 [768], replicated
Inputs may be any that keep to these rules, and one draw needn't show every extreme that they name: `grid_shape`: each row is (height, width) of one image's patch grid, one of 14 x 14, 10 x 20, 20 x 10, 8 x 24, 24 x 8, 12 x 16, 16 x 12, 13 x 15; each of these occurs in every draw.
All inputs are finite; a program needn't handle non-finite values.
Results may differ from a plain program's by a relative error of at most 0.013.
Values sent between devices are 32-bit elements; how exact they have to be, the bound alone decides.
A program may use at most 384 MiB of HBM per device.

v0:
```python
import jax
import jax.numpy as jnp
from jax import lax
from jax.sharding import PartitionSpec as P

HD = 64
MAXG = 24


EPSILON = 1e-06
NEG_LARGE = -1000000000.0
INV_ROOT_TWO = 0.7071067811865476
INV_ROOT_TWO_PI = 0.3989422804014327


def slot_layout(grid_shape, slot_count):
    slot_ids = jnp.arange(slot_count, dtype=jnp.int32)
    patch_ids = slot_ids - 1
    grid_height = grid_shape[:, 0:1]
    grid_width = grid_shape[:, 1:2]
    is_valid = slot_ids[None, :] <= grid_height * grid_width
    row_place = jnp.floor_divide(patch_ids[None, :], grid_width)
    col_place = patch_ids[None, :] - row_place * grid_width
    span_size = 2 * MAXG - 1
    row_delta = row_place[:, :, None] - row_place[:, None, :] + (MAXG - 1)
    col_delta = col_place[:, :, None] - col_place[:, None, :] + (MAXG - 1)
    pair_index = row_delta * span_size + col_delta
    is_patch = jnp.logical_and(slot_ids[None, :] >= 1, is_valid)
    is_class = jnp.broadcast_to(slot_ids[None, :] == 0, is_patch.shape)
    both_patch = jnp.logical_and(is_patch[:, :, None], is_patch[:, None, :])
    class_query = jnp.logical_and(is_class[:, :, None], is_patch[:, None, :])
    class_key = jnp.logical_and(is_patch[:, :, None], is_class[:, None, :])
    last_entry = span_size * span_size
    pair_index = jnp.where(
        both_patch,
        pair_index,
        jnp.where(class_query, last_entry, jnp.where(class_key, last_entry + 1, last_entry + 2)),
    )
    return (pair_index, is_valid)


def norm_stats(values):
    centre = jnp.mean(values, axis=1, keepdims=True)
    centred = values - centre
    inv_root = lax.rsqrt(jnp.mean(centred * centred, axis=1, keepdims=True) + EPSILON)
    return (centred * inv_root, inv_root)


def norm_back(incoming, normed, inv_root, gain):
    scaled = incoming * gain
    return inv_root * (
        scaled
        - jnp.mean(scaled, axis=1, keepdims=True)
        - normed * jnp.mean(scaled * normed, axis=1, keepdims=True)
    )


def gelu_exact(inputs):
    return 0.5 * inputs * (1.0 + lax.erf(inputs * INV_ROOT_TWO))


def gelu_slope(inputs):
    return (
        0.5 * (1.0 + lax.erf(inputs * INV_ROOT_TWO))
        + inputs * jnp.exp(-0.5 * inputs * inputs) * INV_ROOT_TWO_PI
    )


def body(
    tokens,
    grid_shape,
    first_gain,
    first_shift,
    qkv_weight,
    query_bias,
    value_bias,
    rel_table,
    proj_weight,
    proj_bias,
    attn_scale,
    second_gain,
    second_shift,
    up_weight,
    up_bias,
    down_weight,
    down_bias,
    mlp_scale,
    cotangent,
):
    float_type = jnp.float32
    brain_type = jnp.bfloat16
    images, slot_count, model_width = tokens.shape
    local_heads, table_size = rel_table.shape
    head_size = HD
    local_width = local_heads * head_size
    total_rows = images * slot_count
    head_split = (images, slot_count, local_heads, head_size)
    query_scale = head_size ** (-0.5)
    pair_index, is_valid = slot_layout(grid_shape, slot_count)
    key_open = is_valid[:, None, None, :]
    table_f = rel_table.astype(float_type)
    table_bias = jnp.transpose(jnp.take(table_f, pair_index, axis=1), (1, 0, 2, 3))
    first_gain_f = first_gain.astype(float_type)
    second_gain_f = second_gain.astype(float_type)
    attn_scale_f = attn_scale.astype(float_type)
    mlp_scale_f = mlp_scale.astype(float_type)
    flat_in = tokens.reshape(total_rows, model_width).astype(float_type)
    normed_one, inv_one = norm_stats(flat_in)
    first_in = (normed_one * first_gain_f + first_shift.astype(float_type)).astype(brain_type)
    projected = jnp.einsum("rd,cde->cre", first_in, qkv_weight, preferred_element_type=float_type)
    queries = ((projected[0] + query_bias.astype(float_type)) * query_scale).astype(brain_type)
    keys_low = projected[1].astype(brain_type)
    values_low = (projected[2] + value_bias.astype(float_type)).astype(brain_type)
    query_heads = queries.reshape(head_split)
    key_heads = keys_low.reshape(head_split)
    value_heads = values_low.reshape(head_split)

    def attention_scores():
        raw_scores = jnp.einsum(
            "ishd,ithd->ihst", query_heads, key_heads, preferred_element_type=float_type
        )
        return jnp.where(key_open, raw_scores + table_bias, NEG_LARGE)

    scores = attention_scores()
    row_top = jnp.max(scores, axis=-1, keepdims=True)
    log_total = row_top + jnp.log(jnp.sum(jnp.exp(scores - row_top), axis=-1, keepdims=True))
    probs_low = jnp.exp(scores - log_total).astype(brain_type)
    attended = jnp.einsum(
        "ihst,ithd->ishd", probs_low, value_heads, preferred_element_type=float_type
    )
    attended = attended.reshape(total_rows, local_width).astype(brain_type)
    attn_part = jnp.dot(attended, proj_weight, preferred_element_type=float_type)
    attn_branch = lax.psum(attn_part, "narrow") + proj_bias.astype(float_type)
    middle = flat_in + attn_scale_f * attn_branch
    normed_two, inv_two = norm_stats(middle)
    second_in = (normed_two * second_gain_f + second_shift.astype(float_type)).astype(brain_type)
    up_pre = jnp.dot(second_in, up_weight, preferred_element_type=float_type) + up_bias.astype(
        float_type
    )
    hidden_low = gelu_exact(up_pre).astype(brain_type)
    down_part = jnp.dot(hidden_low, down_weight, preferred_element_type=float_type)
    mlp_branch = lax.psum(down_part, "narrow") + down_bias.astype(float_type)
    layer_out = (
        (middle + mlp_scale_f * mlp_branch)
        .astype(brain_type)
        .reshape(images, slot_count, model_width)
    )
    out_grad = cotangent.reshape(total_rows, model_width).astype(float_type) * is_valid.reshape(
        total_rows, 1
    ).astype(float_type)
    mlp_scale_grad = jnp.sum(out_grad * mlp_branch, axis=0)
    down_bias_grad = jnp.sum(out_grad, axis=0) * mlp_scale_f
    branch_low = (out_grad * mlp_scale_f).astype(brain_type)
    down_weight_grad = jnp.einsum(
        "rf,rd->fd", hidden_low, branch_low, preferred_element_type=float_type
    )
    hidden_grad = jnp.einsum(
        "rd,fd->rf", branch_low, down_weight, preferred_element_type=float_type
    )
    pre_low = (hidden_grad * gelu_slope(up_pre)).astype(brain_type)
    up_bias_grad = jnp.sum(pre_low.astype(float_type), axis=0)
    up_weight_grad = jnp.einsum("rd,rf->df", second_in, pre_low, preferred_element_type=float_type)
    second_part = jnp.einsum("rf,df->rd", pre_low, up_weight, preferred_element_type=float_type)
    second_grad = lax.psum(second_part, "narrow")
    second_gain_grad = jnp.sum(second_grad * normed_two, axis=0)
    second_shift_grad = jnp.sum(second_grad, axis=0)
    middle_grad = out_grad + norm_back(second_grad, normed_two, inv_two, second_gain_f)
    attn_scale_grad = jnp.sum(middle_grad * attn_branch, axis=0)
    proj_bias_grad = jnp.sum(middle_grad, axis=0) * attn_scale_f
    attn_low = (middle_grad * attn_scale_f).astype(brain_type)
    proj_weight_grad = jnp.einsum(
        "re,rd->ed", attended, attn_low, preferred_element_type=float_type
    )
    attended_grad = (
        jnp.einsum("rd,ed->re", attn_low, proj_weight, preferred_element_type=float_type)
        .astype(brain_type)
        .reshape(head_split)
    )
    probs_again = jnp.exp(attention_scores() - log_total)
    probs_again_low = probs_again.astype(brain_type)
    prob_grad = jnp.einsum(
        "ishd,ithd->ihst", attended_grad, value_heads, preferred_element_type=float_type
    )
    value_grad = jnp.einsum(
        "ihst,ishd->ithd", probs_again_low, attended_grad, preferred_element_type=float_type
    ).astype(brain_type)
    row_inner = jnp.sum(probs_again * prob_grad, axis=-1, keepdims=True)
    score_grad = probs_again * (prob_grad - row_inner)
    flat_index = pair_index.reshape(-1)
    head_major = jnp.transpose(score_grad, (1, 0, 2, 3)).reshape(local_heads, -1)
    rel_table_grad = jax.vmap(
        lambda entries: jax.ops.segment_sum(entries, flat_index, num_segments=table_size)
    )(head_major)
    score_low = score_grad.astype(brain_type)
    query_grad = jnp.einsum(
        "ihst,ithd->ishd", score_low, key_heads, preferred_element_type=float_type
    ).astype(brain_type) * jnp.asarray(query_scale, brain_type)
    key_grad = jnp.einsum(
        "ihst,ishd->ithd", score_low, query_heads, preferred_element_type=float_type
    ).astype(brain_type)
    query_grad = query_grad.reshape(total_rows, local_width)
    key_grad = key_grad.reshape(total_rows, local_width)
    value_grad = value_grad.reshape(total_rows, local_width)
    query_bias_grad = jnp.sum(query_grad.astype(float_type), axis=0)
    value_bias_grad = jnp.sum(value_grad.astype(float_type), axis=0)
    stacked_grads = jnp.stack([query_grad, key_grad, value_grad])
    qkv_weight_grad = jnp.einsum(
        "rd,cre->cde", first_in, stacked_grads, preferred_element_type=float_type
    )
    first_part = jnp.einsum(
        "cre,cde->rd", stacked_grads, qkv_weight, preferred_element_type=float_type
    )
    first_grad = lax.psum(first_part, "narrow")
    first_gain_grad = jnp.sum(first_grad * normed_one, axis=0)
    first_shift_grad = jnp.sum(first_grad, axis=0)
    tokens_grad = (middle_grad + norm_back(first_grad, normed_one, inv_one, first_gain_f)).reshape(
        images, slot_count, model_width
    )
    (
        first_gain_grad,
        first_shift_grad,
        qkv_weight_grad,
        query_bias_grad,
        value_bias_grad,
        rel_table_grad,
        proj_weight_grad,
        proj_bias_grad,
        attn_scale_grad,
        second_gain_grad,
        second_shift_grad,
        up_weight_grad,
        up_bias_grad,
        down_weight_grad,
        down_bias_grad,
        mlp_scale_grad,
    ) = lax.psum(
        (
            first_gain_grad,
            first_shift_grad,
            qkv_weight_grad,
            query_bias_grad,
            value_bias_grad,
            rel_table_grad,
            proj_weight_grad,
            proj_bias_grad,
            attn_scale_grad,
            second_gain_grad,
            second_shift_grad,
            up_weight_grad,
            up_bias_grad,
            down_weight_grad,
            down_bias_grad,
            mlp_scale_grad,
        ),
        "wide",
    )
    return (
        layer_out,
        tokens_grad,
        first_gain_grad,
        first_shift_grad,
        qkv_weight_grad,
        query_bias_grad,
        value_bias_grad,
        rel_table_grad,
        proj_weight_grad,
        proj_bias_grad,
        attn_scale_grad,
        second_gain_grad,
        second_shift_grad,
        up_weight_grad,
        up_bias_grad,
        down_weight_grad,
        down_bias_grad,
        mlp_scale_grad,
    )


def solution(mesh):
    return jax.shard_map(
        body,
        mesh=mesh,
        in_specs=(
            P("wide", None, None),
            P("wide", None),
            P(),
            P(),
            P(None, None, "narrow"),
            P("narrow"),
            P("narrow"),
            P("narrow", None),
            P("narrow", None),
            P(),
            P(),
            P(),
            P(),
            P(None, "narrow"),
            P("narrow"),
            P("narrow", None),
            P(),
            P(),
            P("wide", None, None),
        ),
        out_specs=(
            P("wide", None, None),
            P("wide", None, None),
            P(),
            P(),
            P(None, None, "narrow"),
            P("narrow"),
            P("narrow"),
            P("narrow", None),
            P("narrow", None),
            P(),
            P(),
            P(),
            P(),
            P(None, "narrow"),
            P("narrow"),
            P("narrow", None),
            P(),
            P(),
        ),
        check_vma=False,
    )
```

profile of v0, /device:TPU:1, one launch (start us, length us, event | category | flops | bytes accessed | tf_op | source)
XLA Modules:
  0.0 3936.5 jit_solution(91646839557959551)
XLA Ops:
  25.9 3.4 reshape.864
  34.3 3.5 squeeze.7
  37.8 3.2 squeeze.8
  41.0 1253.0 %gather_fusion = f32[346112,3]{1,0:T(8,128)} fusion(f32[3,2212]{0,1:T(8,128)S(1)} %copy.53, s32[346112]{0:T(1024)} %broadcast_clamp_fusion), kind=kCustom, calls=%fused_computation | custom fusion | bytes 9691136 | tf_op jit(solution)/shard_map/jit(_take)/gather | solution.py:102
  1294.0 102.1 %copy.55 = f32[8,208,208,3]{1,2,3,0:T(8,128)} copy(f32[8,208,208,3]{3,2,1,0:T(8,128)} %bitcast.9) | data formatting | bytes 8306688 | tf_op jit(solution)/shard_map/jit(_take)/gather | solution.py:102
  1396.1 5.7 fusion.61
  1408.8 4.1 fusion.65
  1413.8 3.9 multiply_convert_fusion.2
  1417.6 182.2 %all-reduce.8.cloned.1.call-done = f32[1664,768]{1,0:T(8,128)} async-done(((f32[1664,768]{1,0:T(8,128)}), f32[1664,768]{1,0:T(8,128)}) %all-reduce.8.cloned.1.call-update) | async-done | bytes 5111824 | tf_op jit(solution)/shard_map/psum | solution.py:133
  1599.9 4.2 fusion.60
  1607.5 6.7 multiply_convert_fusion.3
  1614.2 4.7 convert_reduce_fusion.1
  1620.4 4.4 fusion.67
  1626.1 6.2 fusion.66
  1632.3 176.4 %all-reduce.10.cloned.1.call-done = f32[1664,768]{1,0:T(8,128)} async-done(((f32[1664,768]{1,0:T(8,128)}), f32[1664,768]{1,0:T(8,128)}) %all-reduce.10.cloned.1.call-update) | async-done | bytes 5111824 | tf_op jit(solution)/shard_map/psum | solution.py:164
  1808.6 5.3 multiply_reduce_fusion.2
  1814.8 6.0 multiply_reduce_fusion.3
  1827.5 3.7 convert_reduce_fusion.2
  1831.3 4.3 multiply_reduce_fusion.4
  1849.5 4.4 convolution_bitcast_fusion
  1862.2 5.7 fusion.69
  1867.9 3.8 fusion.68
  1871.9 4.1 fusion.39
  1880.0 8.8 fusion.6
  1888.8 6.2 copy.67
  1895.0 10.1 reshape.871
  1905.1 76.8 %copy.68 = f32[346112,3]{1,0:T(8,128)} copy(f32[346112,3]{0,1:T(4,128)} %bitcast.148) | data formatting | bytes 8306688 | tf_op jit(solution)/shard_map/reshape | solution.py:190
  1982.0 1861.4 %scatter_custom_fusion = f32[3,2212]{0,1:T(8,128)S(1)} fusion(s32[346112]{0:T(1024)S(1)} %reshape.872, f32[346112,3]{1,0:T(8,128)} %copy.68, f32[]{:T(128)} %constant.22.clone.1), kind=kCustom, calls=%fused_computation.92 | custom fusion | flops 1038336 | bytes 27056 | tf_op jit(solution)/shard_map/vmap()/scatter-add | solution.py:192
  3843.5 5.6 fusion.24
  3849.1 4.6 multiply_reduce_fusion
  3853.7 60.1 %all-reduce = (f32[768]{0:T(1024)}, f32[768]{0:T(1024)}, f32[192]{0:T(256)}, f32[192]{0:T(256)}, f32[3,2212]{0,1:T(8,128)S(1)}, /*index=5*/f32[768]{0:T(1024)}, ...) all-reduce(f32[768]{0:T(1024)S(1)} %get-tuple-element.56, ...), channel_id=1, replica_groups=mesh['wide'=8,'narrow'=4] {'wide'}, use_global_device_ids=true, to_apply=%region_16.17 | all-reduce | flops 13932 | bytes 111456 | tf_op jit(solution)/shard_map/psum | solution.py:236
  3914.8 7.1 fusion.23
  (219 shorter events, 79.8 us)
Async XLA Ops:
  7.2 1600.2 %copy-start = (bf16[768,768]{1,0:T(8,128)(2,1)S(1)}, bf16[768,768]{1,0:T(8,128)(2,1)}, u32[]{:S(2)}) copy-start(bf16[768,768]{1,0:T(8,128)(2,1)} %param.32) | copy-start | bytes 3538948
  7.2 1592.7 %all-reduce.8.cloned.1.call-start = ((), (), s32[]{:S(2)}) async-start(), calls=%async_computation | async-start | bytes 10223616 | tf_op jit(solution)/shard_map/psum | solution.py:133
  7.3 7.5 copy-start.45
  7.3 5.0 copy-start.58
  9.5 7.3 copy-start.51
  9.6 7.3 copy-start.52
  9.7 9.9 copy-start.37
  12.9 4.0 copy-start.41
  34.3 1361.8 %copy-start.16 = (bf16[8,208,3,64]{1,0,3,2:T(8,128)(2,1)}, bf16[8,208,3,64]{1,0,3,2:T(8,128)(2,1)S(1)}, u32[]{:S(2)}) copy-start(bf16[8,208,3,64]{1,0,3,2:T(8,128)(2,1)S(1)} %convert_element_type.154) | copy-start | bytes 1916932
  1294.0 102.1 %copy-start.9 = (f32[8,208,3,64]{1,0,3,2:T(8,128)S(1)}, f32[8,208,3,64]{1,0,3,2:T(8,128)}, u32[]{:S(2)}) copy-start(f32[8,208,3,64]{1,0,3,2:T(8,128)} %squeeze.8) | copy-start | bytes 3833860
  1413.0 395.7 %all-reduce.10.cloned.1.call-start = ((), (), s32[]{:S(2)}) async-start(), calls=%async_computation.1 | async-start | bytes 10223616 | tf_op jit(solution)/shard_map/psum | solution.py:164
  1607.4 6.7 copy-start.14
  1607.4 6.7 copy-start.12
  1607.5 6.7 copy-start.61
  1624.8 2218.6 %all-reduce.14.cloned.1.call-start = ((), (), s32[]{:S(2)}) async-start(), calls=%async_computation.3 | async-start | bytes 20447232 | tf_op jit(solution)/shard_map/psum | solution.py:142
  1808.6 5.4 copy-start.6
  1808.6 6.2 copy-start.8
  1814.8 8.2 copy-start.29
  1827.5 8.1 slice-start
  1831.3 4.4 slice-start.1
  1854.0 2067.9 %all-reduce.12.cloned.1.call-start = ((), (), s32[]{:S(2)}) async-start(), calls=%async_computation.2 | async-start | bytes 14155776 | tf_op jit(solution)/shard_map/psum | solution.py:236
  1862.2 5.7 copy-start.15
  1862.2 5.7 copy-start.22
  1871.9 4.1 copy-start.24
  1871.9 4.1 copy-start.36
  1905.1 1938.3 %copy-start.38 = (f32[1664]{0:T(1024)S(1)}, f32[1664]{0:T(1024)}, u32[]{:S(2)}) copy-start(f32[1664]{0:T(1024)} %copy-done.37) | copy-start | bytes 19972
  1905.1 1938.3 %copy-start.40 = (f32[1664]{0:T(1024)S(1)}, f32[1664]{0:T(1024)}, u32[]{:S(2)}) copy-start(f32[1664]{0:T(1024)} %copy-done.39) | copy-start | bytes 19972
  1905.1 1938.3 %copy-start.44 = (f32[768]{0:T(1024)S(1)}, f32[768]{0:T(1024)}, u32[]{:S(2)}) copy-start(f32[768]{0:T(1024)} %copy-done.43) | copy-start | bytes 9220
  3843.4 5.6 copy-start.7
  3843.4 5.6 copy-start.18
  3921.9 3.8 copy-start.28
  3925.6 3.9 copy-start.1
  (39 other events, 72.2 us)
Sparse Core Ops, SparseCore 0:
  1413.1 186.7 all-reduce.7
  1624.9 183.6 all-reduce.9
  1854.1 349.7 all-reduce.13
  2208.6 112.3 all-reduce.11
where the time goes:
time: 3970 us; the launch traced here: 3940 us
  other arithmetic  1930 us (49%)
  local copies, waits for them, and re-layouts  1500 us (38%)
  waiting for transfers between devices  359 us (9%)
  matrix products  68.2 us (2%)
  blocking collectives  60.1 us (2%)
    scatter-add x1, other arithmetic, body(): jax.ops.segment_sum(entries, flat_index, num_segments=table_size)  1860 us
    gather x2, local copies, waits for them, and re-layouts, body(): jnp.take(table_f, pair_index, axis=1)  1360 us
    psum x1, waiting for transfers between devices, body(): attn_branch = lax.psum(attn_part, 'narrow') + proj_bias.astype(float_type)  182 us
    psum x1, waiting for transfers between devices, body(): second_grad = lax.psum(second_part, 'narrow')  176 us
    reshape x2, local copies, waits for them, and re-layouts, body(): jnp.transpose(score_grad, (1, 0, 2, 3)).reshape(local_heads, -1)  86.9 us
  transfers between devices with their start and end apart: 4, of which 2 were waited for; matrix products, arithmetic and copies ran while one was open for 51% of the time, Pallas kernels for 0%

commit v1 on v0

v1 whole, which is shorter than its diff:
```python
import functools

import jax
import jax.numpy as jnp
from jax import lax
from jax.experimental import pallas as pl
from jax.experimental.pallas import tpu as pltpu
from jax.sharding import PartitionSpec as P

HD = 64
MAXG = 24
SPAN = 2 * MAXG - 1
EPSILON = 1e-06
MASKED = -1e30
INV_ROOT_TWO = 0.7071067811865476
INV_ROOT_TWO_PI = 0.3989422804014327
GRIDS = ((14, 14), (10, 20), (20, 10), (8, 24), (24, 8), (12, 16), (16, 12), (13, 15))
DIAG = 512
F32 = jnp.float32
BF16 = jnp.bfloat16
VMEM_LIMIT = 60 * 1024 * 1024


def dot_nn(a, b):
    return lax.dot_general(a, b, (((1,), (0,)), ((), ())), preferred_element_type=F32)


def dot_nt(a, b):
    return lax.dot_general(a, b, (((1,), (1,)), ((), ())), preferred_element_type=F32)


def dot_tn(a, b):
    return lax.dot_general(a, b, (((0,), (0,)), ((), ())), preferred_element_type=F32)


def row_mean(v):
    return jnp.sum(v, axis=-1, keepdims=True) * (1.0 / v.shape[-1])


def norm_stats(v):
    centred = v - row_mean(v)
    inv = lax.rsqrt(row_mean(centred * centred) + EPSILON)
    return centred * inv, inv


def norm_back(incoming, normed, inv, gain):
    scaled = incoming * gain
    return inv * (scaled - row_mean(scaled) - normed * row_mean(scaled * normed))


def fold_rows(v):
    rows = v.shape[0]
    return jnp.sum(v.reshape(rows // 8, 8, v.shape[1]), axis=0)


def windows(shape_at):
    high, wide = GRIDS[shape_at]
    centre = MAXG - 1
    for m in range(-high, high):
        at = 207 + m * wide
        if m > -high:
            yield 0, centre + m, centre, at, wide
        if m < high - 1:
            yield 1, centre + 1 + m, centre + 1 - wide, at + 1, wide - 1


def diag_kernel(table_ref, out_ref):
    out_ref[...] = jnp.zeros_like(out_ref)
    for shape_at in range(len(GRIDS)):
        for which, row, col, at, size in windows(shape_at):
            out_ref[shape_at, which, :, at : at + size] = table_ref[row, :, col : col + size]


def undiag_kernel(diag_ref, out_ref):
    out_ref[...] = jnp.zeros_like(out_ref)
    for shape_at in range(len(GRIDS)):
        for which, row, col, at, size in windows(shape_at):
            out_ref[row, :, col : col + size] += diag_ref[shape_at, which, :, at : at + size]


def slot_masks(high, wide, reverse):
    rows = lax.broadcasted_iota(jnp.int32, (208, 1), 0)
    p = 207 - rows if reverse else rows
    s = lax.broadcasted_iota(jnp.int32, (1, 256), 1)
    limit = high * wide
    wide_f = wide.astype(F32)

    def column(slot):
        patch = (slot - 1).astype(F32)
        return patch - wide_f * jnp.floor((patch + 0.5) / wide_f)

    later = column(s) >= column(p)
    p_patch = (p >= 1) & (p <= limit)
    s_patch = (s >= 1) & (s <= limit)
    return p, s, limit, later, p_patch, s_patch


def load_pieces(pidx_ref, pieces, stage, sems, rows):
    copies = []
    for r, piece in enumerate(pieces):
        at = pl.multiple_of(pidx_ref[r] * rows, 8)
        copies.append(
            pltpu.make_async_copy(piece, stage.at[:, pl.ds(at, rows), :], sems.at[r])
        )
    for copy in copies:
        copy.start()
    return copies


def attention_forward(
    sid_ref, grid_ref, pidx_ref, tok_ref, gain_ref, shift_ref, qb_ref, vb_ref, pb_ref, own_ref, diag_ref, cls_ref,
    *rest,
):
    pieces = rest[:8]
    q_ref, k_ref, v_ref, prob_ref, att_ref, branch_ref, wa_ref = rest[8:15]
    stage, k_pad, v_pad, sems = rest[15:]
    image = pl.program_id(0)

    @pl.when(image == 0)
    def _():
        copies = load_pieces(pidx_ref, pieces, stage, sems, 96)
        k_pad[208:256, :] = jnp.zeros((48, 768), BF16)
        v_pad[208:256, :] = jnp.zeros((48, 768), BF16)
        for part in range(4):
            wa_ref[part, 0:192, :] = own_ref[part * 192 : (part + 1) * 192, :]
        for copy in copies:
            copy.wait()
        for slot in range(3):
            for part in range(4):
                wa_ref[part, (slot + 1) * 192 : (slot + 2) * 192, :] = stage[
                    slot, part * 192 : (part + 1) * 192, :
                ].astype(BF16)

    normed, _ = norm_stats(tok_ref[0].astype(F32))
    first_in = (normed * gain_ref[...] + shift_ref[...]).astype(BF16)
    q_ref[0] = ((dot_nt(first_in, wa_ref[0]) + qb_ref[...]) * (HD ** -0.5)).astype(BF16)
    keys = dot_nt(first_in, wa_ref[1]).astype(BF16)
    k_ref[0] = keys
    k_pad[0:208, :] = keys
    values = (dot_nt(first_in, wa_ref[2]) + vb_ref[...]).astype(BF16)
    v_ref[0] = values
    v_pad[0:208, :] = values

    p, s, limit, later, p_patch, s_patch = slot_masks(grid_ref[image, 0], grid_ref[image, 1], False)
    both = p_patch & s_patch
    open_key = s <= limit
    head_of = lax.broadcasted_iota(jnp.int32, (1, 256), 1) // HD

    @pl.loop(0, 3)
    def _(group):
        lanes = pl.ds(pl.multiple_of(group * 256, 256), 256)
        q_group = q_ref[0, :, lanes]
        k_group = k_pad[:, lanes]
        v_group = v_pad[:, lanes]
        stacked = jnp.concatenate(
            [jnp.where(head_of == h, q_group, jnp.zeros_like(q_group)) for h in range(4)], axis=0
        )
        raw = dot_nt(stacked, k_group)
        probs = []
        for h in range(4):
            head = group * 4 + h
            f0 = diag_ref[0, 0, pl.ds(head, 1), :]
            f1 = diag_ref[0, 1, pl.ds(head, 1), :]
            toep0 = pltpu.roll(jnp.broadcast_to(f0, (208, DIAG)), DIAG - 207, 1, stride=1, stride_axis=0)[:, :256]
            toep1 = pltpu.roll(jnp.broadcast_to(f1, (208, DIAG)), DIAG - 207, 1, stride=1, stride_axis=0)[:, :256]
            c0, c1, c2 = cls_ref[head, 0], cls_ref[head, 1], cls_ref[head, 2]
            outer = jnp.where((p == 0) & s_patch, c0, jnp.where(p_patch & (s == 0), c1, c2))
            bias = jnp.where(both, jnp.where(later, toep0, toep1), outer)
            scores = jnp.where(open_key, raw[h * 208 : (h + 1) * 208, :] + bias, MASKED)
            top = jnp.max(scores, axis=-1, keepdims=True)
            raised = jnp.exp(scores - top)
            prob = (raised * (1.0 / jnp.sum(raised, axis=-1, keepdims=True))).astype(BF16)
            prob_ref[0, head] = prob
            probs.append(prob)
        mixed = dot_nn(jnp.concatenate(probs, axis=0), v_group)
        out = mixed[0:208]
        for h in range(1, 4):
            out = jnp.where(head_of == h, mixed[h * 208 : (h + 1) * 208], out)
        att_ref[0, :, lanes] = out.astype(BF16)

    branch_ref[0] = dot_nn(att_ref[0], wa_ref[3]) + pb_ref[...]


def feed_forward(
    grid_ref, pidx_ref, tok_ref, branch_ref, cot_ref, vec_ref, ub_ref, ownb_ref, ownc_ref, *rest
):
    pieces_b, pieces_c = rest[:8], rest[8:16]
    out_ref, mg_ref, gb_ref, gc_ref, sums_ref = rest[16:21]
    stage, wb, wc, mlp_acc, second_acc, sems = rest[21:]
    image = pl.program_id(0)

    @pl.when(image == 0)
    def _():
        for own_ref, pieces, weights in ((ownb_ref, pieces_b, wb), (ownc_ref, pieces_c, wc)):
            copies = load_pieces(pidx_ref, pieces, stage, sems, 96)
            weights[0] = own_ref[...]
            for copy in copies:
                copy.wait()
            for slot in range(3):
                weights[slot + 1] = stage[slot].astype(BF16)
        gb_ref[...] = jnp.zeros_like(gb_ref)
        gc_ref[...] = jnp.zeros_like(gc_ref)
        sums_ref[...] = jnp.zeros_like(sums_ref)

    attn_scale, second_gain, second_shift, mlp_scale, down_bias = (vec_ref[i : i + 1, :] for i in range(5))
    branch = branch_ref[0]
    middle = tok_ref[0].astype(F32) + attn_scale * branch
    normed, inv = norm_stats(middle)
    second_in = (normed * second_gain + second_shift).astype(BF16)
    valid = lax.broadcasted_iota(jnp.int32, (208, 1), 0) <= grid_ref[image, 0] * grid_ref[image, 1]
    out_grad = jnp.where(valid, cot_ref[0].astype(F32), 0.0)
    branch_low = (out_grad * mlp_scale).astype(BF16)
    mlp_acc[...] = jnp.zeros_like(mlp_acc)
    second_acc[...] = jnp.zeros_like(second_acc)

    @pl.loop(0, 4)
    def _(slot):
        up_pre = dot_nn(second_in, wb[slot]) + ub_ref[pl.ds(slot, 1), :]
        cdf = 0.5 * (1.0 + lax.erf(up_pre * INV_ROOT_TWO))
        hidden = (up_pre * cdf).astype(BF16)
        slope = cdf + up_pre * jnp.exp(-0.5 * up_pre * up_pre) * INV_ROOT_TWO_PI
        mlp_acc[...] += dot_nn(hidden, wc[slot])
        pre_low = (dot_nt(branch_low, wc[slot]) * slope).astype(BF16)
        second_acc[...] += dot_nt(pre_low, wb[slot])

        @pl.when(slot == 0)
        def _():
            gc_ref[...] += dot_tn(hidden, branch_low)
            gb_ref[...] += dot_tn(second_in, pre_low)
            sums_ref[6] += fold_rows(pre_low.astype(F32))

    mlp_branch = mlp_acc[...] + down_bias
    out_ref[0] = (middle + mlp_scale * mlp_branch).astype(BF16)
    second_grad = second_acc[...]
    middle_grad = out_grad + norm_back(second_grad, normed, inv, second_gain)
    mg_ref[0] = middle_grad
    sums_ref[0] += fold_rows(out_grad * mlp_branch)
    sums_ref[1] += fold_rows(out_grad)
    sums_ref[2] += fold_rows(second_grad * normed)
    sums_ref[3] += fold_rows(second_grad)
    sums_ref[4] += fold_rows(middle_grad * branch)
    sums_ref[5] += fold_rows(middle_grad)


def attention_backward(
    sid_ref, grid_ref, tok_ref, mg_ref, att_ref, q_ref, k_ref, v_ref, prob_ref, vec_ref, wa_ref,
    tg_ref, ga_ref, sums_ref, diag_ref, cls_ref,
    k_pad, v_pad, dq, dk, dv,
):
    image = pl.program_id(0)

    @pl.when(image == 0)
    def _():
        k_pad[208:256, :] = jnp.zeros((48, 768), BF16)
        v_pad[208:256, :] = jnp.zeros((48, 768), BF16)
        ga_ref[...] = jnp.zeros_like(ga_ref)
        sums_ref[...] = jnp.zeros_like(sums_ref)
        diag_ref[...] = jnp.zeros_like(diag_ref)
        cls_ref[...] = jnp.zeros_like(cls_ref)

    k_pad[0:208, :] = k_ref[0]
    v_pad[0:208, :] = v_ref[0]
    attn_scale, first_gain, first_shift = (vec_ref[i : i + 1, :] for i in range(3))
    middle_grad = mg_ref[0]
    attn_low = (middle_grad * attn_scale).astype(BF16)
    attended_grad = dot_nt(attn_low, wa_ref[3]).astype(BF16)
    ga_ref[576:768, :] += dot_tn(att_ref[0], attn_low)[0:192, :]

    p, s, limit, later, p_patch, s_patch = slot_masks(grid_ref[image, 0], grid_ref[image, 1], True)
    both = p_patch & s_patch
    flip = (
        lax.broadcasted_iota(jnp.int32, (208, 208), 0) + lax.broadcasted_iota(jnp.int32, (208, 208), 1) == 207
    ).astype(BF16)
    head_of = lax.broadcasted_iota(jnp.int32, (1, 256), 1) // HD

    for group in range(3):
        lanes = slice(group * 256, group * 256 + 256)
        k_group, v_group = k_pad[:, lanes], v_pad[:, lanes]
        q_group = q_ref[0, :, lanes]
        g_group = attended_grad[:, lanes]
        q_stack = jnp.concatenate(
            [jnp.where(head_of == h, q_group, jnp.zeros_like(q_group)) for h in range(4)], axis=0
        )
        g_stack = jnp.concatenate(
            [jnp.where(head_of == h, g_group, jnp.zeros_like(g_group)) for h in range(4)], axis=0
        )
        prob_grads = dot_nt(g_stack, v_group)
        lows = []
        for h in range(4):
            prob = prob_ref[0, group * 4 + h].astype(F32)
            prob_grad = prob_grads[h * 208 : (h + 1) * 208]
            inner = jnp.sum(prob * prob_grad, axis=-1, keepdims=True)
            score_grad = prob * (prob_grad - inner)
            low = score_grad.astype(BF16)
            lows.append(low)
            if group == 0 and h < 3:
                rest = (score_grad - low.astype(F32)).astype(BF16)
                turned = dot_nn(flip, low) + dot_nn(flip, rest)
                patches = jnp.where(both, turned, 0.0)
                edge = turned - patches
                parts = [jnp.where(later, patches, 0.0), jnp.where(later, 0.0, patches)]
                for which in range(2):
                    wide = jnp.concatenate([parts[which], jnp.zeros((208, 256), F32)], axis=1)
                    lined = pltpu.roll(wide, 0, 1, stride=1, stride_axis=0)
                    diag_ref[pl.ds(sid_ref[image], 1), which, h] += fold_rows(lined)[None]
                class_query = jnp.where((p == 0) & s_patch, edge, 0.0)
                class_key = jnp.where(p_patch & (s == 0), edge, 0.0)
                cls_ref[0, h] += fold_rows(class_query)
                cls_ref[1, h] += fold_rows(class_key)
                cls_ref[2, h] += fold_rows(edge - class_query - class_key)
        low_stack = jnp.concatenate(lows, axis=0)
        mixed = dot_nn(low_stack, k_group)
        out = mixed[0:208]
        for h in range(1, 4):
            out = jnp.where(head_of == h, mixed[h * 208 : (h + 1) * 208], out)
        dq[:, lanes] = out.astype(BF16) * jnp.asarray(HD ** -0.5, BF16)
        dk[:, lanes] = dot_tn(low_stack, q_stack)[0:208].astype(BF16)
        prob_stack = jnp.concatenate([prob_ref[0, group * 4 + h] for h in range(4)], axis=0)
        dv[:, lanes] = dot_tn(prob_stack, g_stack)[0:208].astype(BF16)

    normed, inv = norm_stats(tok_ref[0].astype(F32))
    first_in = (normed * first_gain + first_shift).astype(BF16)
    for c, grad in enumerate((dq, dk, dv)):
        ga_ref[c * 192 : (c + 1) * 192, :] += dot_tn(grad[:, 0:256], first_in)[0:192, :]
    first_grad = dot_nn(dq[...], wa_ref[0]) + dot_nn(dk[...], wa_ref[1]) + dot_nn(dv[...], wa_ref[2])
    tg_ref[0] = middle_grad + norm_back(first_grad, normed, inv, first_gain)
    sums_ref[0] += fold_rows(first_grad * normed)
    sums_ref[1] += fold_rows(first_grad)
    sums_ref[2] += fold_rows(dq[...].astype(F32))
    sums_ref[3] += fold_rows(dv[...].astype(F32))


def make_body(wide_size, narrow_size):
    def shift(value, steps):
        return lax.ppermute(value, "narrow", [(i, (i - steps) % narrow_size) for i in range(narrow_size)])

    def swap(value, partner):
        return lax.ppermute(value, "wide", [(j, partner(j)) for j in range(wide_size)])

    def gather_rows(own, me):
        rows = own.shape[0] // wide_size
        mine = lax.dynamic_slice_in_dim(own, me * rows, rows, axis=0).astype(F32)
        across = jnp.stack([shift(mine, k) for k in range(1, narrow_size)])
        if wide_size != 8:
            full = lax.all_gather(across, "wide", axis=1, tiled=True)
            step = own.shape[0] // 8
            return [lax.dynamic_slice_in_dim(full, ((me % 8) ^ r) * step, step, axis=1) for r in range(8)]
        one = swap(across, lambda j: j ^ 2 if j % 2 == 0 else j ^ 4)
        two = swap(across, lambda j: j ^ 4 if j % 2 == 0 else j ^ 2)
        three = swap(one, lambda j: j ^ 4 if j % 2 == 0 else j ^ 2)
        held = [across, one, two, three]
        return held + [swap(value, lambda j: j ^ 1) for value in held]

    def piece_places(me):
        if wide_size != 8:
            return jnp.stack([(me % 8) ^ r for r in range(8)]).astype(jnp.int32)
        core = me % 2
        first, second = jnp.where(core == 0, 2, 4), jnp.where(core == 0, 4, 2)
        there = me ^ 1
        return jnp.stack(
            [me, me ^ first, me ^ second, me ^ 6, there, there ^ second, there ^ first, there ^ 6]
        ).astype(jnp.int32)

    def body(
        tokens, grid_shape, first_gain, first_shift, qkv_weight, query_bias, value_bias, rel_table, proj_weight,
        proj_bias, attn_scale, second_gain, second_shift, up_weight, up_bias, down_weight, down_bias, mlp_scale,
        cotangent,
    ):
        images, slots, width = tokens.shape
        heads, table_size = rel_table.shape
        local = heads * HD
        me = lax.axis_index("wide")
        places = piece_places(me)

        own_a = jnp.concatenate(
            [jnp.transpose(qkv_weight, (0, 2, 1)).reshape(3 * local, width), proj_weight], axis=0
        )
        small = jnp.concatenate(
            [rel_table.astype(F32).reshape(-1)] + [v.astype(F32) for v in (query_bias, value_bias, up_bias)]
        )
        count = small.shape[0]
        small = jnp.pad(small, (0, 8192 - count)).reshape(64, 128)
        smalls = jnp.stack([small] + [shift(small, k) for k in range(1, narrow_size)]).reshape(narrow_size, -1)
        table = smalls[:, : heads * table_size].reshape(narrow_size * heads, table_size)
        at = heads * table_size
        q_bias = smalls[:, at : at + local].reshape(1, width)
        v_bias = smalls[:, at + local : at + 2 * local].reshape(1, width)
        u_bias = smalls[:, at + 2 * local : count]

        pieces_a = gather_rows(own_a, me)
        pieces_b = gather_rows(up_weight, me)
        pieces_c = gather_rows(down_weight, me)

        all_heads = narrow_size * heads
        cls = table[:, SPAN * SPAN :]
        square = table[:, : SPAN * SPAN].reshape(all_heads, SPAN, SPAN)[:, ::-1, ::-1]
        square = jnp.pad(jnp.transpose(square, (1, 0, 2)), ((0, 0), (0, 16 - all_heads), (0, 128 - SPAN)))
        diag = pl.pallas_call(
            diag_kernel, out_shape=jax.ShapeDtypeStruct((len(GRIDS), 2, 16, DIAG), F32), name="diag"
        )(square)

        kinds = jnp.array(GRIDS, jnp.int32)
        sid = jnp.argmax(jnp.all(grid_shape[:, None, :] == kinds[None], axis=-1), axis=-1).astype(jnp.int32)

        def row(v):
            return v.astype(F32).reshape(1, -1)

        smem = pl.BlockSpec(memory_space=pltpu.SMEM)
        anyspace = pl.BlockSpec(memory_space=pl.ANY)

        def whole(*shape):
            return pl.BlockSpec(shape, lambda i, *_: (0,) * len(shape))

        def per_image(*shape):
            return pl.BlockSpec((1,) + shape, lambda i, *_: (i,) + (0,) * len(shape))

        def struct(*shape, dtype=F32):
            return jax.ShapeDtypeStruct(shape, dtype)

        params = pltpu.CompilerParams(vmem_limit_bytes=VMEM_LIMIT, dimension_semantics=("arbitrary",))
        queries, keys, values, probs, attended, branch, weights_a = pl.pallas_call(
            attention_forward,
            grid_spec=pltpu.PrefetchScalarGridSpec(
                num_scalar_prefetch=3,
                grid=(images,),
                in_specs=[per_image(slots, width)]
                + [whole(1, width)] * 5
                + [
                    whole(width, width),
                    pl.BlockSpec((1, 2, 16, DIAG), lambda i, sid_ref, *_: (sid_ref[i], 0, 0, 0)),
                    smem,
                ]
                + [anyspace] * 8,
                out_specs=[per_image(slots, width)] * 3
                + [per_image(all_heads, slots, 256), per_image(slots, width), per_image(slots, width)]
                + [whole(4, width, width)],
                scratch_shapes=[
                    pltpu.VMEM((3, width, width), F32),
                    pltpu.VMEM((256, width), BF16),
                    pltpu.VMEM((256, width), BF16),
                    pltpu.SemaphoreType.DMA((8,)),
                ],
            ),
            out_shape=[struct(images, slots, width, dtype=BF16)] * 3
            + [
                struct(images, all_heads, slots, 256, dtype=BF16),
                struct(images, slots, width, dtype=BF16),
                struct(images, slots, width),
                struct(4, width, width, dtype=BF16),
            ],
            compiler_params=params,
            name="attention_forward",
        )(
            sid, grid_shape, places, tokens, row(first_gain), row(first_shift), q_bias, v_bias, row(proj_bias),
            own_a, diag, cls, *pieces_a,
        )

        vec = jnp.concatenate([row(v) for v in (attn_scale, second_gain, second_shift, mlp_scale, down_bias)])
        layer_out, middle_grad, grad_b, grad_c, sums = pl.pallas_call(
            feed_forward,
            grid_spec=pltpu.PrefetchScalarGridSpec(
                num_scalar_prefetch=2,
                grid=(images,),
                in_specs=[per_image(slots, width)] * 3
                + [whole(5, width), whole(narrow_size, width), whole(width, width), whole(width, width)]
                + [anyspace] * 16,
                out_specs=[per_image(slots, width)] * 2
                + [whole(width, width), whole(width, width), whole(7, 8, width)],
                scratch_shapes=[
                    pltpu.VMEM((3, width, width), F32),
                    pltpu.VMEM((4, width, width), BF16),
                    pltpu.VMEM((4, width, width), BF16),
                    pltpu.VMEM((slots, width), F32),
                    pltpu.VMEM((slots, width), F32),
                    pltpu.SemaphoreType.DMA((8,)),
                ],
            ),
            out_shape=[
                struct(images, slots, width, dtype=BF16),
                struct(images, slots, width),
                struct(width, width),
                struct(width, width),
                struct(7, 8, width),
            ],
            compiler_params=params,
            name="feed_forward",
        )(
            grid_shape, places, tokens, branch, cotangent, vec, u_bias, up_weight, down_weight, *pieces_b, *pieces_c
        )

        grad_b, grad_c = lax.psum((grad_b, grad_c), "wide")

        vec = jnp.concatenate([row(v) for v in (attn_scale, first_gain, first_shift)])
        tokens_grad, grad_a, more, diag_grad, cls_grad = pl.pallas_call(
            attention_backward,
            grid_spec=pltpu.PrefetchScalarGridSpec(
                num_scalar_prefetch=2,
                grid=(images,),
                in_specs=[
                    per_image(slots, width),
                    per_image(slots, width),
                    pl.BlockSpec((1, slots, 256), lambda i, *_: (i, 0, 0)),
                    per_image(slots, width),
                    per_image(slots, width),
                    per_image(slots, width),
                    per_image(all_heads, slots, 256),
                    whole(3, width),
                    whole(4, width, width),
                ],
                out_specs=[
                    per_image(slots, width),
                    whole(width, width),
                    whole(4, 8, width),
                    whole(len(GRIDS), 2, 3, 8, DIAG),
                    whole(3, 3, 8, 256),
                ],
                scratch_shapes=[
                    pltpu.VMEM((256, width), BF16),
                    pltpu.VMEM((256, width), BF16),
                    pltpu.VMEM((slots, width), BF16),
                    pltpu.VMEM((slots, width), BF16),
                    pltpu.VMEM((slots, width), BF16),
                ],
            ),
            out_shape=[
                struct(images, slots, width),
                struct(width, width),
                struct(4, 8, width),
                struct(len(GRIDS), 2, 3, 8, DIAG),
                struct(3, 3, 8, 256),
            ],
            compiler_params=params,
            name="attention_backward",
        )(sid, grid_shape, tokens, middle_grad, attended, queries, keys, values, probs, vec, weights_a)

        diag_grad = jnp.pad(jnp.sum(diag_grad, axis=3), ((0, 0), (0, 0), (0, 8 - heads), (0, 0)))
        square_grad = pl.pallas_call(
            undiag_kernel, out_shape=struct(SPAN, 8, 128), name="undiag"
        )(diag_grad)
        square_grad = jnp.transpose(square_grad[:, :heads, :SPAN], (1, 0, 2))[:, ::-1, ::-1]
        table_grad = jnp.concatenate(
            [square_grad.reshape(heads, SPAN * SPAN), jnp.sum(cls_grad, axis=(2, 3)).T], axis=1
        )
        sums = jnp.sum(sums, axis=1)
        more = jnp.sum(more, axis=1)
        grad_a, table_grad, sums, more = lax.psum((grad_a, table_grad, sums, more), "wide")
        qkv_grad = jnp.transpose(grad_a[: 3 * local].reshape(3, local, width), (0, 2, 1))
        return (
            layer_out,
            tokens_grad,
            more[0],
            more[1],
            qkv_grad,
            more[2, :local],
            more[3, :local],
            table_grad,
            grad_a[3 * local :],
            sums[5] * attn_scale.astype(F32),
            sums[4],
            sums[2],
            sums[3],
            grad_b,
            sums[6],
            grad_c,
            sums[1] * mlp_scale.astype(F32),
            sums[0],
        )

    return body


def solution(mesh):
    rows = P("wide", None, None)
    return jax.shard_map(
        make_body(mesh.shape["wide"], mesh.shape["narrow"]),
        mesh=mesh,
        in_specs=(
            rows, P("wide", None), P(), P(), P(None, None, "narrow"), P("narrow"), P("narrow"), P("narrow", None),
            P("narrow", None), P(), P(), P(), P(), P(None, "narrow"), P("narrow"), P("narrow", None), P(), P(), rows,
        ),
        out_specs=(
            rows, rows, P(), P(), P(None, None, "narrow"), P("narrow"), P("narrow"), P("narrow", None),
            P("narrow", None), P(), P(), P(), P(), P(None, "narrow"), P("narrow"), P("narrow", None), P(), P(),
        ),
        check_vma=False,
    )
```

time: 3970 us -> 509 us (0.13)
  other arithmetic: 1930 us -> 14.7 us
  local copies, waits for them, and re-layouts: 1500 us -> 29.2 us
  Pallas kernels: 0 us -> 197 us
  waiting for transfers between devices: 359 us -> 176 us
  matrix products: 68.2 us -> 0 us
  starting transfers between devices: 0.16 us -> 52 us
    scatter-add x1 -> x0, other arithmetic: 1860 us -> none  [body(): jax.ops.segment_sum(entries, flat_index, num_segments=table_size)]
    gather x2 -> x0, local copies, waits for them, and re-layouts: 1360 us -> none  [body(): jnp.take(table_f, pair_index, axis=1)]
    psum x4 -> x1, waiting for transfers between devices: 359 us -> 82.7 us  [body(): lax.psum((grad_a, table_grad, sums, more), 'wide')]
    pallas_call x0 -> x5, Pallas kernels: none -> 197 us  [the longest x1 75 us: body(): pl.pallas_call(attention_forward, grid_spec=pltpu.PrefetchScalarGridSpec(...]
    ppermute x0 -> x33, waiting for transfers between devices: none -> 93 us  [the longest x12 51.2 us: shift(): lax.ppermute(value, 'narrow', [(i, (i - steps) % narrow_size) for i in ra...]
    reshape x3 -> x15, local copies, waits for them, and re-layouts: 89.5 us -> 9.05 us  [the longest x8 5.74 us: row(): return v.astype(F32).reshape(1, -1)]
    dot_general x17 -> x0, matrix products: 66.4 us -> none  [the longest x1 6.7 us: body(): jnp.dot(second_in, up_weight, preferred_element_type=float_type)]
    ppermute x0 -> x33, starting transfers between devices: none -> 52 us  [the longest x21 28.9 us: swap(): lax.ppermute(value, 'wide', [(j, partner(j)) for j in range(wide_size)])]
  transfers between devices with their start and end apart: 4 -> 34, of which waited for: 2 -> 11; matrix products, arithmetic and copies ran while one was open for 51% -> 6% of each run, Pallas kernels for 0% -> 16%
where the time goes in v1:
time: 509 us; the launch traced here: 508 us
  Pallas kernels  197 us (39%)
  waiting for transfers between devices  176 us (35%)
  starting transfers between devices  52 us (10%)
  local copies, waits for them, and re-layouts  29.2 us (6%)
  blocking collectives  24 us (5%)
  other arithmetic  14.7 us (3%)
  between operations  14.5 us (3%)
    psum x1, waiting for transfers between devices, body(): lax.psum((grad_a, table_grad, sums, more), 'wide')  82.7 us
    pallas_call x1, Pallas kernels, body(): pl.pallas_call(attention_forward, grid_spec=pltpu.PrefetchScalarGridSpec(...  75 us
    pallas_call x1, Pallas kernels, body(): pl.pallas_call(feed_forward, grid_spec=pltpu.PrefetchScalarGridSpec(num_s...  74.7 us
    ppermute x12, waiting for transfers between devices, shift(): lax.ppermute(value, 'narrow', [(i, (i - steps) % narrow_size) for i in ra...  51.2 us
    pallas_call x1, Pallas kernels, body(): pl.pallas_call(attention_backward, grid_spec=pltpu.PrefetchScalarGridSpec...  42.5 us
    ppermute x21, waiting for transfers between devices, swap(): lax.ppermute(value, 'wide', [(j, partner(j)) for j in range(wide_size)])  41.9 us
    ppermute x21, starting transfers between devices, swap(): lax.ppermute(value, 'wide', [(j, partner(j)) for j in range(wide_size)])  28.9 us
    psum x1, blocking collectives, body(): lax.psum((grad_a, table_grad, sums, more), 'wide')  24 us
  transfers between devices with their start and end apart: 34, of which 11 were waited for; matrix products, arithmetic and copies ran while one was open for 6% of the time, Pallas kernels for 16%

profile of v1, /device:TPU:1, one launch (start us, length us, event | category | flops | bytes accessed | tf_op | source)
XLA Modules:
  0.0 507.6 jit_solution(11127182949216352901)
XLA Ops:
  8.2 4.2 collective-permute-start.3
  12.9 5.4 %collective-permute-done.3 = f32[96,768]{1,0:T(8,128)S(1)} collective-permute-done((f32[96,768]{1,0:T(8,128)S(1)}, f32[96,768]{1,0:T(8,128)S(1)}, u32[]{:S(2)}, u32[]{:S(2)}) %collective-permute-start.3) | collective-permute-done | bytes 294944 | tf_op jit(solution)/shard_map/ppermute | solution.py:335
  18.2 18.7 %collective-permute-done.4 = f32[96,768]{1,0:T(8,128)S(1)} collective-permute-done((f32[96,768]{1,0:T(8,128)S(1)}, f32[96,768]{1,0:T(8,128)S(1)}, u32[]{:S(2)}, u32[]{:S(2)}) %collective-permute-start.4) | collective-permute-done | bytes 294944 | tf_op jit(solution)/shard_map/ppermute | solution.py:335
  39.4 2.9 collective-permute-start.14
  45.3 1.9 collective-permute-start.23
  47.1 2.1 collective-permute-start.24
  49.2 17.7 %collective-permute-done.14 = f32[96,768]{1,0:T(8,128)S(1)} collective-permute-done((f32[96,768]{1,0:T(8,128)S(1)}, f32[96,768]{1,0:T(8,128)S(1)}, u32[]{:S(2)}, u32[]{:S(2)}) %collective-permute-start.14) | collective-permute-done | bytes 294944 | tf_op jit(solution)/shard_map/ppermute | solution.py:335
  68.3 2.8 concatenate.17
  71.8 3.3 collective-permute-start
  76.3 6.9 %collective-permute-start.1 = (f32[64,128]{1,0:T(8,128)S(1)}, f32[64,128]{1,0:T(8,128)S(1)}, u32[]{:S(2)}, u32[]{:S(2)}) collective-permute-start(f32[64,128]{1,0:T(8,128)S(1)} %get-tuple-element.72), channel_id=1, source_target_pairs={{0,2},{1,3},{2,0},{3,1},{4,6},{5,7},{6,4},{7,5},{8,10},{9,11},{10,... | collective-permute-start | bytes 98312 | tf_op jit(solution)/shard_map/ppermute | solution.py:335
  83.1 9.4 %collective-permute-done.24 = f32[96,768]{1,0:T(8,128)S(1)} collective-permute-done((f32[96,768]{1,0:T(8,128)}, f32[96,768]{1,0:T(8,128)S(1)}, u32[]{:S(2)}, u32[]{:S(2)}) %collective-permute-start.24) | collective-permute-done | bytes 294944 | tf_op jit(solution)/shard_map/ppermute | solution.py:335
  92.5 2.7 collective-permute-start.7
  100.6 10.3 %collective-permute-done.7.rest_2_ = f32[3,96,768]{2,1,0:T(8,128)} collective-permute-done((f32[3,96,768]{2,1,0:T(8,128)S(1)}, f32[3,96,768]{2,1,0:T(8,128)}, u32[]{:S(2)}, u32[]{:S(2)}) %collective-permute-start.7) | collective-permute-done | bytes 884768 | tf_op jit(solution)/shard_map/ppermute | solution.py:338
  112.5 4.5 collective-permute-start.19
  117.0 2.6 collective-permute-done.16.rest_1_
  120.6 18.0 %collective-permute-done.26.rest_9_ = f32[3,96,768]{2,1,0:T(8,128)} collective-permute-done((f32[3,96,768]{2,1,0:T(8,128)S(1)}, f32[3,96,768]{2,1,0:T(8,128)}, u32[]{:S(2)}, u32[]{:S(2)}) %collective-permute-start.26) | collective-permute-done | bytes 884768 | tf_op jit(solution)/shard_map/ppermute | solution.py:338
  140.9 3.1 collective-permute-done.27.rest_10_
  144.0 2.9 collective-permute-start.11
  148.4 5.0 collective-permute-done.8.rest_3_
  153.5 2.9 collective-permute-start.20
  166.3 2.1 pad_maximum_fusion.own_ref
  169.6 2.8 collective-permute-done.28.rest_11_
  172.4 2.9 collective-permute-start.31
  178.1 2.8 diag.1.diag_ref
  184.5 75.0 %attention_forward.1 = (bf16[8,208,768]{2,1,0:T(8,128)(2,1)}, bf16[8,208,768]{2,1,0:T(8,128)(2,1)}, bf16[8,208,768]{2,1,0:T(8,128)(2,1)}, bf16[8,12,208,256]{3,2...) custom-call(s32[8]{0:T(128)} %get-tuple-element.36.sid_ref, ...), custom_call_target="tpu_custom_call" | custom-call | tf_op jit(solution)/shard_map/attention_forward/pallas_call | solution.py:421
  259.6 74.7 %feed_forward.1 = (bf16[8,208,768]{2,1,0:T(8,128)(2,1)}, f32[8,208,768]{2,1,0:T(8,128)}, f32[768,768]{1,0:T(8,128)}, f32[768,768]{1,0:T(8,128)}, f32[7,8,768]{2,1,0:T(8,128)}) custom-call(s32[8,2]{1,0:T(8,128)} %copy.58.grid_ref, s32[8]{0:T(128)} %stack.85.pidx_ref, bf16[8,208,768]{2,1,0:T(8,128)(2,1)} %tok_ref.5, ...), custom_call_target="tpu_custom_call" | custom-call | tf_op jit(solution)/shard_map/feed_forward/pallas_call | solution.py:459
  334.3 42.5 %attention_backward.1 = (f32[8,208,768]{2,1,0:T(8,128)}, f32[768,768]{1,0:T(8,128)}, f32[4,8,768]{2,1,0:T(8,128)}, f32[8,2,3,8,512]{4,3,2,1,0:T(8,128)}, f32[3,3,8,256]{3,2,1,0:T(8,128)}) custom-call(s32[8]{0:T(128)} %get-tuple-element.36.sid_ref, s32[8,2]{1,0:T(8,128)} %copy.58.grid_ref, bf16[8,208,768]{2,1,0:T(8,128)(2,1)} %tok_ref.5, ...), custom_call_target="tpu_custom_call" | custom-call | tf_op jit(solution)/shard_map/attention_backward/pallas_call | solution.py:494
  378.8 2.4 undiag.1
  382.8 24.0 %all-reduce.3 = (f32[4,768]{1,0:T(4,128)S(1)}, f32[3,2212]{1,0:T(4,128)}, f32[7,768]{1,0:T(8,128)S(1)}) all-reduce(f32[4,768]{1,0:T(4,128)S(1)} %reduce_sum.36, f32[3,2212]{1,0:T(4,128)S(1)} %pad_maximum_fusion.5, f32[7,768]{1,0:T(8,128)S(1)} %reduce_sum.39), channel_id=1, replica_groups=mesh['wide'=8,'narrow'=4] {'wide'}, use_global_device_ids=true, to_apply=%region_3.4 | all-reduce | flops 15084 | bytes 120672 | tf_op jit(solution)/shard_map/psum | solution.py:546
  409.2 82.7 %all-reduce.7.cloned.1.call-done = (f32[768,768]{1,0:T(8,128)}, f32[768,768]{1,0:T(8,128)}, f32[768,768]{1,0:T(8,128)}) async-done(((f32[768,768]{1,0:T(8,128)}, f32[768,768]{1,0:T(8,128)}, f32[768,768]{1,0:T(8,128)}), (f32[768,768]{1,0:T(8,128)}, f32[768,768]{1,0:T(8,128)}, f32[768,768]{1,0:T(8,128)})) %all-reduce.7.cloned.1.call-update) | async-done | bytes 7077904 | tf_op jit(solution)/shard_map/psum | solution.py:546
  491.9 2.9 slice.85
  494.9 1.9 slice.89
  (168 shorter events, 49.2 us)
Async XLA Ops:
  7.2 484.7 %all-reduce.7.cloned.1.call-start = ((), (), s32[]{:S(2)}) async-start(), calls=%async_computation | async-start | bytes 14155776 | tf_op jit(solution)/shard_map/psum | solution.py:546
  8.2 10.0 %collective-permute-start.3 = (f32[96,768]{1,0:T(8,128)S(1)}, f32[96,768]{1,0:T(8,128)S(1)}, u32[]{:S(2)}, u32[]{:S(2)}) collective-permute-start(f32[96,768]{1,0:T(8,128)S(1)} %fusion.1), channel_id=1, source_target_pairs={{0,3},{1,0},{2,1},{3,2},{4,7},{5,4},{6,5},{7,6},{8,11},{9,8},{10,9... | collective-permute-start | bytes 884744 | tf_op jit(solution)/shard_map/ppermute | solution.py:335
  12.4 24.5 %collective-permute-start.4 = (f32[96,768]{1,0:T(8,128)S(1)}, f32[96,768]{1,0:T(8,128)S(1)}, u32[]{:S(2)}, u32[]{:S(2)}) collective-permute-start(f32[96,768]{1,0:T(8,128)S(1)} %fusion.1), channel_id=1, source_target_pairs={{0,2},{1,3},{2,0},{3,1},{4,6},{5,7},{6,4},{7,5},{8,10},{9,11},{10,... | collective-permute-start | bytes 884744 | tf_op jit(solution)/shard_map/ppermute | solution.py:335
  12.4 24.5 %collective-permute-start.5 = (f32[96,768]{1,0:T(8,128)S(1)}, f32[96,768]{1,0:T(8,128)S(1)}, u32[]{:S(2)}, u32[]{:S(2)}) collective-permute-start(f32[96,768]{1,0:T(8,128)S(1)} %fusion.1), channel_id=1, source_target_pairs={{0,1},{1,2},{2,3},{3,0},{4,5},{5,6},{6,7},{7,4},{8,9},{9,10},{10,1... | collective-permute-start | bytes 884744 | tf_op jit(solution)/shard_map/ppermute | solution.py:335
  37.1 62.2 %collective-permute-start.6 = (f32[3,96,768]{2,1,0:T(8,128)S(1)}, f32[3,96,768]{2,1,0:T(8,128)}, u32[]{:S(2)}, u32[]{:S(2)}) collective-permute-start(f32[3,96,768]{2,1,0:T(8,128)S(1)} %pad_maximum_fusion.1.rest_0_), channel_id=1, source_target_pairs={{0,8},{4,20},{8,0},{12,28},{16,24},{20,4},{24,16},{28,12},{1,9},{5... | collective-permute-start | bytes 2654216 | tf_op jit(solution)/shard_map/ppermute | solution.py:338
  39.4 27.5 %collective-permute-start.14 = (f32[96,768]{1,0:T(8,128)S(1)}, f32[96,768]{1,0:T(8,128)S(1)}, u32[]{:S(2)}, u32[]{:S(2)}) collective-permute-start(f32[96,768]{1,0:T(8,128)S(1)} %dynamic-slice_convert_fusion.1), channel_id=1, source_target_pairs={{0,2},{1,3},{2,0},{3,1},{4,6},{5,7},{6,4},{7,5},{8,10},{9,11},{10,... | collective-permute-start | bytes 884744 | tf_op jit(solution)/shard_map/ppermute | solution.py:335
  42.2 29.6 %collective-permute-start.15 = (f32[96,768]{1,0:T(8,128)S(1)}, f32[96,768]{1,0:T(8,128)S(1)}, u32[]{:S(2)}, u32[]{:S(2)}) collective-permute-start(f32[96,768]{1,0:T(8,128)S(1)} %dynamic-slice_convert_fusion.1), channel_id=1, source_target_pairs={{0,1},{1,2},{2,3},{3,0},{4,5},{5,6},{6,7},{7,4},{8,9},{9,10},{10,1... | collective-permute-start | bytes 884744 | tf_op jit(solution)/shard_map/ppermute | solution.py:335
  45.3 31.0 %collective-permute-start.23 = (f32[96,768]{1,0:T(8,128)}, f32[96,768]{1,0:T(8,128)S(1)}, u32[]{:S(2)}, u32[]{:S(2)}) collective-permute-start(f32[96,768]{1,0:T(8,128)} %dynamic-slice_convert_fusion), channel_id=1, source_target_pairs={{0,3},{1,0},{2,1},{3,2},{4,7},{5,4},{6,5},{7,6},{8,11},{9,8},{10,9... | collective-permute-start | bytes 884744 | tf_op jit(solution)/shard_map/ppermute | solution.py:335
  47.1 45.4 %collective-permute-start.24 = (f32[96,768]{1,0:T(8,128)}, f32[96,768]{1,0:T(8,128)S(1)}, u32[]{:S(2)}, u32[]{:S(2)}) collective-permute-start(f32[96,768]{1,0:T(8,128)} %dynamic-slice_convert_fusion), channel_id=1, source_target_pairs={{0,2},{1,3},{2,0},{3,1},{4,6},{5,7},{6,4},{7,5},{8,10},{9,11},{10,... | collective-permute-start | bytes 884744 | tf_op jit(solution)/shard_map/ppermute | solution.py:335
  66.9 25.6 %collective-permute-start.25 = (f32[96,768]{1,0:T(8,128)}, f32[96,768]{1,0:T(8,128)}, u32[]{:S(2)}, u32[]{:S(2)}) collective-permute-start(f32[96,768]{1,0:T(8,128)} %dynamic-slice_convert_fusion), channel_id=1, source_target_pairs={{0,1},{1,2},{2,3},{3,0},{4,5},{5,6},{6,7},{7,4},{8,9},{9,10},{10,1... | collective-permute-start | bytes 884744 | tf_op jit(solution)/shard_map/ppermute | solution.py:335
  71.8 24.6 %collective-permute-start = (f32[64,128]{1,0:T(8,128)S(1)}, f32[64,128]{1,0:T(8,128)S(1)}, u32[]{:S(2)}, u32[]{:S(2)}) collective-permute-start(f32[64,128]{1,0:T(8,128)S(1)} %get-tuple-element.72), channel_id=1, source_target_pairs={{0,3},{1,0},{2,1},{3,2},{4,7},{5,4},{6,5},{7,6},{8,11},{9,8},{10,9... | collective-permute-start | bytes 98312 | tf_op jit(solution)/shard_map/ppermute | solution.py:335
  76.3 21.5 %collective-permute-start.1 = (f32[64,128]{1,0:T(8,128)S(1)}, f32[64,128]{1,0:T(8,128)S(1)}, u32[]{:S(2)}, u32[]{:S(2)}) collective-permute-start(f32[64,128]{1,0:T(8,128)S(1)} %get-tuple-element.72), channel_id=1, source_target_pairs={{0,2},{1,3},{2,0},{3,1},{4,6},{5,7},{6,4},{7,5},{8,10},{9,11},{10,... | collective-permute-start | bytes 98312 | tf_op jit(solution)/shard_map/ppermute | solution.py:335
  92.5 18.4 %collective-permute-start.7 = (f32[3,96,768]{2,1,0:T(8,128)S(1)}, f32[3,96,768]{2,1,0:T(8,128)}, u32[]{:S(2)}, u32[]{:S(2)}) collective-permute-start(f32[3,96,768]{2,1,0:T(8,128)S(1)} %pad_maximum_fusion.1.rest_0_), channel_id=1, source_target_pairs={{0,16},{4,12},{8,24},{12,4},{16,0},{20,28},{24,8},{28,20},{1,17},{... | collective-permute-start | bytes 2654216 | tf_op jit(solution)/shard_map/ppermute | solution.py:338
  96.5 16.0 %collective-permute-start.9 = (f32[3,96,768]{2,1,0:T(8,128)S(1)}, f32[3,96,768]{2,1,0:T(8,128)S(1)}, u32[]{:S(2)}, u32[]{:S(2)}) collective-permute-start(f32[3,96,768]{2,1,0:T(8,128)S(1)} %pad_maximum_fusion.1.rest_0_), channel_id=1, source_target_pairs={{0,4},{4,0},{8,12},{12,8},{16,20},{20,16},{24,28},{28,24},{1,5},{5... | collective-permute-start | bytes 2654216 | tf_op jit(solution)/shard_map/ppermute | solution.py:338
  97.8 21.8 %collective-permute-start.16 = (f32[3,96,768]{2,1,0:T(8,128)S(1)}, f32[3,96,768]{2,1,0:T(8,128)}, u32[]{:S(2)}, u32[]{:S(2)}) collective-permute-start(f32[3,96,768]{2,1,0:T(8,128)S(1)} %pad_maximum_fusion.2.rest_0_), channel_id=1, source_target_pairs={{0,8},{4,20},{8,0},{12,28},{16,24},{20,4},{24,16},{28,12},{1,9},{5... | collective-permute-start | bytes 2654216 | tf_op jit(solution)/shard_map/ppermute | solution.py:338
  98.9 39.7 %collective-permute-start.26 = (f32[3,96,768]{2,1,0:T(8,128)S(1)}, f32[3,96,768]{2,1,0:T(8,128)}, u32[]{:S(2)}, u32[]{:S(2)}) collective-permute-start(f32[3,96,768]{2,1,0:T(8,128)S(1)} %pad_maximum_fusion.3.rest_8_), channel_id=1, source_target_pairs={{0,8},{4,20},{8,0},{12,28},{16,24},{20,4},{24,16},{28,12},{1,9},{5... | collective-permute-start | bytes 2654216 | tf_op jit(solution)/shard_map/ppermute | solution.py:338
  99.2 40.7 %collective-permute-start.17 = (f32[3,96,768]{2,1,0:T(8,128)S(1)}, f32[3,96,768]{2,1,0:T(8,128)S(1)}, u32[]{:S(2)}, u32[]{:S(2)}) collective-permute-start(f32[3,96,768]{2,1,0:T(8,128)S(1)} %pad_maximum_fusion.2.rest_0_), channel_id=1, source_target_pairs={{0,16},{4,12},{8,24},{12,4},{16,0},{20,28},{24,8},{28,20},{1,17},{... | collective-permute-start | bytes 2654216 | tf_op jit(solution)/shard_map/ppermute | solution.py:338
  110.9 33.1 %collective-permute-start.27 = (f32[3,96,768]{2,1,0:T(8,128)S(1)}, f32[3,96,768]{2,1,0:T(8,128)}, u32[]{:S(2)}, u32[]{:S(2)}) collective-permute-start(f32[3,96,768]{2,1,0:T(8,128)S(1)} %pad_maximum_fusion.3.rest_8_), channel_id=1, source_target_pairs={{0,16},{4,12},{8,24},{12,4},{16,0},{20,28},{24,8},{28,20},{1,17},{... | collective-permute-start | bytes 2654216 | tf_op jit(solution)/shard_map/ppermute | solution.py:338
  112.5 34.4 %collective-permute-start.19 = (f32[3,96,768]{2,1,0:T(8,128)S(1)}, f32[3,96,768]{2,1,0:T(8,128)S(1)}, u32[]{:S(2)}, u32[]{:S(2)}) collective-permute-start(f32[3,96,768]{2,1,0:T(8,128)S(1)} %pad_maximum_fusion.2.rest_0_), channel_id=1, source_target_pairs={{0,4},{4,0},{8,12},{12,8},{16,20},{20,16},{24,28},{28,24},{1,5},{5... | collective-permute-start | bytes 2654216 | tf_op jit(solution)/shard_map/ppermute | solution.py:338
  119.6 28.5 %collective-permute-start.29 = (f32[3,96,768]{2,1,0:T(8,128)S(1)}, f32[3,96,768]{2,1,0:T(8,128)S(1)}, u32[]{:S(2)}, u32[]{:S(2)}) collective-permute-start(f32[3,96,768]{2,1,0:T(8,128)S(1)} %pad_maximum_fusion.3.rest_8_), channel_id=1, source_target_pairs={{0,4},{4,0},{8,12},{12,8},{16,20},{20,16},{24,28},{28,24},{1,5},{5... | collective-permute-start | bytes 2654216 | tf_op jit(solution)/shard_map/ppermute | solution.py:338
  138.6 14.9 %collective-permute-start.8 = (f32[3,96,768]{2,1,0:T(8,128)}, f32[3,96,768]{2,1,0:T(8,128)}, u32[]{:S(2)}, u32[]{:S(2)}) collective-permute-start(f32[3,96,768]{2,1,0:T(8,128)} %collective-permute-done.6.rest_1_), channel_id=1, source_target_pairs={{0,16},{4,12},{8,24},{12,4},{16,0},{20,28},{24,8},{28,20},{1,17},{... | collective-permute-start | bytes 2654216 | tf_op jit(solution)/shard_map/ppermute | solution.py:338
  139.9 16.4 %collective-permute-start.10 = (f32[3,96,768]{2,1,0:T(8,128)}, f32[3,96,768]{2,1,0:T(8,128)}, u32[]{:S(2)}, u32[]{:S(2)}) collective-permute-start(f32[3,96,768]{2,1,0:T(8,128)} %collective-permute-done.6.rest_1_), channel_id=1, source_target_pairs={{0,4},{4,0},{8,12},{12,8},{16,20},{20,16},{24,28},{28,24},{1,5},{5... | collective-permute-start | bytes 2654216 | tf_op jit(solution)/shard_map/ppermute | solution.py:338
  144.0 25.1 %collective-permute-start.11 = (f32[3,96,768]{2,1,0:T(8,128)}, f32[3,96,768]{2,1,0:T(8,128)}, u32[]{:S(2)}, u32[]{:S(2)}) collective-permute-start(f32[3,96,768]{2,1,0:T(8,128)} %collective-permute-done.7.rest_2_), channel_id=1, source_target_pairs={{0,4},{4,0},{8,12},{12,8},{16,20},{20,16},{24,28},{28,24},{1,5},{5... | collective-permute-start | bytes 2654216 | tf_op jit(solution)/shard_map/ppermute | solution.py:338
  146.9 22.6 %collective-permute-start.18 = (f32[3,96,768]{2,1,0:T(8,128)}, f32[3,96,768]{2,1,0:T(8,128)}, u32[]{:S(2)}, u32[]{:S(2)}) collective-permute-start(f32[3,96,768]{2,1,0:T(8,128)} %collective-permute-done.16.rest_1_), channel_id=1, source_target_pairs={{0,16},{4,12},{8,24},{12,4},{16,0},{20,28},{24,8},{28,20},{1,17},{... | collective-permute-start | bytes 2654216 | tf_op jit(solution)/shard_map/ppermute | solution.py:338
  148.1 24.3 %collective-permute-start.28 = (f32[3,96,768]{2,1,0:T(8,128)}, f32[3,96,768]{2,1,0:T(8,128)}, u32[]{:S(2)}, u32[]{:S(2)}) collective-permute-start(f32[3,96,768]{2,1,0:T(8,128)} %collective-permute-done.26.rest_9_), channel_id=1, source_target_pairs={{0,16},{4,12},{8,24},{12,4},{16,0},{20,28},{24,8},{28,20},{1,17},{... | collective-permute-start | bytes 2654216 | tf_op jit(solution)/shard_map/ppermute | solution.py:338
  153.5 21.9 %collective-permute-start.20 = (f32[3,96,768]{2,1,0:T(8,128)}, f32[3,96,768]{2,1,0:T(8,128)}, u32[]{:S(2)}, u32[]{:S(2)}) collective-permute-start(f32[3,96,768]{2,1,0:T(8,128)} %collective-permute-done.16.rest_1_), channel_id=1, source_target_pairs={{0,4},{4,0},{8,12},{12,8},{16,20},{20,16},{24,28},{28,24},{1,5},{5... | collective-permute-start | bytes 2654216 | tf_op jit(solution)/shard_map/ppermute | solution.py:338
  156.4 18.9 %collective-permute-start.12 = (f32[3,96,768]{2,1,0:T(8,128)}, f32[3,96,768]{2,1,0:T(8,128)}, u32[]{:S(2)}, u32[]{:S(2)}) collective-permute-start(f32[3,96,768]{2,1,0:T(8,128)} %collective-permute-done.8.rest_3_), channel_id=1, source_target_pairs={{0,4},{4,0},{8,12},{12,8},{16,20},{20,16},{24,28},{28,24},{1,5},{5... | collective-permute-start | bytes 2654216 | tf_op jit(solution)/shard_map/ppermute | solution.py:338
  169.1 90.4 %collective-permute-start.30 = (f32[3,96,768]{2,1,0:T(8,128)}, f32[3,96,768]{2,1,0:T(8,128)}, u32[]{:S(2)}, u32[]{:S(2)}) collective-permute-start(f32[3,96,768]{2,1,0:T(8,128)} %collective-permute-done.26.rest_9_), channel_id=1, source_target_pairs={{0,4},{4,0},{8,12},{12,8},{16,20},{20,16},{24,28},{28,24},{1,5},{5... | collective-permute-start | bytes 2654216 | tf_op jit(solution)/shard_map/ppermute | solution.py:338
  169.5 90.0 %collective-permute-start.21 = (f32[3,96,768]{2,1,0:T(8,128)S(1)}, f32[3,96,768]{2,1,0:T(8,128)}, u32[]{:S(2)}, u32[]{:S(2)}) collective-permute-start(f32[3,96,768]{2,1,0:T(8,128)S(1)} %copy-done.8), channel_id=1, source_target_pairs={{0,4},{4,0},{8,12},{12,8},{16,20},{20,16},{24,28},{28,24},{1,5},{5... | collective-permute-start | bytes 2654216 | tf_op jit(solution)/shard_map/ppermute | solution.py:338
  172.4 87.1 %collective-permute-start.31 = (f32[3,96,768]{2,1,0:T(8,128)}, f32[3,96,768]{2,1,0:T(8,128)}, u32[]{:S(2)}, u32[]{:S(2)}) collective-permute-start(f32[3,96,768]{2,1,0:T(8,128)} %collective-permute-done.27.rest_10_), channel_id=1, source_target_pairs={{0,4},{4,0},{8,12},{12,8},{16,20},{20,16},{24,28},{28,24},{1,5},{5... | collective-permute-start | bytes 2654216 | tf_op jit(solution)/shard_map/ppermute | solution.py:338
  175.3 84.2 %collective-permute-start.22 = (f32[3,96,768]{2,1,0:T(8,128)}, f32[3,96,768]{2,1,0:T(8,128)}, u32[]{:S(2)}, u32[]{:S(2)}) collective-permute-start(f32[3,96,768]{2,1,0:T(8,128)} %collective-permute-done.18.rest_3_), channel_id=1, source_target_pairs={{0,4},{4,0},{8,12},{12,8},{16,20},{20,16},{24,28},{28,24},{1,5},{5... | collective-permute-start | bytes 2654216 | tf_op jit(solution)/shard_map/ppermute | solution.py:338
  175.3 84.2 %collective-permute-start.32 = (f32[3,96,768]{2,1,0:T(8,128)}, f32[3,96,768]{2,1,0:T(8,128)}, u32[]{:S(2)}, u32[]{:S(2)}) collective-permute-start(f32[3,96,768]{2,1,0:T(8,128)} %collective-permute-done.28.rest_11_), channel_id=1, source_target_pairs={{0,4},{4,0},{8,12},{12,8},{16,20},{20,16},{24,28},{28,24},{1,5},{5... | collective-permute-start | bytes 2654216 | tf_op jit(solution)/shard_map/ppermute | solution.py:338
  (37 other events, 1252.6 us)
Sparse Core Ops, SparseCore 0:
  376.9 115.0 all-reduce.6

commit v2 on v1

--- a/solution.py
+++ b/solution.py
@@ -64,13 +64,6 @@
             yield 1, centre + 1 + m, centre + 1 - wide, at + 1, wide - 1
 
 
-def diag_kernel(table_ref, out_ref):
-    out_ref[...] = jnp.zeros_like(out_ref)
-    for shape_at in range(len(GRIDS)):
-        for which, row, col, at, size in windows(shape_at):
-            out_ref[shape_at, which, :, at : at + size] = table_ref[row, :, col : col + size]
-
-
 def undiag_kernel(diag_ref, out_ref):
     out_ref[...] = jnp.zeros_like(out_ref)
     for shape_at in range(len(GRIDS)):
@@ -95,63 +88,222 @@
     return p, s, limit, later, p_patch, s_patch
 
 
-def load_pieces(pidx_ref, pieces, stage, sems, rows):
-    copies = []
-    for r, piece in enumerate(pieces):
-        at = pl.multiple_of(pidx_ref[r] * rows, 8)
-        copies.append(
-            pltpu.make_async_copy(piece, stage.at[:, pl.ds(at, rows), :], sems.at[r])
-        )
-    for copy in copies:
-        copy.start()
-    return copies
+MESH = pl.DeviceIdType.MESH
+SLICES = 8
+SLICE_ROWS = 96
+PART_ROWS = 24
+CHUNKS = tuple((group, at, 24) for group in range(3) for at in (0, 24, 48, 72))
+
+
+class Gather:
+    def __init__(self, narrow, slices, buffers, send, recv):
+        self.narrow, self.slices, self.buffers, self.send, self.recv = narrow, slices, buffers, send, recv
+        self.z = lax.axis_index("narrow")
+        wide = lax.axis_index("wide")
+        self.me = wide % SLICES
+        self.base = wide - self.me
+        core = self.me % 2
+        over_x = self.me + 2 - 4 * ((self.me // 2) % 2)
+        over_y = self.me + 4 - 8 * (self.me // 4)
+        self.first = over_x * (1 - core) + over_y * core
+        self.second = over_y * (1 - core) + over_x * core
+        self.third = over_x + over_y - self.me
+        self.twin = self.me + 1 - 2 * core
+        self.per_chunk = narrow - 1 + 7
+        self.started = []
+
+    def copy(self, chunk, phase, piece):
+        group, at, rows = CHUNKS[chunk]
+        buffer = self.buffers[group]
+
+        def part(owner):
+            return buffer.at[:, pl.ds(pl.multiple_of(owner * SLICE_ROWS + at, 8), rows), :]
+
+        place = chunk * self.per_chunk
+        if phase == 0:
+            place += piece - 1
+            source = self.slices.at[group, pl.ds(at, rows), :]
+            target = buffer.at[piece - 1, pl.ds(pl.multiple_of(self.me * SLICE_ROWS + at, 8), rows), :]
+            device = {"narrow": (self.z + self.narrow - piece) % self.narrow}
+        else:
+            owners = (self.me, self.first, self.second, self.third)
+            place += self.narrow - 1 + (0, 1, 3)[phase - 1] + piece
+            source = target = part(owners[piece])
+            device = {"wide": self.base + (self.first, self.second, self.twin)[phase - 1]}
+        return pltpu.make_async_remote_copy(
+            src_ref=source, dst_ref=target, send_sem=self.send.at[place], recv_sem=self.recv.at[place],
+            device_id=device, device_id_type=MESH,
+        )
+
+    def pieces(self, phase):
+        return (range(1, self.narrow), range(1), range(2), range(4))[phase]
+
+    def start(self, chunk, phase):
+        for piece in self.pieces(phase):
+            self.copy(chunk, phase, piece).start()
+
+    def arrive(self, chunk, phase):
+        for piece in self.pieces(phase):
+            self.copy(chunk, phase, piece).wait_recv()
+
+    def run(self, steps):
+        for chunk, phase in steps:
+            if phase > 0:
+                self.arrive(chunk, phase - 1)
+            self.start(chunk, phase)
+
+    def drain(self):
+        for chunk in range(len(CHUNKS)):
+            for phase in range(4):
+                for piece in self.pieces(phase):
+                    self.copy(chunk, phase, piece).wait_send()
+
+    def barrier(self):
+        sem = pltpu.get_barrier_semaphore()
+        for k in range(1, self.narrow):
+            pl.semaphore_signal(
+                sem, inc=1, device_id={"narrow": (self.z + k) % self.narrow}, device_id_type=MESH
+            )
+        for other in (self.first, self.second, self.twin):
+            pl.semaphore_signal(sem, inc=1, device_id={"wide": self.base + other}, device_id_type=MESH)
+        pl.semaphore_wait(sem, self.narrow - 1 + 3)
+
+
+def tick(t):
+    steps = ((t, 1), (t + 2, 0), (t - 1, 2), (t - 2, 3))
+    return tuple((chunk, phase) for chunk, phase in steps if 0 <= chunk < len(CHUNKS))
+
+
+LATE = {3: 7, 11: 8, 20: 9}
+LAST = range(10, len(CHUNKS) + 2)
 
 
 def attention_forward(
-    sid_ref, grid_ref, pidx_ref, tok_ref, gain_ref, shift_ref, qb_ref, vb_ref, pb_ref, own_ref, diag_ref, cls_ref,
-    *rest,
+    sid_ref, grid_ref, tok_ref, gain_ref, shift_ref, pb_ref, own_ref, slices, table_ref, small_ref,
+    prob_ref, att_ref, branch_ref, wa_ref, small_out, q_out, k_out, v_out, gath_b, gath_c,
+    stage, first_in, queries, k_pad, v_pad, bias, lined, diag, far, smalls, send, recv, extra_send, extra_recv, local,
+    narrow,
 ):
-    pieces = rest[:8]
-    q_ref, k_ref, v_ref, prob_ref, att_ref, branch_ref, wa_ref = rest[8:15]
-    stage, k_pad, v_pad, sems = rest[15:]
     image = pl.program_id(0)
+    images = pl.num_programs(0)
+    gather = Gather(narrow, slices, (stage, gath_b, gath_c), send, recv)
+
+    def extra(which, k):
+        source = diag if which else small_ref.at[k]
+        target = far.at[k - 1] if which else smalls.at[k]
+        place = which * (narrow - 1) + k - 1
+        return pltpu.make_async_remote_copy(
+            src_ref=source, dst_ref=target, send_sem=extra_send.at[place], recv_sem=extra_recv.at[place],
+            device_id={"narrow": (gather.z + narrow - k) % narrow}, device_id_type=MESH,
+        )
+
+    def keep(which):
+        source, target = ((queries, q_out), (k_pad, k_out), (v_pad, v_out))[which]
+        return pltpu.make_async_copy(source, target, local.at[which])
 
     @pl.when(image == 0)
     def _():
-        copies = load_pieces(pidx_ref, pieces, stage, sems, 96)
-        k_pad[208:256, :] = jnp.zeros((48, 768), BF16)
-        v_pad[208:256, :] = jnp.zeros((48, 768), BF16)
+        def bias_of(slot, at, table):
+            p, s, limit, later, p_patch, s_patch = slot_masks(grid_ref[at, 0], grid_ref[at, 1], False)
+            both = p_patch & s_patch
+            open_key = s <= limit
+            for h in range(3):
+                row = h * 16 + sid_ref[at] * 2
+                toep = [
+                    pltpu.roll(
+                        jnp.broadcast_to(table(row + which), (208, DIAG)), DIAG - 207, 1, stride=1, stride_axis=0
+                    )[:, :256]
+                    for which in range(2)
+                ]
+                c0, c1, c2 = (smalls[slot, 3:4, h * 3 + c : h * 3 + c + 1] for c in range(3))
+                outer = jnp.where((p == 0) & s_patch, c0, jnp.where(p_patch & (s == 0), c1, c2))
+                value = jnp.where(both, jnp.where(later, toep[0], toep[1]), outer)
+                bias[at, slot * 3 + h] = jnp.where(open_key, value, MASKED).astype(BF16)
+
+        def far_bias(slot):
+            @pl.loop(0, 8)
+            def _(at):
+                bias_of(slot, at, lambda row: far[slot - 1, pl.ds(row, 1), :])
+
+        def weights_of(part):
+            gather.arrive(part, 3)
+            for slot in range(narrow - 1):
+                for pair in range(4):
+                    rows = [
+                        stage[slot, pl.ds((2 * pair + i) * SLICE_ROWS + part * PART_ROWS, PART_ROWS), :]
+                        for i in range(2)
+                    ]
+                    at = (slot + 1) * 192 + pair * 2 * PART_ROWS
+                    wa_ref[part, at : at + 2 * PART_ROWS, :] = jnp.concatenate(rows, axis=0).astype(BF16)
+
+        def project(part, target, finish):
+            @pl.loop(0, 8)
+            def _(at):
+                target[at, 0:208, :] = finish(dot_nt(first_in[at], wa_ref[part])).astype(BF16)
+
+            keep(part).start()
+
+        lined[...] = jnp.zeros_like(lined)
+        for shape_at in range(len(GRIDS)):
+            for which, row, col, at, size in windows(shape_at):
+                lined[shape_at * 2 + which, :, at : at + size] = table_ref[row, :, col : col + size]
+        for h in range(3):
+            for r in range(16):
+                diag[h * 16 + r : h * 16 + r + 1, :] = lined[r, h : h + 1, :]
+        gather.barrier()
+        smalls[0] = small_ref[0]
+        for k in range(1, narrow):
+            extra(0, k).start()
+            extra(1, k).start()
+        gather.run(((0, 0), (1, 0)))
+        k_pad[:, 208:256, :] = jnp.zeros((8, 48, 768), BF16)
+        v_pad[:, 208:256, :] = jnp.zeros((8, 48, 768), BF16)
         for part in range(4):
             wa_ref[part, 0:192, :] = own_ref[part * 192 : (part + 1) * 192, :]
-        for copy in copies:
-            copy.wait()
-        for slot in range(3):
-            for part in range(4):
-                wa_ref[part, (slot + 1) * 192 : (slot + 2) * 192, :] = stage[
-                    slot, part * 192 : (part + 1) * 192, :
-                ].astype(BF16)
-
-    normed, _ = norm_stats(tok_ref[0].astype(F32))
-    first_in = (normed * gain_ref[...] + shift_ref[...]).astype(BF16)
-    q_ref[0] = ((dot_nt(first_in, wa_ref[0]) + qb_ref[...]) * (HD ** -0.5)).astype(BF16)
-    keys = dot_nt(first_in, wa_ref[1]).astype(BF16)
-    k_ref[0] = keys
-    k_pad[0:208, :] = keys
-    values = (dot_nt(first_in, wa_ref[2]) + vb_ref[...]).astype(BF16)
-    v_ref[0] = values
-    v_pad[0:208, :] = values
-
-    p, s, limit, later, p_patch, s_patch = slot_masks(grid_ref[image, 0], grid_ref[image, 1], False)
-    both = p_patch & s_patch
-    open_key = s <= limit
+
+        @pl.loop(0, 8)
+        def _(at):
+            normed, _ = norm_stats(tok_ref[at].astype(F32))
+            first_in[at] = (normed * gain_ref[...] + shift_ref[...]).astype(BF16)
+            bias_of(0, at, lambda row: diag[pl.ds(row, 1), :])
+
+        gather.run(tick(0))
+        for k in range(1, narrow):
+            extra(0, k).wait_recv()
+            extra(1, k).wait_recv()
+        far_bias(1)
+        gather.run(tick(1))
+        far_bias(2)
+        gather.run(tick(2))
+        far_bias(3)
+        gather.run(tick(3))
+        q_bias = sum(smalls[k, 0:1, :] for k in range(narrow))
+        v_bias = sum(smalls[k, 1:2, :] for k in range(narrow))
+        small_out[...] = smalls[...]
+        weights_of(0)
+        project(0, queries, lambda v: (v + q_bias) * (HD ** -0.5))
+        gather.run(tick(4))
+        weights_of(1)
+        project(1, k_pad, lambda v: v)
+        gather.run(tick(5))
+        weights_of(2)
+        project(2, v_pad, lambda v: v + v_bias)
+        gather.run(tick(6))
+        weights_of(3)
+
     head_of = lax.broadcasted_iota(jnp.int32, (1, 256), 1) // HD
 
     @pl.loop(0, 3)
     def _(group):
+        for when, t in LATE.items():
+            @pl.when(image * 3 + group == when)
+            def _():
+                gather.run(tick(t))
+
         lanes = pl.ds(pl.multiple_of(group * 256, 256), 256)
-        q_group = q_ref[0, :, lanes]
-        k_group = k_pad[:, lanes]
-        v_group = v_pad[:, lanes]
+        q_group = queries[image, :, lanes]
+        k_group = k_pad[image, :, lanes]
+        v_group = v_pad[image, :, lanes]
         stacked = jnp.concatenate(
             [jnp.where(head_of == h, q_group, jnp.zeros_like(q_group)) for h in range(4)], axis=0
         )
@@ -159,14 +311,7 @@
         probs = []
         for h in range(4):
             head = group * 4 + h
-            f0 = diag_ref[0, 0, pl.ds(head, 1), :]
-            f1 = diag_ref[0, 1, pl.ds(head, 1), :]
-            toep0 = pltpu.roll(jnp.broadcast_to(f0, (208, DIAG)), DIAG - 207, 1, stride=1, stride_axis=0)[:, :256]
-            toep1 = pltpu.roll(jnp.broadcast_to(f1, (208, DIAG)), DIAG - 207, 1, stride=1, stride_axis=0)[:, :256]
-            c0, c1, c2 = cls_ref[head, 0], cls_ref[head, 1], cls_ref[head, 2]
-            outer = jnp.where((p == 0) & s_patch, c0, jnp.where(p_patch & (s == 0), c1, c2))
-            bias = jnp.where(both, jnp.where(later, toep0, toep1), outer)
-            scores = jnp.where(open_key, raw[h * 208 : (h + 1) * 208, :] + bias, MASKED)
+            scores = raw[h * 208 : (h + 1) * 208, :] + bias[image, head].astype(F32)
             top = jnp.max(scores, axis=-1, keepdims=True)
             raised = jnp.exp(scores - top)
             prob = (raised * (1.0 / jnp.sum(raised, axis=-1, keepdims=True))).astype(BF16)
@@ -180,24 +325,42 @@
 
     branch_ref[0] = dot_nn(att_ref[0], wa_ref[3]) + pb_ref[...]
 
+    @pl.when(image == images - 1)
+    def _():
+        for t in LAST:
+            gather.run(tick(t))
+        for chunk in range(4, len(CHUNKS)):
+            gather.arrive(chunk, 3)
+        gather.drain()
+        for k in range(1, narrow):
+            extra(0, k).wait_send()
+            extra(1, k).wait_send()
+        for which in range(3):
+            keep(which).wait()
+
 
 def feed_forward(
-    grid_ref, pidx_ref, tok_ref, branch_ref, cot_ref, vec_ref, ub_ref, ownb_ref, ownc_ref, *rest
+    grid_ref, tok_ref, branch_ref, cot_ref, vec_ref, small_ref, ownb_ref, ownc_ref, gath_b, gath_c,
+    out_ref, mg_ref, gb_ref, gc_ref, sums_ref,
+    stage, wb, wc, mlp_acc, second_acc, sems,
 ):
-    pieces_b, pieces_c = rest[:8], rest[8:16]
-    out_ref, mg_ref, gb_ref, gc_ref, sums_ref = rest[16:21]
-    stage, wb, wc, mlp_acc, second_acc, sems = rest[21:]
     image = pl.program_id(0)
 
     @pl.when(image == 0)
     def _():
-        for own_ref, pieces, weights in ((ownb_ref, pieces_b, wb), (ownc_ref, pieces_c, wc)):
-            copies = load_pieces(pidx_ref, pieces, stage, sems, 96)
-            weights[0] = own_ref[...]
-            for copy in copies:
-                copy.wait()
+        copies = [
+            pltpu.make_async_copy(gath.at[slot], stage.at[which * 3 + slot], sems.at[which * 3 + slot])
+            for which, gath in enumerate((gath_b, gath_c))
+            for slot in range(3)
+        ]
+        for copy in copies:
+            copy.start()
+        wb[0] = ownb_ref[...]
+        wc[0] = ownc_ref[...]
+        for which, weights in enumerate((wb, wc)):
             for slot in range(3):
-                weights[slot + 1] = stage[slot].astype(BF16)
+                copies[which * 3 + slot].wait()
+                weights[slot + 1] = stage[which * 3 + slot].astype(BF16)
         gb_ref[...] = jnp.zeros_like(gb_ref)
         gc_ref[...] = jnp.zeros_like(gc_ref)
         sums_ref[...] = jnp.zeros_like(sums_ref)
@@ -215,7 +378,7 @@
 
     @pl.loop(0, 4)
     def _(slot):
-        up_pre = dot_nn(second_in, wb[slot]) + ub_ref[pl.ds(slot, 1), :]
+        up_pre = dot_nn(second_in, wb[slot]) + small_ref[slot, 2:3, :]
         cdf = 0.5 * (1.0 + lax.erf(up_pre * INV_ROOT_TWO))
         hidden = (up_pre * cdf).astype(BF16)
         slope = cdf + up_pre * jnp.exp(-0.5 * up_pre * up_pre) * INV_ROOT_TWO_PI
@@ -245,21 +408,17 @@
 def attention_backward(
     sid_ref, grid_ref, tok_ref, mg_ref, att_ref, q_ref, k_ref, v_ref, prob_ref, vec_ref, wa_ref,
     tg_ref, ga_ref, sums_ref, diag_ref, cls_ref,
-    k_pad, v_pad, dq, dk, dv,
+    dq, dk, dv,
 ):
     image = pl.program_id(0)
 
     @pl.when(image == 0)
     def _():
-        k_pad[208:256, :] = jnp.zeros((48, 768), BF16)
-        v_pad[208:256, :] = jnp.zeros((48, 768), BF16)
         ga_ref[...] = jnp.zeros_like(ga_ref)
         sums_ref[...] = jnp.zeros_like(sums_ref)
         diag_ref[...] = jnp.zeros_like(diag_ref)
         cls_ref[...] = jnp.zeros_like(cls_ref)
 
-    k_pad[0:208, :] = k_ref[0]
-    v_pad[0:208, :] = v_ref[0]
     attn_scale, first_gain, first_shift = (vec_ref[i : i + 1, :] for i in range(3))
     middle_grad = mg_ref[0]
     attn_low = (middle_grad * attn_scale).astype(BF16)
@@ -275,7 +434,7 @@
 
     for group in range(3):
         lanes = slice(group * 256, group * 256 + 256)
-        k_group, v_group = k_pad[:, lanes], v_pad[:, lanes]
+        k_group, v_group = k_ref[0, :, lanes], v_ref[0, :, lanes]
         q_group = q_ref[0, :, lanes]
         g_group = attended_grad[:, lanes]
         q_stack = jnp.concatenate(
@@ -331,36 +490,6 @@
 
 
 def make_body(wide_size, narrow_size):
-    def shift(value, steps):
-        return lax.ppermute(value, "narrow", [(i, (i - steps) % narrow_size) for i in range(narrow_size)])
-
-    def swap(value, partner):
-        return lax.ppermute(value, "wide", [(j, partner(j)) for j in range(wide_size)])
-
-    def gather_rows(own, me):
-        rows = own.shape[0] // wide_size
-        mine = lax.dynamic_slice_in_dim(own, me * rows, rows, axis=0).astype(F32)
-        across = jnp.stack([shift(mine, k) for k in range(1, narrow_size)])
-        if wide_size != 8:
-            full = lax.all_gather(across, "wide", axis=1, tiled=True)
-            step = own.shape[0] // 8
-            return [lax.dynamic_slice_in_dim(full, ((me % 8) ^ r) * step, step, axis=1) for r in range(8)]
-        one = swap(across, lambda j: j ^ 2 if j % 2 == 0 else j ^ 4)
-        two = swap(across, lambda j: j ^ 4 if j % 2 == 0 else j ^ 2)
-        three = swap(one, lambda j: j ^ 4 if j % 2 == 0 else j ^ 2)
-        held = [across, one, two, three]
-        return held + [swap(value, lambda j: j ^ 1) for value in held]
-
-    def piece_places(me):
-        if wide_size != 8:
-            return jnp.stack([(me % 8) ^ r for r in range(8)]).astype(jnp.int32)
-        core = me % 2
-        first, second = jnp.where(core == 0, 2, 4), jnp.where(core == 0, 4, 2)
-        there = me ^ 1
-        return jnp.stack(
-            [me, me ^ first, me ^ second, me ^ 6, there, there ^ second, there ^ first, there ^ 6]
-        ).astype(jnp.int32)
-
     def body(
         tokens, grid_shape, first_gain, first_shift, qkv_weight, query_bias, value_bias, rel_table, proj_weight,
         proj_bias, attn_scale, second_gain, second_shift, up_weight, up_bias, down_weight, down_bias, mlp_scale,
@@ -369,35 +498,26 @@
         images, slots, width = tokens.shape
         heads, table_size = rel_table.shape
         local = heads * HD
-        me = lax.axis_index("wide")
-        places = piece_places(me)
-
         own_a = jnp.concatenate(
             [jnp.transpose(qkv_weight, (0, 2, 1)).reshape(3 * local, width), proj_weight], axis=0
         )
-        small = jnp.concatenate(
-            [rel_table.astype(F32).reshape(-1)] + [v.astype(F32) for v in (query_bias, value_bias, up_bias)]
-        )
-        count = small.shape[0]
-        small = jnp.pad(small, (0, 8192 - count)).reshape(64, 128)
-        smalls = jnp.stack([small] + [shift(small, k) for k in range(1, narrow_size)]).reshape(narrow_size, -1)
-        table = smalls[:, : heads * table_size].reshape(narrow_size * heads, table_size)
-        at = heads * table_size
-        q_bias = smalls[:, at : at + local].reshape(1, width)
-        v_bias = smalls[:, at + local : at + 2 * local].reshape(1, width)
-        u_bias = smalls[:, at + 2 * local : count]
-
-        pieces_a = gather_rows(own_a, me)
-        pieces_b = gather_rows(up_weight, me)
-        pieces_c = gather_rows(down_weight, me)
-
+        table = rel_table.astype(F32)
+        square = table[:, : SPAN * SPAN].reshape(heads, SPAN, SPAN)[:, ::-1, ::-1]
+        square = jnp.pad(jnp.transpose(square, (1, 0, 2)), ((0, 0), (0, 8 - heads), (0, 128 - SPAN)))
+
+        def small_for(k):
+            def at(v, start):
+                return jnp.pad(v.astype(F32).reshape(1, -1), ((0, 0), (start, width - start - v.size)))
+
+            return jnp.concatenate(
+                [
+                    at(query_bias, k * local), at(value_bias, k * local), at(up_bias, 0),
+                    at(table[:, SPAN * SPAN :].reshape(-1), 0), jnp.zeros((4, width), F32),
+                ]
+            )
+
+        small = jnp.stack([small_for(k) for k in range(narrow_size)])
         all_heads = narrow_size * heads
-        cls = table[:, SPAN * SPAN :]
-        square = table[:, : SPAN * SPAN].reshape(all_heads, SPAN, SPAN)[:, ::-1, ::-1]
-        square = jnp.pad(jnp.transpose(square, (1, 0, 2)), ((0, 0), (0, 16 - all_heads), (0, 128 - SPAN)))
-        diag = pl.pallas_call(
-            diag_kernel, out_shape=jax.ShapeDtypeStruct((len(GRIDS), 2, 16, DIAG), F32), name="diag"
-        )(square)
 
         kinds = jnp.array(GRIDS, jnp.int32)
         sid = jnp.argmax(jnp.all(grid_shape[:, None, :] == kinds[None], axis=-1), axis=-1).astype(jnp.int32)
@@ -407,6 +527,7 @@
 
         smem = pl.BlockSpec(memory_space=pltpu.SMEM)
         anyspace = pl.BlockSpec(memory_space=pl.ANY)
+        vmem = pl.BlockSpec(memory_space=pltpu.VMEM)
 
         def whole(*shape):
             return pl.BlockSpec(shape, lambda i, *_: (0,) * len(shape))
@@ -418,61 +539,75 @@
             return jax.ShapeDtypeStruct(shape, dtype)
 
         params = pltpu.CompilerParams(vmem_limit_bytes=VMEM_LIMIT, dimension_semantics=("arbitrary",))
-        queries, keys, values, probs, attended, branch, weights_a = pl.pallas_call(
-            attention_forward,
-            grid_spec=pltpu.PrefetchScalarGridSpec(
-                num_scalar_prefetch=3,
-                grid=(images,),
-                in_specs=[per_image(slots, width)]
-                + [whole(1, width)] * 5
-                + [
-                    whole(width, width),
-                    pl.BlockSpec((1, 2, 16, DIAG), lambda i, sid_ref, *_: (sid_ref[i], 0, 0, 0)),
-                    smem,
-                ]
-                + [anyspace] * 8,
-                out_specs=[per_image(slots, width)] * 3
-                + [per_image(all_heads, slots, 256), per_image(slots, width), per_image(slots, width)]
-                + [whole(4, width, width)],
-                scratch_shapes=[
-                    pltpu.VMEM((3, width, width), F32),
-                    pltpu.VMEM((256, width), BF16),
-                    pltpu.VMEM((256, width), BF16),
-                    pltpu.SemaphoreType.DMA((8,)),
-                ],
-            ),
-            out_shape=[struct(images, slots, width, dtype=BF16)] * 3
-            + [
+        copies = len(CHUNKS) * (narrow_size - 1 + 7)
+        copies = len(CHUNKS) * (narrow_size - 1 + 7)
+        me = lax.axis_index("wide") % SLICES
+        slices = jnp.stack(
+            [lax.dynamic_slice_in_dim(own_a.reshape(4, local, width), me * PART_ROWS, PART_ROWS, 1).reshape(-1, width)]
+            + [lax.dynamic_slice_in_dim(w, me * SLICE_ROWS, SLICE_ROWS, 0) for w in (up_weight, down_weight)]
+        ).astype(F32)
+        probs, attended, branch, weights_a, small, queries, keys, values, gath_b, gath_c = pl.pallas_call(
+            functools.partial(attention_forward, narrow=narrow_size),
+            grid=(images,),
+            in_specs=[smem, smem, vmem] + [whole(1, width)] * 3 + [vmem] * 4,
+            out_specs=[per_image(all_heads, slots, 256), per_image(slots, width), per_image(slots, width)]
+            + [vmem, vmem] + [anyspace] * 5,
+            scratch_shapes=[
+                pltpu.VMEM((narrow_size - 1, width, width), F32),
+                pltpu.VMEM((images, slots, width), BF16),
+                pltpu.VMEM((images, slots, width), BF16),
+                pltpu.VMEM((images, 256, width), BF16),
+                pltpu.VMEM((images, 256, width), BF16),
+                pltpu.VMEM((images, all_heads, slots, 256), BF16),
+                pltpu.VMEM((16, 8, DIAG), F32),
+                pltpu.VMEM((48, DIAG), F32),
+                pltpu.VMEM((narrow_size - 1, 48, DIAG), F32),
+                pltpu.VMEM((narrow_size, 8, width), F32),
+                pltpu.SemaphoreType.DMA((copies,)),
+                pltpu.SemaphoreType.DMA((copies,)),
+                pltpu.SemaphoreType.DMA((2 * narrow_size - 2,)),
+                pltpu.SemaphoreType.DMA((2 * narrow_size - 2,)),
+                pltpu.SemaphoreType.DMA((3,)),
+            ],
+            out_shape=[
                 struct(images, all_heads, slots, 256, dtype=BF16),
                 struct(images, slots, width, dtype=BF16),
                 struct(images, slots, width),
                 struct(4, width, width, dtype=BF16),
+                struct(narrow_size, 8, width),
+                struct(images, slots, width, dtype=BF16),
+                struct(images, 256, width, dtype=BF16),
+                struct(images, 256, width, dtype=BF16),
+                struct(narrow_size - 1, width, width),
+                struct(narrow_size - 1, width, width),
             ],
-            compiler_params=params,
+            compiler_params=pltpu.CompilerParams(
+                vmem_limit_bytes=VMEM_LIMIT, dimension_semantics=("arbitrary",), collective_id=0,
+                has_side_effects=True,
+            ),
             name="attention_forward",
         )(
-            sid, grid_shape, places, tokens, row(first_gain), row(first_shift), q_bias, v_bias, row(proj_bias),
-            own_a, diag, cls, *pieces_a,
+            sid, grid_shape, tokens, row(first_gain), row(first_shift), row(proj_bias), own_a, slices, square, small,
         )
 
         vec = jnp.concatenate([row(v) for v in (attn_scale, second_gain, second_shift, mlp_scale, down_bias)])
         layer_out, middle_grad, grad_b, grad_c, sums = pl.pallas_call(
             feed_forward,
             grid_spec=pltpu.PrefetchScalarGridSpec(
-                num_scalar_prefetch=2,
+                num_scalar_prefetch=1,
                 grid=(images,),
                 in_specs=[per_image(slots, width)] * 3
-                + [whole(5, width), whole(narrow_size, width), whole(width, width), whole(width, width)]
-                + [anyspace] * 16,
+                + [whole(5, width), whole(narrow_size, 8, width), whole(width, width), whole(width, width)]
+                + [anyspace] * 2,
                 out_specs=[per_image(slots, width)] * 2
                 + [whole(width, width), whole(width, width), whole(7, 8, width)],
                 scratch_shapes=[
-                    pltpu.VMEM((3, width, width), F32),
+                    pltpu.VMEM((6, width, width), F32),
                     pltpu.VMEM((4, width, width), BF16),
                     pltpu.VMEM((4, width, width), BF16),
                     pltpu.VMEM((slots, width), F32),
                     pltpu.VMEM((slots, width), F32),
-                    pltpu.SemaphoreType.DMA((8,)),
+                    pltpu.SemaphoreType.DMA((6,)),
                 ],
             ),
             out_shape=[
@@ -485,7 +620,7 @@
             compiler_params=params,
             name="feed_forward",
         )(
-            grid_shape, places, tokens, branch, cotangent, vec, u_bias, up_weight, down_weight, *pieces_b, *pieces_c
+            grid_shape, tokens, branch, cotangent, vec, small, up_weight, down_weight, gath_b, gath_c
         )
 
         grad_b, grad_c = lax.psum((grad_b, grad_c), "wide")
@@ -501,8 +636,8 @@
                     per_image(slots, width),
                     pl.BlockSpec((1, slots, 256), lambda i, *_: (i, 0, 0)),
                     per_image(slots, width),
-                    per_image(slots, width),
-                    per_image(slots, width),
+                    per_image(256, width),
+                    per_image(256, width),
                     per_image(all_heads, slots, 256),
                     whole(3, width),
                     whole(4, width, width),
@@ -515,8 +650,6 @@
                     whole(3, 3, 8, 256),
                 ],
                 scratch_shapes=[
-                    pltpu.VMEM((256, width), BF16),
-                    pltpu.VMEM((256, width), BF16),
                     pltpu.VMEM((slots, width), BF16),
                     pltpu.VMEM((slots, width), BF16),
                     pltpu.VMEM((slots, width), BF16),

time: 509 us -> 408 us (0.80)
  waiting for transfers between devices: 176 us -> 78.8 us
  Pallas kernels: 197 us -> 254 us
  starting transfers between devices: 52 us -> 0.04 us
  other arithmetic: 14.7 us -> 8.02 us
    ppermute x33 -> x0, waiting for transfers between devices: 93 us -> none  [the longest x12 51.2 us: shift(): lax.ppermute(value, 'narrow', [(i, (i - steps) % narrow_size) for i in ra...]
    pallas_call x2 -> x1, Pallas kernels: 77.8 us -> 136 us  [body(): pl.pallas_call(functools.partial(attention_forward, narrow=narrow_size),...]
    ppermute x33 -> x0, starting transfers between devices: 52 us -> none  [the longest x21 28.9 us: swap(): lax.ppermute(value, 'wide', [(j, partner(j)) for j in range(wide_size)])]
  transfers between devices with their start and end apart: 34 -> 1, of which waited for: 11 -> 1; matrix products, arithmetic and copies ran while one was open for 6% -> 1% of each run, Pallas kernels for 16% -> 1%
where the time goes in v2:
time: 408 us; the launch traced here: 406 us
  Pallas kernels  254 us (62%)
  waiting for transfers between devices  78.8 us (19%)
  local copies, waits for them, and re-layouts  26.5 us (6%)
  blocking collectives  24.5 us (6%)
  between operations  14.3 us (4%)
  other arithmetic  8.02 us (2%)
    pallas_call x1, Pallas kernels, body(): pl.pallas_call(functools.partial(attention_forward, narrow=narrow_size),...  136 us
    psum x1, waiting for transfers between devices, body(): lax.psum((grad_a, table_grad, sums, more), 'wide')  78.7 us
    pallas_call x1, Pallas kernels, body(): pl.pallas_call(feed_forward, grid_spec=pltpu.PrefetchScalarGridSpec(num_s...  73.1 us
    pallas_call x1, Pallas kernels, body(): pl.pallas_call(attention_backward, grid_spec=pltpu.PrefetchScalarGridSpec...  42.4 us
    psum x1, blocking collectives, body(): lax.psum((grad_a, table_grad, sums, more), 'wide')  24.5 us
  transfers between devices with their start and end apart: 1, of which 1 were waited for; matrix products, arithmetic and copies ran while one was open for 1% of the time, Pallas kernels for 1%

profile of v2, /device:TPU:1, one launch (start us, length us, event | category | flops | bytes accessed | tf_op | source)
XLA Modules:
  0.0 406.0 jit_solution(12124123562915835073)
XLA Ops:
  7.2 0.8 slice.68
  8.0 0.7 slice.67
  10.1 0.7 reshape.158
  10.8 1.3 copy.57.grid_ref
  12.2 0.7 reshape.148.gain_ref
  12.8 0.7 reshape.150.shift_ref
  13.5 0.8 compare_reduce_fusion
  14.3 0.7 iota_reduce_fusion
  15.3 0.7 pad.43.table_ref
  16.0 1.3 reshape.152.pb_ref
  17.3 0.7 reshape.137
  18.0 0.7 reshape.142
  18.7 0.7 reshape.160
  19.3 0.7 reshape.162
  20.0 0.7 reshape.164
  20.7 1.3 pad_maximum_fusion.own_ref
  22.4 1.1 dynamic-slice_bitcast_fusion
  23.5 1.0 maximum_convert_fusion.slices
  26.4 136.2 %attention_forward.1 = (bf16[8,12,208,256]{3,2,1,0:T(8,128)(2,1)}, bf16[8,208,768]{2,1,0:T(8,128)(2,1)}, f32[8,208,768]{2,1,0:T(8,128)}, bf16[4,768,768]{2,1,0:T...) custom-call(s32[8]{0:T(128)} %get-tuple-element.39.sid_ref, ...), custom_call_target="tpu_custom_call" | custom-call | tf_op jit(solution)/shard_map/attention_forward/pallas_call | solution.py:549
  162.5 73.1 %feed_forward.1 = (bf16[8,208,768]{2,1,0:T(8,128)(2,1)}, f32[8,208,768]{2,1,0:T(8,128)}, f32[768,768]{1,0:T(8,128)}, f32[768,768]{1,0:T(8,128)}, f32[7,8,768]{2,1,0:T(8,128)}) custom-call(s32[8,2]{1,0:T(8,128)} %copy.57.grid_ref, bf16[8,208,768]{2,1,0:T(8,128)(2,1)} %tok_ref.5, f32[8,208,768]{2,1,0:T(8,128)} %get-tuple-element.40.branch_ref, ...), custom_call_target="tpu_custom_call" | custom-call | tf_op jit(solution)/shard_map/feed_forward/pallas_call | solution.py:594
  235.6 42.4 %attention_backward.1 = (f32[8,208,768]{2,1,0:T(8,128)}, f32[768,768]{1,0:T(8,128)}, f32[4,8,768]{2,1,0:T(8,128)}, f32[8,2,3,8,512]{4,3,2,1,0:T(8,128)}, f32[3,3,8,256]{3,2,1,0:T(8,128)}) custom-call(s32[8]{0:T(128)} %get-tuple-element.39.sid_ref, s32[8,2]{1,0:T(8,128)} %copy.57.grid_ref, bf16[8,208,768]{2,1,0:T(8,128)(2,1)} %tok_ref.5, ...), custom_call_target="tpu_custom_call" | custom-call | tf_op jit(solution)/shard_map/attention_backward/pallas_call | solution.py:629
  278.1 1.0 copy-done.3
  279.4 0.7 pad.53.diag_ref
  280.1 2.4 undiag.1
  282.5 1.0 slice_bitcast_fusion
  284.1 24.5 %all-reduce.11 = (f32[4,768]{1,0:T(4,128)S(1)}, f32[3,2212]{1,0:T(4,128)}, f32[7,768]{1,0:T(8,128)S(1)}) all-reduce(f32[4,768]{1,0:T(4,128)S(1)} %reduce_sum.36, f32[3,2212]{1,0:T(4,128)S(1)} %pad_maximum_fusion.2, f32[7,768]{1,0:T(8,128)S(1)} %reduce_sum.39), channel_id=1, replica_groups=mesh['wide'=8,'narrow'=4] {'wide'}, use_global_device_ids=true, to_apply=%region_3.4 | all-reduce | flops 15084 | bytes 120672 | tf_op jit(solution)/shard_map/psum | solution.py:679
  311.6 78.7 %all-reduce.15.cloned.1.call-done = (f32[768,768]{1,0:T(8,128)}, f32[768,768]{1,0:T(8,128)}, f32[768,768]{1,0:T(8,128)}) async-done(((f32[768,768]{1,0:T(8,128)}, f32[768,768]{1,0:T(8,128)}, f32[768,768]{1,0:T(8,128)}), (f32[768,768]{1,0:T(8,128)}, f32[768,768]{1,0:T(8,128)}, f32[768,768]{1,0:T(8,128)})) %all-reduce.15.cloned.1.call-update) | async-done | bytes 7077904 | tf_op jit(solution)/shard_map/psum | solution.py:679
  390.4 2.9 slice.71
  393.3 1.9 slice.75
  395.2 1.4 copy.64
  396.6 1.1 copy-done.1
  397.8 1.4 copy.65
  (53 shorter events, 7.9 us)
Async XLA Ops:
  7.2 383.2 %all-reduce.15.cloned.1.call-start = ((), (), s32[]{:S(2)}) async-start(), calls=%async_computation | async-start | bytes 14155776 | tf_op jit(solution)/shard_map/psum | solution.py:679
  12.8 11.6 %copy-start.7 = (f32[1,768]{1,0:T(1,128)}, f32[1,768]{1,0:T(1,128)S(1)}, u32[]{:S(2)}) copy-start(f32[1,768]{1,0:T(1,128)S(1)} %reshape.148.gain_ref) | copy-start | bytes 9220
  13.5 10.9 %copy-start.8 = (f32[1,768]{1,0:T(1,128)}, f32[1,768]{1,0:T(1,128)S(1)}, u32[]{:S(2)}) copy-start(f32[1,768]{1,0:T(1,128)S(1)} %reshape.150.shift_ref) | copy-start | bytes 9220
  22.0 4.3 %copy-start = (bf16[768,768]{1,0:T(8,128)(2,1)}, bf16[768,768]{1,0:T(8,128)(2,1)S(1)}, u32[]{:S(2)}) copy-start(bf16[768,768]{1,0:T(8,128)(2,1)S(1)} %pad_maximum_fusion.own_ref) | copy-start | bytes 3538948
  278.0 1.1 copy-start.3
  278.1 5.7 %copy-start.6 = (f32[3,3,8,256]{3,2,1,0:T(8,128)S(1)}, f32[3,3,8,256]{3,2,1,0:T(8,128)}, u32[]{:S(2)}) copy-start(f32[3,3,8,256]{3,2,1,0:T(8,128)} %get-tuple-element.56) | copy-start | bytes 221188
  278.1 5.9 %copy-start.5 = (f32[4,8,768]{2,1,0:T(8,128)S(1)}, f32[4,8,768]{2,1,0:T(8,128)}, u32[]{:S(2)}) copy-start(f32[4,8,768]{2,1,0:T(8,128)} %get-tuple-element.53) | copy-start | bytes 294916
  278.1 5.9 %copy-start.4 = (f32[7,8,768]{2,1,0:T(8,128)S(1)}, f32[7,8,768]{2,1,0:T(8,128)}, u32[]{:S(2)}) copy-start(f32[7,8,768]{2,1,0:T(8,128)} %get-tuple-element.57) | copy-start | bytes 516100
  278.1 32.4 %copy-start.9 = (bf16[768]{0:T(1024)(128)(2,1)S(1)}, bf16[768]{0:T(1024)(128)(2,1)}, u32[]{:S(2)}) copy-start(bf16[768]{0:T(1024)(128)(2,1)} %param.37) | copy-start | bytes 4612
  278.1 32.9 %copy-start.10 = (bf16[768]{0:T(1024)(128)(2,1)S(1)}, bf16[768]{0:T(1024)(128)(2,1)}, u32[]{:S(2)}) copy-start(bf16[768]{0:T(1024)(128)(2,1)} %param.30) | copy-start | bytes 4612
  390.4 4.9 %copy-start.2 = (f32[768,768]{1,0:T(8,128)S(1)}, f32[768,768]{1,0:T(8,128)}, u32[]{:S(2)}) copy-start(f32[768,768]{1,0:T(8,128)} %get-tuple-element.104) | copy-start | bytes 7077892
  395.2 2.5 copy-start.1
Sparse Core Ops, SparseCore 0:
  278.2 112.1 all-reduce.14

commit v3 on v2

--- a/solution.py
+++ b/solution.py
@@ -95,22 +95,32 @@
 CHUNKS = tuple((group, at, 24) for group in range(3) for at in (0, 24, 48, 72))
 
 
-class Gather:
+class Neighbours:
+    def __init__(self):
+        self.wide = lax.axis_index("wide")
+        self.me = self.wide % SLICES
+        self.base = self.wide - self.me
+        self.core = core = self.me % 2
+        x_bit, y_bit = (self.me // 2) % 2, self.me // 4
+        over_x, over_y = self.me + 2 - 4 * x_bit, self.me + 4 - 8 * y_bit
+        self.first = over_x * (1 - core) + over_y * core
+        self.second = over_y * (1 - core) + over_x * core
+        self.first_bit = x_bit * (1 - core) + y_bit * core
+        self.second_bit = y_bit * (1 - core) + x_bit * core
+        self.third = over_x + over_y - self.me
+        self.twin = self.me + 1 - 2 * core
+
+    def beyond(self, step):
+        size = SLICES << step
+        return self.wide + size - 2 * size * ((self.wide // size) % 2)
+
+
+class Gather(Neighbours):
     def __init__(self, narrow, slices, buffers, send, recv):
+        super().__init__()
         self.narrow, self.slices, self.buffers, self.send, self.recv = narrow, slices, buffers, send, recv
         self.z = lax.axis_index("narrow")
-        wide = lax.axis_index("wide")
-        self.me = wide % SLICES
-        self.base = wide - self.me
-        core = self.me % 2
-        over_x = self.me + 2 - 4 * ((self.me // 2) % 2)
-        over_y = self.me + 4 - 8 * (self.me // 4)
-        self.first = over_x * (1 - core) + over_y * core
-        self.second = over_y * (1 - core) + over_x * core
-        self.third = over_x + over_y - self.me
-        self.twin = self.me + 1 - 2 * core
         self.per_chunk = narrow - 1 + 7
-        self.started = []
 
     def copy(self, chunk, phase, piece):
         group, at, rows = CHUNKS[chunk]
@@ -339,154 +349,381 @@
             keep(which).wait()
 
 
+class Reduce:
+    STEPS = 7
+
+    def __init__(self, near, beyond, source, half, quarter, eighth, between, total, send, recv, first_sem):
+        self.near, self.beyond, self.source, self.total = near, beyond, source, total
+        self.half, self.quarter, self.eighth, self.between = half, quarter, eighth, between
+        self.send, self.recv, self.first_sem = send, recv, first_sem
+        self.rows = eighth.shape[0]
+
+    @staticmethod
+    def scratch(rows, width, beyond):
+        shapes = [(rows // 2, width), (rows // 4, width), (rows // 8, width), (2 * max(beyond, 1), rows // 8, width)]
+        return [pltpu.VMEM(shape, F32) for shape in shapes]
+
+    def span(self, ref, start, count):
+        return ref.at[pl.ds(pl.multiple_of(start, 8), count), :]
+
+    def value(self, ref, start, count):
+        return ref[pl.ds(pl.multiple_of(start, 8), count), :]
+
+    def copy(self, step):
+        near, rows = self.near, self.rows
+        half_at = near.core * 4 * rows
+        quarter_at = half_at + near.first_bit * 2 * rows
+        own_at = quarter_at + near.second_bit * rows
+        if step == 0:
+            source, target, to = self.span(self.source, (1 - near.core) * 4 * rows, 4 * rows), self.half, near.twin
+        elif step == 1:
+            source, target, to = (
+                self.span(self.half, (1 - near.first_bit) * 2 * rows, 2 * rows), self.quarter, near.first
+            )
+        elif step == 2:
+            source, target, to = self.span(self.quarter, (1 - near.second_bit) * rows, rows), self.eighth, near.second
+        else:
+            at, count, to = (
+                (own_at, rows, near.second), (quarter_at, 2 * rows, near.first), (half_at, 4 * rows, near.twin)
+            )[step - 3]
+            source = target = self.span(self.total, at, count)
+        return self.remote(source, target, step, near.base + to)
+
+    def remote(self, source, target, place, to):
+        place += self.first_sem
+        return pltpu.make_async_remote_copy(
+            src_ref=source, dst_ref=target, send_sem=self.send.at[place], recv_sem=self.recv.at[place],
+            device_id={"wide": to}, device_id_type=MESH,
+        )
+
+    def run(self, step):
+        near, rows = self.near, self.rows
+        if step > 0:
+            self.copy(step - 1).wait_recv()
+        if step == 1:
+            self.half[...] += self.value(self.source, near.core * 4 * rows, 4 * rows)
+        if step == 2:
+            self.quarter[...] += self.value(self.half, near.first_bit * 2 * rows, 2 * rows)
+        if step == 3:
+            summed = self.eighth[...] + self.value(self.quarter, near.second_bit * rows, rows)
+            for i in range(self.beyond):
+                self.between[2 * i] = summed
+                copy = self.remote(self.between.at[2 * i], self.between.at[2 * i + 1], 6 + i, near.beyond(i))
+                copy.start()
+                copy.wait()
+                summed = self.between[2 * i] + self.between[2 * i + 1]
+            own_at = (near.core * 4 + near.first_bit * 2 + near.second_bit) * rows
+            self.total[pl.ds(pl.multiple_of(own_at, 8), rows), :] = summed
+        if step < 6:
+            self.copy(step).start()
+
+    def drain(self):
+        for step in range(6):
+            self.copy(step).wait_send()
+
+
+def greet(near, beyond):
+    sem = pltpu.get_barrier_semaphore()
+    for k in range(1, SLICES):
+        other = near.base + (near.me + k) % SLICES
+        pl.semaphore_signal(sem, inc=1, device_id={"wide": other}, device_id_type=MESH)
+    for i in range(beyond):
+        pl.semaphore_signal(sem, inc=1, device_id={"wide": near.beyond(i)}, device_id_type=MESH)
+    pl.semaphore_wait(sem, SLICES - 1 + beyond)
+
+
+PAIR = 2
+FF_TICKS = {
+    4: ((0, 0), (1, 0)), 5: ((0, 1), (1, 1)), 7: ((0, 2),), 9: ((1, 2), (0, 3)), 10: ((0, 4), (1, 3)), 12: ((0, 5), (1, 4)),
+    14: ((1, 5),), 15: ((0, 6),),
+}
+
+
 def feed_forward(
     grid_ref, tok_ref, branch_ref, cot_ref, vec_ref, small_ref, ownb_ref, ownc_ref, gath_b, gath_c,
-    out_ref, mg_ref, gb_ref, gc_ref, sums_ref,
-    stage, wb, wc, mlp_acc, second_acc, sems,
+    out_ref, mg_ref, out_b, out_c, sums_ref,
+    total_b, total_c, stage, wb, wc, second_ins, branch_lows, mlp_acc, second_acc, grad_b, grad_c, *rest, beyond,
 ):
-    image = pl.program_id(0)
-
-    @pl.when(image == 0)
-    def _():
+    loads, send, recv = rest[8:]
+    slot, pair = pl.program_id(0), pl.program_id(1)
+    slots, pairs = pl.num_programs(0), pl.num_programs(1)
+    rows = PAIR * 208
+    near = Neighbours()
+    sums = [
+        Reduce(near, beyond, grad, *rest[4 * i : 4 * i + 4], total, send, recv, i * (6 + beyond))
+        for i, (grad, total) in enumerate(((grad_b, total_b), (grad_c, total_c)))
+    ]
+
+    def load(which, at):
+        return pltpu.make_async_copy((gath_b, gath_c)[which].at[at], stage.at[which], loads.at[which])
+
+    @pl.when((slot == 0) & (pair == 0))
+    def _():
+        greet(near, beyond)
+        wb[0] = ownb_ref[...]
+        wc[0] = ownc_ref[...]
+        grad_b[...] = jnp.zeros_like(grad_b)
+        grad_c[...] = jnp.zeros_like(grad_c)
+        sums_ref[...] = jnp.zeros_like(sums_ref)
+
+    @pl.when((pair == 0) & (slot < slots - 1))
+    def _():
+        load(0, slot).start()
+        load(1, slot).start()
+
+    for when, steps in FF_TICKS.items():
+        @pl.when(slot * pairs + pair == when)
+        def _():
+            for chain, step in steps:
+                sums[chain].run(step)
+
+    attn_scale, second_gain, second_shift, mlp_scale, down_bias = (vec_ref[i : i + 1, :] for i in range(5))
+
+    def residual():
+        branch = branch_ref[...].reshape(rows, 768)
+        return branch, tok_ref[...].reshape(rows, 768).astype(F32) + attn_scale * branch
+
+    def masked_cotangent():
+        at = lax.broadcasted_iota(jnp.int32, (rows, 1), 0)
+        limit = jnp.zeros((rows, 1), jnp.int32)
+        for i in range(PAIR):
+            image = pair * PAIR + i
+            inside = (at >= i * 208) & (at < (i + 1) * 208)
+            limit = jnp.where(inside, grid_ref[image, 0] * grid_ref[image, 1] + i * 208, limit)
+        return jnp.where(at <= limit, cot_ref[...].reshape(rows, 768).astype(F32), 0.0)
+
+    @pl.when(slot == 0)
+    def _():
+        _, middle = residual()
+        normed, _ = norm_stats(middle)
+        second_ins[pair] = (normed * second_gain + second_shift).astype(BF16)
+        branch_lows[pair] = (masked_cotangent() * mlp_scale).astype(BF16)
+        mlp_acc[pair] = jnp.zeros((rows, 768), F32)
+        second_acc[pair] = jnp.zeros((rows, 768), F32)
+
+    second_in, branch_low = second_ins[pair], branch_lows[pair]
+    up, down = wb[slot % 2], wc[slot % 2]
+    up_pre = dot_nn(second_in, up) + small_ref[slot, 2:3, :]
+    cdf = 0.5 * (1.0 + lax.erf(up_pre * INV_ROOT_TWO))
+    hidden = (up_pre * cdf).astype(BF16)
+    slope = cdf + up_pre * jnp.exp(-0.5 * up_pre * up_pre) * INV_ROOT_TWO_PI
+    mlp_acc[pair] += dot_nn(hidden, down)
+    pre_low = (dot_nt(branch_low, down) * slope).astype(BF16)
+    second_acc[pair] += dot_nt(pre_low, up)
+
+    @pl.when(slot == 0)
+    def _():
+        grad_c[...] += dot_tn(hidden, branch_low)
+        grad_b[...] += dot_tn(second_in, pre_low)
+        sums_ref[6] += fold_rows(pre_low.astype(F32))
+
+    @pl.when((pair == pairs - 1) & (slot < slots - 1))
+    def _():
+        for which, weights in enumerate((wb, wc)):
+            load(which, slot).wait()
+            weights[(slot + 1) % 2] = stage[which].astype(BF16)
+
+    @pl.when(slot == slots - 1)
+    def _():
+        branch, middle = residual()
+        normed, inv = norm_stats(middle)
+        out_grad = masked_cotangent()
+        mlp_branch = mlp_acc[pair] + down_bias
+        out_ref[...] = (middle + mlp_scale * mlp_branch).astype(BF16).reshape(PAIR, 208, 768)
+        second_grad = second_acc[pair]
+        middle_grad = out_grad + norm_back(second_grad, normed, inv, second_gain)
+        mg_ref[...] = middle_grad.reshape(PAIR, 208, 768)
+        sums_ref[0] += fold_rows(out_grad * mlp_branch)
+        sums_ref[1] += fold_rows(out_grad)
+        sums_ref[2] += fold_rows(second_grad * normed)
+        sums_ref[3] += fold_rows(second_grad)
+        sums_ref[4] += fold_rows(middle_grad * branch)
+        sums_ref[5] += fold_rows(middle_grad)
+
+    @pl.when((slot == slots - 1) & (pair == pairs - 1))
+    def _():
+        sums[1].run(6)
         copies = [
-            pltpu.make_async_copy(gath.at[slot], stage.at[which * 3 + slot], sems.at[which * 3 + slot])
-            for which, gath in enumerate((gath_b, gath_c))
-            for slot in range(3)
+            pltpu.make_async_copy(chain.total, out, loads.at[i])
+            for i, (chain, out) in enumerate(zip(sums, (out_b, out_c)))
         ]
         for copy in copies:
             copy.start()
-        wb[0] = ownb_ref[...]
-        wc[0] = ownc_ref[...]
-        for which, weights in enumerate((wb, wc)):
-            for slot in range(3):
-                copies[which * 3 + slot].wait()
-                weights[slot + 1] = stage[which * 3 + slot].astype(BF16)
-        gb_ref[...] = jnp.zeros_like(gb_ref)
-        gc_ref[...] = jnp.zeros_like(gc_ref)
-        sums_ref[...] = jnp.zeros_like(sums_ref)
-
-    attn_scale, second_gain, second_shift, mlp_scale, down_bias = (vec_ref[i : i + 1, :] for i in range(5))
-    branch = branch_ref[0]
-    middle = tok_ref[0].astype(F32) + attn_scale * branch
-    normed, inv = norm_stats(middle)
-    second_in = (normed * second_gain + second_shift).astype(BF16)
-    valid = lax.broadcasted_iota(jnp.int32, (208, 1), 0) <= grid_ref[image, 0] * grid_ref[image, 1]
-    out_grad = jnp.where(valid, cot_ref[0].astype(F32), 0.0)
-    branch_low = (out_grad * mlp_scale).astype(BF16)
-    mlp_acc[...] = jnp.zeros_like(mlp_acc)
-    second_acc[...] = jnp.zeros_like(second_acc)
-
-    @pl.loop(0, 4)
-    def _(slot):
-        up_pre = dot_nn(second_in, wb[slot]) + small_ref[slot, 2:3, :]
-        cdf = 0.5 * (1.0 + lax.erf(up_pre * INV_ROOT_TWO))
-        hidden = (up_pre * cdf).astype(BF16)
-        slope = cdf + up_pre * jnp.exp(-0.5 * up_pre * up_pre) * INV_ROOT_TWO_PI
-        mlp_acc[...] += dot_nn(hidden, wc[slot])
-        pre_low = (dot_nt(branch_low, wc[slot]) * slope).astype(BF16)
-        second_acc[...] += dot_nt(pre_low, wb[slot])
-
-        @pl.when(slot == 0)
-        def _():
-            gc_ref[...] += dot_tn(hidden, branch_low)
-            gb_ref[...] += dot_tn(second_in, pre_low)
-            sums_ref[6] += fold_rows(pre_low.astype(F32))
-
-    mlp_branch = mlp_acc[...] + down_bias
-    out_ref[0] = (middle + mlp_scale * mlp_branch).astype(BF16)
-    second_grad = second_acc[...]
-    middle_grad = out_grad + norm_back(second_grad, normed, inv, second_gain)
-    mg_ref[0] = middle_grad
-    sums_ref[0] += fold_rows(out_grad * mlp_branch)
-    sums_ref[1] += fold_rows(out_grad)
-    sums_ref[2] += fold_rows(second_grad * normed)
-    sums_ref[3] += fold_rows(second_grad)
-    sums_ref[4] += fold_rows(middle_grad * branch)
-    sums_ref[5] += fold_rows(middle_grad)
+        for copy in copies:
+            copy.wait()
+        for chain in sums:
+            chain.drain()
+
+
+SMALL_ROWS = 128
+AB_TICKS = {8: (0,), 10: (1,), 13: (2,), 15: (3,)}
+AB_LAST = (4, 5, 6)
 
 
 def attention_backward(
-    sid_ref, grid_ref, tok_ref, mg_ref, att_ref, q_ref, k_ref, v_ref, prob_ref, vec_ref, wa_ref,
-    tg_ref, ga_ref, sums_ref, diag_ref, cls_ref,
-    dq, dk, dv,
+    sid_ref, grid_ref, tok_ref, mg_ref, att_ref, q0_ref, k0_ref, v0_ref, p0_ref, q_ref, k_ref, v_ref, p1_ref, p2_ref,
+    vec_ref, wa_ref, ff_sums_ref,
+    tg_ref, total_out, late_total,
+    total, grads, attn_lows, kept, dq, dk, dv, lines, edges, sums, late, late_in, late_between,
+    half, quarter, eighth, between, send, recv, late_send, late_recv, local, beyond,
 ):
-    image = pl.program_id(0)
-
-    @pl.when(image == 0)
-    def _():
-        ga_ref[...] = jnp.zeros_like(ga_ref)
-        sums_ref[...] = jnp.zeros_like(sums_ref)
-        diag_ref[...] = jnp.zeros_like(diag_ref)
-        cls_ref[...] = jnp.zeros_like(cls_ref)
-
+    step = pl.program_id(0)
+    images = pl.num_programs(0) // 2
+    near = Neighbours()
+    reduction = Reduce(near, beyond, grads, half, quarter, eighth, between, total, send, recv, 0)
     attn_scale, first_gain, first_shift = (vec_ref[i : i + 1, :] for i in range(3))
-    middle_grad = mg_ref[0]
-    attn_low = (middle_grad * attn_scale).astype(BF16)
-    attended_grad = dot_nt(attn_low, wa_ref[3]).astype(BF16)
-    ga_ref[576:768, :] += dot_tn(att_ref[0], attn_low)[0:192, :]
-
-    p, s, limit, later, p_patch, s_patch = slot_masks(grid_ref[image, 0], grid_ref[image, 1], True)
-    both = p_patch & s_patch
-    flip = (
-        lax.broadcasted_iota(jnp.int32, (208, 208), 0) + lax.broadcasted_iota(jnp.int32, (208, 208), 1) == 207
-    ).astype(BF16)
     head_of = lax.broadcasted_iota(jnp.int32, (1, 256), 1) // HD
 
-    for group in range(3):
-        lanes = slice(group * 256, group * 256 + 256)
-        k_group, v_group = k_ref[0, :, lanes], v_ref[0, :, lanes]
-        q_group = q_ref[0, :, lanes]
-        g_group = attended_grad[:, lanes]
-        q_stack = jnp.concatenate(
-            [jnp.where(head_of == h, q_group, jnp.zeros_like(q_group)) for h in range(4)], axis=0
-        )
-        g_stack = jnp.concatenate(
-            [jnp.where(head_of == h, g_group, jnp.zeros_like(g_group)) for h in range(4)], axis=0
-        )
+    def stack(group):
+        return jnp.concatenate([jnp.where(head_of == h, group, jnp.zeros_like(group)) for h in range(4)], axis=0)
+
+    def merge(mixed):
+        out = mixed[0:208]
+        for h in range(1, 4):
+            out = jnp.where(head_of == h, mixed[h * 208 : (h + 1) * 208], out)
+        return out
+
+    def heads_back(q_group, k_group, v_group, g_group, prob_at, each):
+        q_stack, g_stack = stack(q_group), stack(g_group)
         prob_grads = dot_nt(g_stack, v_group)
         lows = []
         for h in range(4):
-            prob = prob_ref[0, group * 4 + h].astype(F32)
+            prob = prob_at(h).astype(F32)
             prob_grad = prob_grads[h * 208 : (h + 1) * 208]
-            inner = jnp.sum(prob * prob_grad, axis=-1, keepdims=True)
-            score_grad = prob * (prob_grad - inner)
+            score_grad = prob * (prob_grad - jnp.sum(prob * prob_grad, axis=-1, keepdims=True))
             low = score_grad.astype(BF16)
             lows.append(low)
-            if group == 0 and h < 3:
-                rest = (score_grad - low.astype(F32)).astype(BF16)
-                turned = dot_nn(flip, low) + dot_nn(flip, rest)
-                patches = jnp.where(both, turned, 0.0)
-                edge = turned - patches
-                parts = [jnp.where(later, patches, 0.0), jnp.where(later, 0.0, patches)]
-                for which in range(2):
-                    wide = jnp.concatenate([parts[which], jnp.zeros((208, 256), F32)], axis=1)
-                    lined = pltpu.roll(wide, 0, 1, stride=1, stride_axis=0)
-                    diag_ref[pl.ds(sid_ref[image], 1), which, h] += fold_rows(lined)[None]
-                class_query = jnp.where((p == 0) & s_patch, edge, 0.0)
-                class_key = jnp.where(p_patch & (s == 0), edge, 0.0)
-                cls_ref[0, h] += fold_rows(class_query)
-                cls_ref[1, h] += fold_rows(class_key)
-                cls_ref[2, h] += fold_rows(edge - class_query - class_key)
+            each(h, score_grad, low)
         low_stack = jnp.concatenate(lows, axis=0)
-        mixed = dot_nn(low_stack, k_group)
-        out = mixed[0:208]
-        for h in range(1, 4):
-            out = jnp.where(head_of == h, mixed[h * 208 : (h + 1) * 208], out)
-        dq[:, lanes] = out.astype(BF16) * jnp.asarray(HD ** -0.5, BF16)
-        dk[:, lanes] = dot_tn(low_stack, q_stack)[0:208].astype(BF16)
-        prob_stack = jnp.concatenate([prob_ref[0, group * 4 + h] for h in range(4)], axis=0)
-        dv[:, lanes] = dot_tn(prob_stack, g_stack)[0:208].astype(BF16)
+        prob_stack = jnp.concatenate([prob_at(h) for h in range(4)], axis=0)
+        return (
+            merge(dot_nn(low_stack, k_group)).astype(BF16) * jnp.asarray(HD ** -0.5, BF16),
+            dot_tn(low_stack, q_stack)[0:208].astype(BF16),
+            dot_tn(prob_stack, g_stack)[0:208].astype(BF16),
+        )
+
+    @pl.when(step == 0)
+    def _():
+        greet(near, beyond)
+        grads[...] = jnp.zeros_like(grads)
+        sums[...] = jnp.zeros_like(sums)
+        lines[...] = jnp.zeros_like(lines)
+        edges[...] = jnp.zeros_like(edges)
+        late[...] = jnp.zeros_like(late)
 
     normed, inv = norm_stats(tok_ref[0].astype(F32))
-    first_in = (normed * first_gain + first_shift).astype(BF16)
-    for c, grad in enumerate((dq, dk, dv)):
-        ga_ref[c * 192 : (c + 1) * 192, :] += dot_tn(grad[:, 0:256], first_in)[0:192, :]
-    first_grad = dot_nn(dq[...], wa_ref[0]) + dot_nn(dk[...], wa_ref[1]) + dot_nn(dv[...], wa_ref[2])
-    tg_ref[0] = middle_grad + norm_back(first_grad, normed, inv, first_gain)
-    sums_ref[0] += fold_rows(first_grad * normed)
-    sums_ref[1] += fold_rows(first_grad)
-    sums_ref[2] += fold_rows(dq[...].astype(F32))
-    sums_ref[3] += fold_rows(dv[...].astype(F32))
+
+    @pl.when(step < images)
+    def _():
+        attn_low = (mg_ref[0] * attn_scale).astype(BF16)
+        attn_lows[step] = attn_low
+        g_group = dot_nt(attn_low, wa_ref[3, 0:256, :]).astype(BF16)
+        grads[576:768, :] += dot_tn(att_ref[0], attn_low)[0:192, :]
+        p, s, limit, later, p_patch, s_patch = slot_masks(grid_ref[step, 0], grid_ref[step, 1], True)
+        both = p_patch & s_patch
+        flip = (
+            lax.broadcasted_iota(jnp.int32, (208, 208), 0) + lax.broadcasted_iota(jnp.int32, (208, 208), 1) == 207
+        ).astype(BF16)
+        kind = sid_ref[step]
+
+        def table_grad(h, score_grad, low):
+            if h == 3:
+                return
+            rest = (score_grad - low.astype(F32)).astype(BF16)
+            turned = dot_nn(flip, low) + dot_nn(flip, rest)
+            patches = jnp.where(both, turned, 0.0)
+            edge = turned - patches
+            for which, part in enumerate((jnp.where(later, patches, 0.0), jnp.where(later, 0.0, patches))):
+                wide = jnp.concatenate([part, jnp.zeros((208, 256), F32)], axis=1)
+                folded = jnp.sum(pltpu.roll(wide, 0, 1, stride=1, stride_axis=0), axis=0, keepdims=True)
+                row = which * 3 + h
+                for shape_at in range(len(GRIDS)):
+                    lines[shape_at, row : row + 1, :] += jnp.where(kind == shape_at, folded, 0.0)
+            class_query = jnp.where((p == 0) & s_patch, edge, 0.0)
+            class_key = jnp.where(p_patch & (s == 0), edge, 0.0)
+            for at, part in enumerate((class_query, class_key, edge - class_query - class_key)):
+                edges[at * 3 + h] += fold_rows(part)
+
+        own = heads_back(q0_ref[0], k0_ref[0], v0_ref[0], g_group, lambda h: p0_ref[0, h], table_grad)
+        first_in = (normed * first_gain + first_shift).astype(BF16)
+        for c, grad in enumerate(own):
+            kept[c, step] = grad
+            grads[c * 192 : (c + 1) * 192, :] += dot_tn(grad, first_in)[0:192, :]
+        sums[0] += fold_rows(own[0].astype(F32))
+        sums[1] += fold_rows(own[2].astype(F32))
+
+    @pl.when(step == images)
+    def _():
+        grads[768 : 768 + SMALL_ROWS, :] = jnp.zeros((SMALL_ROWS, 768), F32)
+        for shape_at in range(len(GRIDS)):
+            grads[768 + shape_at * 8 : 776 + shape_at * 8, 0:DIAG] = lines[shape_at]
+        for at in range(9):
+            grads[832 + at : 833 + at, 0:256] = jnp.sum(edges[at], axis=0, keepdims=True)
+        for at in range(2):
+            grads[848 + at : 849 + at, 0:256] = jnp.sum(sums[at], axis=0, keepdims=True)
+        for at in range(7):
+            grads[856 + at : 857 + at, :] = jnp.sum(ff_sums_ref[at], axis=0, keepdims=True)
+
+    for when, steps in AB_TICKS.items():
+        @pl.when(step == when)
+        def _():
+            for at in steps:
+                reduction.run(at)
+
+    @pl.when(step >= images)
+    def _():
+        image = step - images
+        attn_low = attn_lows[image]
+        for c, ref in enumerate((dq, dk, dv)):
+            ref[:, 0:256] = kept[c, image]
+        for group in (1, 2):
+            lanes = slice(group * 256, group * 256 + 256)
+            g_group = dot_nt(attn_low, wa_ref[3, lanes, :]).astype(BF16)
+            probs = (p1_ref, p2_ref)[group - 1]
+            parts = heads_back(
+                q_ref[0, :, lanes], k_ref[0, :, lanes], v_ref[0, :, lanes], g_group,
+                lambda h: probs[0, h], lambda *_: None,
+            )
+            for ref, part in zip((dq, dk, dv), parts):
+                ref[:, lanes] = part
+        first_grad = dot_nn(dq[...], wa_ref[0]) + dot_nn(dk[...], wa_ref[1]) + dot_nn(dv[...], wa_ref[2])
+        tg_ref[0] = mg_ref[0] + norm_back(first_grad, normed, inv, first_gain)
+        late[0:8, :] += fold_rows(first_grad * normed)
+        late[8:16, :] += fold_rows(first_grad)
+
+    @pl.when(step == 2 * images - 1)
+    def _():
+        copies = [
+            pltpu.make_async_remote_copy(
+                src_ref=late, dst_ref=late_in.at[k - 1], send_sem=late_send.at[k - 1], recv_sem=late_recv.at[k - 1],
+                device_id={"wide": near.base + (near.me + k) % SLICES}, device_id_type=MESH,
+            )
+            for k in range(1, SLICES)
+        ]
+        for copy in copies:
+            copy.start()
+        for at in AB_LAST:
+            reduction.run(at)
+        for copy in copies:
+            copy.wait()
+        summed = late[...]
+        for k in range(SLICES - 1):
+            summed = summed + late_in[k]
+        for i in range(beyond):
+            late_between[2 * i] = summed
+            copy = pltpu.make_async_remote_copy(
+                src_ref=late_between.at[2 * i], dst_ref=late_between.at[2 * i + 1],
+                send_sem=late_send.at[SLICES - 1 + i], recv_sem=late_recv.at[SLICES - 1 + i],
+                device_id={"wide": near.beyond(i)}, device_id_type=MESH,
+            )
+            copy.start()
+            copy.wait()
+            summed = late_between[2 * i] + late_between[2 * i + 1]
+        late_total[...] = summed
+        copy = pltpu.make_async_copy(total, total_out, local.at[0])
+        copy.start()
+        copy.wait()
+        reduction.drain()
 
 
 def make_body(wide_size, narrow_size):
@@ -591,25 +828,42 @@
         )
 
         vec = jnp.concatenate([row(v) for v in (attn_scale, second_gain, second_shift, mlp_scale, down_bias)])
+        beyond = (wide_size // SLICES).bit_length() - 1
+        rows = PAIR * slots
+        pairs = images // PAIR
+        last = narrow_size - 1
+
+        def remote_params(at):
+            return pltpu.CompilerParams(
+                vmem_limit_bytes=VMEM_LIMIT, collective_id=at, has_side_effects=True,
+            )
+
+        ends = pl.BlockSpec((PAIR, slots, width), lambda s, i: (jnp.where((s > 0) & (s < last), pairs - 1, i), 0, 0))
+        outs = pl.BlockSpec((PAIR, slots, width), lambda s, i: (jnp.where(s < last, 0, i), 0, 0))
         layer_out, middle_grad, grad_b, grad_c, sums = pl.pallas_call(
-            feed_forward,
-            grid_spec=pltpu.PrefetchScalarGridSpec(
-                num_scalar_prefetch=1,
-                grid=(images,),
-                in_specs=[per_image(slots, width)] * 3
-                + [whole(5, width), whole(narrow_size, 8, width), whole(width, width), whole(width, width)]
-                + [anyspace] * 2,
-                out_specs=[per_image(slots, width)] * 2
-                + [whole(width, width), whole(width, width), whole(7, 8, width)],
-                scratch_shapes=[
-                    pltpu.VMEM((6, width, width), F32),
-                    pltpu.VMEM((4, width, width), BF16),
-                    pltpu.VMEM((4, width, width), BF16),
-                    pltpu.VMEM((slots, width), F32),
-                    pltpu.VMEM((slots, width), F32),
-                    pltpu.SemaphoreType.DMA((6,)),
-                ],
-            ),
+            functools.partial(feed_forward, beyond=beyond),
+            grid=(narrow_size, pairs),
+            in_specs=[smem] + [ends] * 3 + [vmem] * 4 + [anyspace] * 2,
+            out_specs=[outs] * 2 + [anyspace] * 2 + [vmem],
+            scratch_shapes=[
+                pltpu.VMEM((width, width), F32),
+                pltpu.VMEM((width, width), F32),
+                pltpu.VMEM((2, width, width), F32),
+                pltpu.VMEM((2, width, width), BF16),
+                pltpu.VMEM((2, width, width), BF16),
+                pltpu.VMEM((pairs, rows, width), BF16),
+                pltpu.VMEM((pairs, rows, width), BF16),
+                pltpu.VMEM((pairs, rows, width), F32),
+                pltpu.VMEM((pairs, rows, width), F32),
+                pltpu.VMEM((width, width), F32),
+                pltpu.VMEM((width, width), F32),
+            ]
+            + Reduce.scratch(width, width, beyond) * 2
+            + [
+                pltpu.SemaphoreType.DMA((2,)),
+                pltpu.SemaphoreType.DMA((2 * (6 + beyond),)),
+                pltpu.SemaphoreType.DMA((2 * (6 + beyond),)),
+            ],
             out_shape=[
                 struct(images, slots, width, dtype=BF16),
                 struct(images, slots, width),
@@ -617,75 +871,82 @@
                 struct(width, width),
                 struct(7, 8, width),
             ],
-            compiler_params=params,
+            compiler_params=remote_params(1),
             name="feed_forward",
+        )(grid_shape, tokens, branch, cotangent, vec, small, up_weight, down_weight, gath_b, gath_c)
+
+        def first_pass(*shape):
+            return pl.BlockSpec((1,) + shape, lambda i: (jnp.minimum(i, images - 1),) + (0,) * len(shape))
+
+        def second_pass(*shape, at=0):
+            return pl.BlockSpec((1,) + shape, lambda i: (jnp.maximum(i - images, 0), at) + (0,) * (len(shape) - 1))
+
+        both_passes = pl.BlockSpec((1, slots, width), lambda i: (i % images, 0, 0))
+        total_rows = width + SMALL_ROWS
+        vec = jnp.concatenate([row(v) for v in (attn_scale, first_gain, first_shift)])
+        tokens_grad, total, late = pl.pallas_call(
+            functools.partial(attention_backward, beyond=beyond),
+            grid=(2 * images,),
+            in_specs=[smem, smem, both_passes, both_passes]
+            + [first_pass(slots, 256)] * 2
+            + [first_pass(256, 256)] * 2
+            + [first_pass(4, slots, 256)]
+            + [second_pass(slots, width), second_pass(256, width), second_pass(256, width)]
+            + [second_pass(4, slots, 256, at=1), second_pass(4, slots, 256, at=2)]
+            + [vmem] * 3,
+            out_specs=[second_pass(slots, width), anyspace, vmem],
+            scratch_shapes=[
+                pltpu.VMEM((total_rows, width), F32),
+                pltpu.VMEM((total_rows, width), F32),
+                pltpu.VMEM((images, slots, width), BF16),
+                pltpu.VMEM((3, images, slots, 256), BF16),
+                pltpu.VMEM((slots, width), BF16),
+                pltpu.VMEM((slots, width), BF16),
+                pltpu.VMEM((slots, width), BF16),
+                pltpu.VMEM((len(GRIDS), 8, DIAG), F32),
+                pltpu.VMEM((9, 8, 256), F32),
+                pltpu.VMEM((2, 8, 256), F32),
+                pltpu.VMEM((16, width), F32),
+                pltpu.VMEM((SLICES - 1, 16, width), F32),
+                pltpu.VMEM((2 * max(beyond, 1), 16, width), F32),
+            ]
+            + Reduce.scratch(total_rows, width, beyond)
+            + [
+                pltpu.SemaphoreType.DMA((6 + beyond,)),
+                pltpu.SemaphoreType.DMA((6 + beyond,)),
+                pltpu.SemaphoreType.DMA((SLICES - 1 + beyond,)),
+                pltpu.SemaphoreType.DMA((SLICES - 1 + beyond,)),
+                pltpu.SemaphoreType.DMA((1,)),
+            ],
+            out_shape=[struct(images, slots, width), struct(total_rows, width), struct(16, width)],
+            compiler_params=remote_params(2),
+            name="attention_backward",
         )(
-            grid_shape, tokens, branch, cotangent, vec, small, up_weight, down_weight, gath_b, gath_c
+            sid, grid_shape, tokens, middle_grad, attended, queries, keys, values, probs, queries, keys, values, probs,
+            probs, vec, weights_a, sums,
         )
 
-        grad_b, grad_c = lax.psum((grad_b, grad_c), "wide")
-
-        vec = jnp.concatenate([row(v) for v in (attn_scale, first_gain, first_shift)])
-        tokens_grad, grad_a, more, diag_grad, cls_grad = pl.pallas_call(
-            attention_backward,
-            grid_spec=pltpu.PrefetchScalarGridSpec(
-                num_scalar_prefetch=2,
-                grid=(images,),
-                in_specs=[
-                    per_image(slots, width),
-                    per_image(slots, width),
-                    pl.BlockSpec((1, slots, 256), lambda i, *_: (i, 0, 0)),
-                    per_image(slots, width),
-                    per_image(256, width),
-                    per_image(256, width),
-                    per_image(all_heads, slots, 256),
-                    whole(3, width),
-                    whole(4, width, width),
-                ],
-                out_specs=[
-                    per_image(slots, width),
-                    whole(width, width),
-                    whole(4, 8, width),
-                    whole(len(GRIDS), 2, 3, 8, DIAG),
-                    whole(3, 3, 8, 256),
-                ],
-                scratch_shapes=[
-                    pltpu.VMEM((slots, width), BF16),
-                    pltpu.VMEM((slots, width), BF16),
-                    pltpu.VMEM((slots, width), BF16),
-                ],
-            ),
-            out_shape=[
-                struct(images, slots, width),
-                struct(width, width),
-                struct(4, 8, width),
-                struct(len(GRIDS), 2, 3, 8, DIAG),
-                struct(3, 3, 8, 256),
-            ],
-            compiler_params=params,
-            name="attention_backward",
-        )(sid, grid_shape, tokens, middle_grad, attended, queries, keys, values, probs, vec, weights_a)
-
-        diag_grad = jnp.pad(jnp.sum(diag_grad, axis=3), ((0, 0), (0, 0), (0, 8 - heads), (0, 0)))
+        grad_a = total[:width]
+        lines = total[width : width + 64, :DIAG].reshape(len(GRIDS), 8, DIAG)[:, : 2 * heads]
+        lines = jnp.pad(lines.reshape(len(GRIDS), 2, heads, DIAG), ((0, 0), (0, 0), (0, 8 - heads), (0, 0)))
         square_grad = pl.pallas_call(
             undiag_kernel, out_shape=struct(SPAN, 8, 128), name="undiag"
-        )(diag_grad)
+        )(lines)
         square_grad = jnp.transpose(square_grad[:, :heads, :SPAN], (1, 0, 2))[:, ::-1, ::-1]
-        table_grad = jnp.concatenate(
-            [square_grad.reshape(heads, SPAN * SPAN), jnp.sum(cls_grad, axis=(2, 3)).T], axis=1
-        )
-        sums = jnp.sum(sums, axis=1)
-        more = jnp.sum(more, axis=1)
-        grad_a, table_grad, sums, more = lax.psum((grad_a, table_grad, sums, more), "wide")
+        edges = jnp.sum(total[width + 64 : width + 73, :256], axis=1).reshape(3, heads).T
+        table_grad = jnp.concatenate([square_grad.reshape(heads, SPAN * SPAN), edges], axis=1)
+        more = total[width + 80 : width + 82, :local]
+        sums = total[width + 88 : width + 95]
+        late = jnp.sum(late.reshape(2, 8, width), axis=1)
         qkv_grad = jnp.transpose(grad_a[: 3 * local].reshape(3, local, width), (0, 2, 1))
         return (
             layer_out,
             tokens_grad,
+            late[0],
+            late[1],
+            qkv_grad,
             more[0],
             more[1],
-            qkv_grad,
-            more[2, :local],
-            more[3, :local],
             table_grad,
             grad_a[3 * local :],
             sums[5] * attn_scale.astype(F32),

time: 408 us -> 337 us (0.83)
  waiting for transfers between devices: 78.8 us -> 0 us
  Pallas kernels: 254 us -> 299 us
  blocking collectives: 24.5 us -> 0 us
  between operations: 14.3 us -> 1.06 us
    psum x1 -> x0, waiting for transfers between devices: 78.7 us -> none  [body(): lax.psum((grad_a, table_grad, sums, more), 'wide')]
    pallas_call x2, Pallas kernels: 115 us -> 161 us  [the longest x1 84.7 us: body(): pl.pallas_call(functools.partial(feed_forward, beyond=beyond), grid=(narr...]
    psum x1 -> x0, blocking collectives: 24.5 us -> none  [body(): lax.psum((grad_a, table_grad, sums, more), 'wide')]
    unnamed x25 -> x50, local copies, waits for them, and re-layouts: 6.36 us -> 11.5 us
    reshape x8, local copies, waits for them, and re-layouts: 6.05 us -> 1.77 us  [row(): return v.astype(F32).reshape(1, -1)]
  transfers between devices with their start and end apart: 1 -> 0, of which waited for: 1 -> 0; matrix products, arithmetic and copies ran while one was open for 1% -> 0% of each run, Pallas kernels for 1% -> 0%
where the time goes in v3:
time: 337 us; the launch traced here: 336 us
  Pallas kernels  299 us (89%)
  local copies, waits for them, and re-layouts  28.2 us (8%)
  other arithmetic  7.26 us (2%)
    pallas_call x1, Pallas kernels, body(): pl.pallas_call(functools.partial(attention_forward, narrow=narrow_size),...  136 us
    pallas_call x1, Pallas kernels, body(): pl.pallas_call(functools.partial(feed_forward, beyond=beyond), grid=(narr...  84.7 us
    pallas_call x1, Pallas kernels, body(): pl.pallas_call(functools.partial(attention_backward, beyond=beyond), grid...  76.1 us
    unnamed x50, local copies, waits for them, and re-layouts  11.5 us

profile of v3, /device:TPU:1, one launch (start us, length us, event | category | flops | bytes accessed | tf_op | source)
XLA Modules:
  0.0 335.8 jit_solution(12520163334380233475)
XLA Ops:
  0.8 1.4 pad_maximum_fusion.own_ref
  2.2 1.4 dynamic-slice_bitcast_fusion
  3.5 1.0 maximum_convert_fusion.slices
  5.0 0.6 pad_maximum_fusion.1.small_ref
  5.6 0.7 copy.54.grid_ref
  7.6 0.7 iota_reduce_fusion
  8.6 0.7 pad.43.table_ref
  9.9 136.1 %attention_forward.1 = (bf16[8,12,208,256]{3,2,1,0:T(8,128)(2,1)}, bf16[8,208,768]{2,1,0:T(8,128)(2,1)}, f32[8,208,768]{2,1,0:T(8,128)}, bf16[4,768,768]{2,1,0:T...) custom-call(s32[8]{0:T(128)} %get-tuple-element.37.sid_ref, ...), custom_call_target="tpu_custom_call" | custom-call | tf_op jit(solution)/shard_map/attention_forward/pallas_call | solution.py:786
  146.2 0.6 concatenate.29.vec_ref
  146.8 84.7 %feed_forward.1 = (bf16[8,208,768]{2,1,0:T(8,128)(2,1)}, f32[8,208,768]{2,1,0:T(8,128)}, f32[768,768]{1,0:T(8,128)}, f32[768,768]{1,0:T(8,128)}, f32[7,8,768]{2,1,0:T(8,128)}) custom-call(s32[8,2]{1,0:T(8,128)} %copy.54.grid_ref, bf16[8,208,768]{2,1,0:T(8,128)(2,1)} %tok_ref.5, f32[8,208,768]{2,1,0:T(8,128)} %get-tuple-element.38.branch_ref, ...), custom_call_target="tpu_custom_call" | custom-call | tf_op jit(solution)/shard_map/feed_forward/pallas_call | solution.py:843
  231.5 0.6 pad_maximum_fusion.3.vec_ref
  232.1 76.1 %attention_backward.1 = (f32[8,208,768]{2,1,0:T(8,128)}, f32[896,768]{1,0:T(8,128)}, f32[16,768]{1,0:T(8,128)}) custom-call(s32[8]{0:T(128)} %get-tuple-element.37.sid_ref, s32[8,2]{1,0:T(8,128)} %copy.54.grid_ref, bf16[8,208,768]{2,1,0:T(8,128)(2,1)} %tok_ref.5, f32[8,208,768]{2,1,0:T(8,128)} %get-tuple-element.43.mg_ref, ...), custom_call_target="tpu_custom_call" | custom-call | tf_op jit(solution)/shard_map/attention_backward/pallas_call | solution.py:887
  308.2 0.9 slice_bitcast_fusion
  309.3 0.7 pad.53.diag_ref
  310.0 2.4 undiag.1
  312.4 0.9 slice_bitcast_fusion.1
  313.7 1.0 slice_reduce_fusion
  314.8 0.7 pad_maximum_fusion.2
  315.5 2.8 slice.78
  318.3 1.9 slice.85
  320.2 1.7 slice_reduce_fusion.3
  321.9 0.6 convert_multiply_fusion
  322.5 0.6 convert_multiply_fusion.1
  323.1 0.6 slice_reduce_fusion.1
  323.7 1.3 fusion
  325.1 1.5 copy.65
  326.6 1.9 copy-done.1
  328.5 2.5 copy.66
  331.0 0.8 copy-done.4
  331.9 1.4 copy.67
  333.3 1.1 copy-done.3
  334.4 1.4 copy.68
  (75 shorter events, 3.3 us)
Async XLA Ops:
  0.7 3.9 %copy-start.20 = (bf16[192]{0:T(256)(128)(2,1)S(1)}, bf16[192]{0:T(256)(128)(2,1)}, u32[]{:S(2)}) copy-start(bf16[192]{0:T(256)(128)(2,1)} %param.25) | copy-start | bytes 1156
  0.7 3.9 %copy-start.21 = (bf16[192]{0:T(256)(128)(2,1)S(1)}, bf16[192]{0:T(256)(128)(2,1)}, u32[]{:S(2)}) copy-start(bf16[192]{0:T(256)(128)(2,1)} %param.26) | copy-start | bytes 1156
  0.7 4.0 %copy-start.5 = (bf16[3,2212]{1,0:T(4,128)(2,1)S(1)}, bf16[3,2212]{1,0:T(4,128)(2,1)}, u32[]{:S(2)}) copy-start(bf16[3,2212]{1,0:T(4,128)(2,1)} %param.27) | copy-start | bytes 39820
  0.7 4.1 %copy-start.12 = (bf16[768]{0:T(1024)(128)(2,1)S(1)}, bf16[768]{0:T(1024)(128)(2,1)}, u32[]{:S(2)}) copy-start(bf16[768]{0:T(1024)(128)(2,1)} %param.34) | copy-start | bytes 4612
  0.7 4.9 %copy-start.11 = (s32[8,2]{0,1:T(2,128)S(1)}, s32[8,2]{0,1:T(2,128)}, u32[]{:S(2)}) copy-start(s32[8,2]{0,1:T(2,128)} %param.21) | copy-start | bytes 196
  0.7 5.6 %copy-start.13 = (bf16[768]{0:T(1024)(128)(2,1)S(1)}, bf16[768]{0:T(1024)(128)(2,1)}, u32[]{:S(2)}) copy-start(bf16[768]{0:T(1024)(128)(2,1)} %param.22) | copy-start | bytes 4612
  0.7 6.2 %copy-start.14 = (bf16[768]{0:T(1024)(128)(2,1)S(1)}, bf16[768]{0:T(1024)(128)(2,1)}, u32[]{:S(2)}) copy-start(bf16[768]{0:T(1024)(128)(2,1)} %param.23) | copy-start | bytes 4612
  0.7 6.7 %copy-start.19 = (s32[8,2]{0,1:T(2,128)S(1)}, s32[8,2]{0,1:T(2,128)}, u32[]{:S(2)}) copy-start(s32[8,2]{0,1:T(2,128)} %constant.41.clone) | copy-start | bytes 196
  0.8 8.6 %copy-start.15 = (bf16[768]{0:T(1024)(128)(2,1)S(1)}, bf16[768]{0:T(1024)(128)(2,1)}, u32[]{:S(2)}) copy-start(bf16[768]{0:T(1024)(128)(2,1)} %param.29) | copy-start | bytes 4612
  2.1 7.8 %copy-start = (bf16[768,768]{1,0:T(8,128)(2,1)}, bf16[768,768]{1,0:T(8,128)(2,1)S(1)}, u32[]{:S(2)}) copy-start(bf16[768,768]{1,0:T(8,128)(2,1)S(1)} %pad_maximum_fusion.own_ref) | copy-start | bytes 3538948
  8.6 137.5 %copy-start.10 = (bf16[768]{0:T(1024)(128)(2,1)S(1)}, bf16[768]{0:T(1024)(128)(2,1)}, u32[]{:S(2)}) copy-start(bf16[768]{0:T(1024)(128)(2,1)} %param.30) | copy-start | bytes 4612
  8.6 137.5 %copy-start.9 = (bf16[768]{0:T(1024)(128)(2,1)S(1)}, bf16[768]{0:T(1024)(128)(2,1)}, u32[]{:S(2)}) copy-start(bf16[768]{0:T(1024)(128)(2,1)} %param.37) | copy-start | bytes 4612
  8.6 137.5 %copy-start.16 = (bf16[768]{0:T(1024)(128)(2,1)S(1)}, bf16[768]{0:T(1024)(128)(2,1)}, u32[]{:S(2)}) copy-start(bf16[768]{0:T(1024)(128)(2,1)} %param.31) | copy-start | bytes 4612
  8.6 137.5 %copy-start.17 = (bf16[768]{0:T(1024)(128)(2,1)S(1)}, bf16[768]{0:T(1024)(128)(2,1)}, u32[]{:S(2)}) copy-start(bf16[768]{0:T(1024)(128)(2,1)} %param.32) | copy-start | bytes 4612
  8.6 137.5 %copy-start.18 = (bf16[768]{0:T(1024)(128)(2,1)S(1)}, bf16[768]{0:T(1024)(128)(2,1)}, u32[]{:S(2)}) copy-start(bf16[768]{0:T(1024)(128)(2,1)} %param.36) | copy-start | bytes 4612
  146.8 84.7 %copy-start.7 = (f32[1,768]{1,0:T(1,128)S(1)}, f32[1,768]{1,0:T(1,128)}, u32[]{:S(2)}) copy-start(f32[1,768]{1,0:T(1,128)} %reshape.164.gain_ref) | copy-start | bytes 9220
  146.8 84.7 %copy-start.8 = (f32[1,768]{1,0:T(1,128)S(1)}, f32[1,768]{1,0:T(1,128)}, u32[]{:S(2)}) copy-start(f32[1,768]{1,0:T(1,128)} %reshape.166.shift_ref) | copy-start | bytes 9220
  313.5 9.6 %copy-start.6 = (f32[16,768]{1,0:T(8,128)S(1)}, f32[16,768]{1,0:T(8,128)}, u32[]{:S(2)}) copy-start(f32[16,768]{1,0:T(8,128)} %get-tuple-element.52) | copy-start | bytes 147460
  313.5 11.6 %copy-start.2 = (bf16[8,208,768]{2,1,0:T(8,128)(2,1)S(1)}, bf16[8,208,768]{2,1,0:T(8,128)(2,1)}, u32[]{:S(2)}) copy-start(bf16[8,208,768]{2,1,0:T(8,128)(2,1)} %get-tuple-element.99) | copy-start | bytes 7667716
  325.1 3.4 %copy-start.1 = (f32[8,208,768]{2,1,0:T(8,128)S(1)}, f32[8,208,768]{2,1,0:T(8,128)}, u32[]{:S(2)}) copy-start(f32[8,208,768]{2,1,0:T(8,128)} %get-tuple-element.100) | copy-start | bytes 15335428
  328.5 3.4 %copy-start.4 = (f32[768,768]{1,0:T(8,128)S(1)}, f32[768,768]{1,0:T(8,128)}, u32[]{:S(2)}) copy-start(f32[768,768]{1,0:T(8,128)} %get-tuple-element.112) | copy-start | bytes 7077892
  331.8 2.5 copy-start.3

commit v4 on v3

--- a/solution.py
+++ b/solution.py
@@ -92,7 +92,15 @@
 SLICES = 8
 SLICE_ROWS = 96
 PART_ROWS = 24
-CHUNKS = tuple((group, at, 24) for group in range(3) for at in (0, 24, 48, 72))
+
+
+def chunks_of(narrow):
+    all_shards = tuple(range(1, narrow))
+    rows = [(group, at, 24, all_shards) for group in range(2) for at in (0, 24, 48, 72)]
+    return tuple(rows) + tuple((2, 0, SLICE_ROWS, (k,)) for k in all_shards)
+
+
+ROW_CHUNKS = 8
 
 
 class Neighbours:
@@ -116,18 +124,23 @@
 
 
 class Gather(Neighbours):
-    def __init__(self, narrow, slices, buffers, send, recv):
+    def __init__(self, narrow, slices, buffers, send, recv, done=()):
         super().__init__()
+        self.done = done
         self.narrow, self.slices, self.buffers, self.send, self.recv = narrow, slices, buffers, send, recv
         self.z = lax.axis_index("narrow")
+        self.chunks = chunks_of(narrow)
         self.per_chunk = narrow - 1 + 7
+        self.started = []
 
     def copy(self, chunk, phase, piece):
-        group, at, rows = CHUNKS[chunk]
+        group, at, rows, shards = self.chunks[chunk]
         buffer = self.buffers[group]
 
         def part(owner):
-            return buffer.at[:, pl.ds(pl.multiple_of(owner * SLICE_ROWS + at, 8), rows), :]
+            return buffer.at[
+                pl.ds(shards[0] - 1, len(shards)), pl.ds(pl.multiple_of(owner * SLICE_ROWS + at, 8), rows), :
+            ]
 
         place = chunk * self.per_chunk
         if phase == 0:
@@ -145,28 +158,28 @@
             device_id=device, device_id_type=MESH,
         )
 
-    def pieces(self, phase):
-        return (range(1, self.narrow), range(1), range(2), range(4))[phase]
+    def pieces(self, chunk, phase):
+        return (self.chunks[chunk][3], range(1), range(2), range(4))[phase]
 
     def start(self, chunk, phase):
-        for piece in self.pieces(phase):
+        self.started.append((chunk, phase))
+        for piece in self.pieces(chunk, phase):
             self.copy(chunk, phase, piece).start()
 
     def arrive(self, chunk, phase):
-        for piece in self.pieces(phase):
+        for piece in self.pieces(chunk, phase):
             self.copy(chunk, phase, piece).wait_recv()
 
     def run(self, steps):
         for chunk, phase in steps:
-            if phase > 0:
+            if phase > 0 and (chunk, phase - 1) not in self.done:
                 self.arrive(chunk, phase - 1)
             self.start(chunk, phase)
 
     def drain(self):
-        for chunk in range(len(CHUNKS)):
-            for phase in range(4):
-                for piece in self.pieces(phase):
-                    self.copy(chunk, phase, piece).wait_send()
+        for chunk, phase in self.started:
+            for piece in self.pieces(chunk, phase):
+                self.copy(chunk, phase, piece).wait_send()
 
     def barrier(self):
         sem = pltpu.get_barrier_semaphore()
@@ -181,11 +194,11 @@
 
 def tick(t):
     steps = ((t, 1), (t + 2, 0), (t - 1, 2), (t - 2, 3))
-    return tuple((chunk, phase) for chunk, phase in steps if 0 <= chunk < len(CHUNKS))
-
-
-LATE = {3: 7, 11: 8, 20: 9}
-LAST = range(10, len(CHUNKS) + 2)
+    return tuple((chunk, phase) for chunk, phase in steps if 0 <= chunk < ROW_CHUNKS + 3 * (phase == 0))
+
+
+LATE = {4: 7, 14: 8, 23: 9}
+LAST = ()
 
 
 def attention_forward(
@@ -262,10 +275,10 @@
                 diag[h * 16 + r : h * 16 + r + 1, :] = lined[r, h : h + 1, :]
         gather.barrier()
         smalls[0] = small_ref[0]
+        gather.run(((0, 0), (1, 0)))
         for k in range(1, narrow):
             extra(0, k).start()
             extra(1, k).start()
-        gather.run(((0, 0), (1, 0)))
         k_pad[:, 208:256, :] = jnp.zeros((8, 48, 768), BF16)
         v_pad[:, 208:256, :] = jnp.zeros((8, 48, 768), BF16)
         for part in range(4):
@@ -278,14 +291,14 @@
             bias_of(0, at, lambda row: diag[pl.ds(row, 1), :])
 
         gather.run(tick(0))
+        gather.run(tick(1))
         for k in range(1, narrow):
             extra(0, k).wait_recv()
             extra(1, k).wait_recv()
         far_bias(1)
-        gather.run(tick(1))
-        far_bias(2)
         gather.run(tick(2))
-        far_bias(3)
+        for k in range(2, narrow):
+            far_bias(k)
         gather.run(tick(3))
         q_bias = sum(smalls[k, 0:1, :] for k in range(narrow))
         v_bias = sum(smalls[k, 1:2, :] for k in range(narrow))
@@ -339,8 +352,10 @@
     def _():
         for t in LAST:
             gather.run(tick(t))
-        for chunk in range(4, len(CHUNKS)):
+        for chunk in range(4, ROW_CHUNKS):
             gather.arrive(chunk, 3)
+        for chunk in range(ROW_CHUNKS, len(gather.chunks)):
+            gather.arrive(chunk, 0)
         gather.drain()
         for k in range(1, narrow):
             extra(0, k).wait_send()
@@ -422,60 +437,65 @@
             self.copy(step).wait_send()
 
 
-def greet(near, beyond):
+def greet(near, beyond, narrow=1):
     sem = pltpu.get_barrier_semaphore()
+    for k in range(1, narrow):
+        pl.semaphore_signal(sem, inc=1, device_id={"narrow": (near.z + k) % narrow}, device_id_type=MESH)
     for k in range(1, SLICES):
         other = near.base + (near.me + k) % SLICES
         pl.semaphore_signal(sem, inc=1, device_id={"wide": other}, device_id_type=MESH)
     for i in range(beyond):
         pl.semaphore_signal(sem, inc=1, device_id={"wide": near.beyond(i)}, device_id_type=MESH)
-    pl.semaphore_wait(sem, SLICES - 1 + beyond)
+    pl.semaphore_wait(sem, narrow - 1 + SLICES - 1 + beyond)
 
 
 PAIR = 2
-FF_TICKS = {
-    4: ((0, 0), (1, 0)), 5: ((0, 1), (1, 1)), 7: ((0, 2),), 9: ((1, 2), (0, 3)), 10: ((0, 4), (1, 3)), 12: ((0, 5), (1, 4)),
-    14: ((1, 5),), 15: ((0, 6),),
-}
+FF_GATHER = {0: ((8, 1),), 1: ((8, 2), (9, 1)), 3: ((8, 3), (9, 2), (10, 1)), 5: ((9, 3), (10, 2)), 8: ((10, 3),)}
+
+FF_SUM = {4: 0, 7: 1, 10: 2, 11: 3, 13: 4, 15: 5}
 
 
 def feed_forward(
-    grid_ref, tok_ref, branch_ref, cot_ref, vec_ref, small_ref, ownb_ref, ownc_ref, gath_b, gath_c,
-    out_ref, mg_ref, out_b, out_c, sums_ref,
-    total_b, total_c, stage, wb, wc, second_ins, branch_lows, mlp_acc, second_acc, grad_b, grad_c, *rest, beyond,
+    grid_ref, tok_ref, branch_ref, cot_ref, vec_ref, small_ref, ownb_ref, ownc_ref, slices, gath_b, _,
+    out_ref, mg_ref, out_b, grad_c, sums_ref, gath_c,
+    total_b, stage, wb, wc, second_ins, branch_lows, mlp_acc, second_acc, grad_b, half, quarter, eighth, between,
+    loads, send, recv, gather_send, gather_recv, narrow, beyond,
 ):
-    loads, send, recv = rest[8:]
     slot, pair = pl.program_id(0), pl.program_id(1)
     slots, pairs = pl.num_programs(0), pl.num_programs(1)
     rows = PAIR * 208
-    near = Neighbours()
-    sums = [
-        Reduce(near, beyond, grad, *rest[4 * i : 4 * i + 4], total, send, recv, i * (6 + beyond))
-        for i, (grad, total) in enumerate(((grad_b, total_b), (grad_c, total_c)))
-    ]
+    gather = Gather(narrow, slices, (None, None, gath_c), gather_send, gather_recv, done=tuple((ROW_CHUNKS + k, 0) for k in range(3)))
+    reduction = Reduce(gather, beyond, grad_b, half, quarter, eighth, between, total_b, send, recv, 0)
 
     def load(which, at):
         return pltpu.make_async_copy((gath_b, gath_c)[which].at[at], stage.at[which], loads.at[which])
 
     @pl.when((slot == 0) & (pair == 0))
     def _():
-        greet(near, beyond)
+        greet(gather, beyond, narrow)
         wb[0] = ownb_ref[...]
         wc[0] = ownc_ref[...]
         grad_b[...] = jnp.zeros_like(grad_b)
         grad_c[...] = jnp.zeros_like(grad_c)
         sums_ref[...] = jnp.zeros_like(sums_ref)
 
-    @pl.when((pair == 0) & (slot < slots - 1))
-    def _():
-        load(0, slot).start()
-        load(1, slot).start()
-
-    for when, steps in FF_TICKS.items():
+    for when, steps in FF_GATHER.items():
         @pl.when(slot * pairs + pair == when)
         def _():
-            for chain, step in steps:
-                sums[chain].run(step)
+            gather.run(steps)
+
+    for when, step in FF_SUM.items():
+        @pl.when(slot * pairs + pair == when)
+        def _():
+            reduction.run(step)
+
+    for k in range(1, narrow):
+        @pl.when((pair == pairs - 1) & (slot == k - 1))
+        def _():
+            load(0, k - 1).start()
+            if k > 1:
+                gather.arrive(ROW_CHUNKS + k - 1, 3)
+                load(1, k - 1).start()
 
     attn_scale, second_gain, second_shift, mlp_scale, down_bias = (vec_ref[i : i + 1, :] for i in range(5))
 
@@ -516,6 +536,11 @@
         grad_c[...] += dot_tn(hidden, branch_low)
         grad_b[...] += dot_tn(second_in, pre_low)
         sums_ref[6] += fold_rows(pre_low.astype(F32))
+
+    @pl.when((pair == pairs - 1) & (slot == 0))
+    def _():
+        gather.arrive(ROW_CHUNKS, 3)
+        load(1, 0).start()
 
     @pl.when((pair == pairs - 1) & (slot < slots - 1))
     def _():
@@ -542,37 +567,46 @@
 
     @pl.when((slot == slots - 1) & (pair == pairs - 1))
     def _():
-        sums[1].run(6)
-        copies = [
-            pltpu.make_async_copy(chain.total, out, loads.at[i])
-            for i, (chain, out) in enumerate(zip(sums, (out_b, out_c)))
-        ]
-        for copy in copies:
-            copy.start()
-        for copy in copies:
-            copy.wait()
-        for chain in sums:
-            chain.drain()
+        reduction.run(6)
+        copy = pltpu.make_async_copy(total_b, out_b, loads.at[0])
+        copy.start()
+        copy.wait()
+        reduction.drain()
+        gather.drain()
 
 
 SMALL_ROWS = 128
-AB_TICKS = {8: (0,), 10: (1,), 13: (2,), 15: (3,)}
-AB_LAST = (4, 5, 6)
+AB_TICKS = {0: ((0, 0),), 2: ((0, 1),), 5: ((0, 2),), 7: ((0, 3),), 8: ((1, 0),), 9: ((1, 1),), 12: ((1, 2),), 14: ((1, 3),), 15: ((0, 4),)}
+
+AB_LAST = ((1, 4), (0, 5), (1, 5), (0, 6), (1, 6))
 
 
 def attention_backward(
     sid_ref, grid_ref, tok_ref, mg_ref, att_ref, q0_ref, k0_ref, v0_ref, p0_ref, q_ref, k_ref, v_ref, p1_ref, p2_ref,
-    vec_ref, wa_ref, ff_sums_ref,
-    tg_ref, total_out, late_total,
-    total, grads, attn_lows, kept, dq, dk, dv, lines, edges, sums, late, late_in, late_between,
-    half, quarter, eighth, between, send, recv, late_send, late_recv, local, beyond,
+    vec_ref, wa_ref, ff_sums_ref, grad_c,
+    tg_ref, total_out, out_c, late_total,
+    total, total_c, grads, attn_lows, kept, dq, dk, dv, lines, edges, sums, late, late_in, late_between,
+    *rest, beyond,
 ):
     step = pl.program_id(0)
-    images = pl.num_programs(0) // 2
+    half = pl.num_programs(0) // 2
+    rows = PAIR * 208
     near = Neighbours()
-    reduction = Reduce(near, beyond, grads, half, quarter, eighth, between, total, send, recv, 0)
+    send, recv, late_send, late_recv, local = rest[8:]
+    chains = (
+        Reduce(near, beyond, grad_c, *rest[0:4], total_c, send, recv, 0),
+        Reduce(near, beyond, grads, *rest[4:8], total, send, recv, 6 + beyond),
+    )
     attn_scale, first_gain, first_shift = (vec_ref[i : i + 1, :] for i in range(3))
     head_of = lax.broadcasted_iota(jnp.int32, (1, 256), 1) // HD
+
+    def advance(i):
+        for when, steps in AB_TICKS.items():
+            if when % PAIR == i:
+                @pl.when(step == when // PAIR)
+                def _():
+                    for chain, at in steps:
+                        chains[chain].run(at)
 
     def stack(group):
         return jnp.concatenate([jnp.where(head_of == h, group, jnp.zeros_like(group)) for h in range(4)], axis=0)
@@ -611,48 +645,58 @@
         edges[...] = jnp.zeros_like(edges)
         late[...] = jnp.zeros_like(late)
 
-    normed, inv = norm_stats(tok_ref[0].astype(F32))
-
-    @pl.when(step < images)
-    def _():
-        attn_low = (mg_ref[0] * attn_scale).astype(BF16)
+    normed, inv = norm_stats(tok_ref[...].reshape(rows, 768).astype(F32))
+    middle_grad = mg_ref[...].reshape(rows, 768)
+
+    @pl.when(step < half)
+    def _():
+        attn_low = (middle_grad * attn_scale).astype(BF16)
         attn_lows[step] = attn_low
-        g_group = dot_nt(attn_low, wa_ref[3, 0:256, :]).astype(BF16)
-        grads[576:768, :] += dot_tn(att_ref[0], attn_low)[0:192, :]
-        p, s, limit, later, p_patch, s_patch = slot_masks(grid_ref[step, 0], grid_ref[step, 1], True)
-        both = p_patch & s_patch
+        attended_grad = dot_nt(attn_low, wa_ref[3, 0:256, :]).astype(BF16)
+        grads[576:768, :] += dot_tn(att_ref[...].reshape(rows, 256), attn_low)[0:192, :]
         flip = (
             lax.broadcasted_iota(jnp.int32, (208, 208), 0) + lax.broadcasted_iota(jnp.int32, (208, 208), 1) == 207
         ).astype(BF16)
-        kind = sid_ref[step]
-
-        def table_grad(h, score_grad, low):
-            if h == 3:
-                return
-            rest = (score_grad - low.astype(F32)).astype(BF16)
-            turned = dot_nn(flip, low) + dot_nn(flip, rest)
-            patches = jnp.where(both, turned, 0.0)
-            edge = turned - patches
-            for which, part in enumerate((jnp.where(later, patches, 0.0), jnp.where(later, 0.0, patches))):
-                wide = jnp.concatenate([part, jnp.zeros((208, 256), F32)], axis=1)
-                folded = jnp.sum(pltpu.roll(wide, 0, 1, stride=1, stride_axis=0), axis=0, keepdims=True)
-                row = which * 3 + h
-                for shape_at in range(len(GRIDS)):
-                    lines[shape_at, row : row + 1, :] += jnp.where(kind == shape_at, folded, 0.0)
-            class_query = jnp.where((p == 0) & s_patch, edge, 0.0)
-            class_key = jnp.where(p_patch & (s == 0), edge, 0.0)
-            for at, part in enumerate((class_query, class_key, edge - class_query - class_key)):
-                edges[at * 3 + h] += fold_rows(part)
-
-        own = heads_back(q0_ref[0], k0_ref[0], v0_ref[0], g_group, lambda h: p0_ref[0, h], table_grad)
+
+        for i in range(PAIR):
+            advance(i)
+            image = step * PAIR + i
+            p, s, limit, later, p_patch, s_patch = slot_masks(grid_ref[image, 0], grid_ref[image, 1], True)
+            both = p_patch & s_patch
+            kind = sid_ref[image]
+
+            def table_grad(h, score_grad, low):
+                if h == 3:
+                    return
+                low_rest = (score_grad - low.astype(F32)).astype(BF16)
+                turned = dot_nn(flip, low) + dot_nn(flip, low_rest)
+                patches = jnp.where(both, turned, 0.0)
+                edge = turned - patches
+                for which, part in enumerate((jnp.where(later, patches, 0.0), jnp.where(later, 0.0, patches))):
+                    wide = jnp.concatenate([part, jnp.zeros((208, 256), F32)], axis=1)
+                    folded = jnp.sum(pltpu.roll(wide, 0, 1, stride=1, stride_axis=0), axis=0, keepdims=True)
+                    row = which * 3 + h
+                    for shape_at in range(len(GRIDS)):
+                        lines[shape_at, row : row + 1, :] += jnp.where(kind == shape_at, folded, 0.0)
+                class_query = jnp.where((p == 0) & s_patch, edge, 0.0)
+                class_key = jnp.where(p_patch & (s == 0), edge, 0.0)
+                for at, part in enumerate((class_query, class_key, edge - class_query - class_key)):
+                    edges[at * 3 + h] += fold_rows(part)
+
+            here = slice(i * 208, (i + 1) * 208)
+            own = heads_back(
+                q0_ref[i], k0_ref[i], v0_ref[i], attended_grad[here], lambda h: p0_ref[i, h], table_grad
+            )
+            for c, grad in enumerate(own):
+                kept[c, step, here, :] = grad
+            sums[0] += fold_rows(own[0].astype(F32))
+            sums[1] += fold_rows(own[2].astype(F32))
+
         first_in = (normed * first_gain + first_shift).astype(BF16)
-        for c, grad in enumerate(own):
-            kept[c, step] = grad
-            grads[c * 192 : (c + 1) * 192, :] += dot_tn(grad, first_in)[0:192, :]
-        sums[0] += fold_rows(own[0].astype(F32))
-        sums[1] += fold_rows(own[2].astype(F32))
-
-    @pl.when(step == images)
+        for c in range(3):
+            grads[c * 192 : (c + 1) * 192, :] += dot_tn(kept[c, step], first_in)[0:192, :]
+
+    @pl.when(step == half)
     def _():
         grads[768 : 768 + SMALL_ROWS, :] = jnp.zeros((SMALL_ROWS, 768), F32)
         for shape_at in range(len(GRIDS)):
@@ -664,34 +708,30 @@
         for at in range(7):
             grads[856 + at : 857 + at, :] = jnp.sum(ff_sums_ref[at], axis=0, keepdims=True)
 
-    for when, steps in AB_TICKS.items():
-        @pl.when(step == when)
-        def _():
-            for at in steps:
-                reduction.run(at)
-
-    @pl.when(step >= images)
-    def _():
-        image = step - images
-        attn_low = attn_lows[image]
+    @pl.when(step >= half)
+    def _():
+        at = step - half
+        attended_grad = dot_nt(attn_lows[at], wa_ref[3, 256:768, :]).astype(BF16)
         for c, ref in enumerate((dq, dk, dv)):
-            ref[:, 0:256] = kept[c, image]
-        for group in (1, 2):
-            lanes = slice(group * 256, group * 256 + 256)
-            g_group = dot_nt(attn_low, wa_ref[3, lanes, :]).astype(BF16)
-            probs = (p1_ref, p2_ref)[group - 1]
-            parts = heads_back(
-                q_ref[0, :, lanes], k_ref[0, :, lanes], v_ref[0, :, lanes], g_group,
-                lambda h: probs[0, h], lambda *_: None,
-            )
-            for ref, part in zip((dq, dk, dv), parts):
-                ref[:, lanes] = part
+            ref[:, 0:256] = kept[c, at]
+        for i in range(PAIR):
+            advance(i)
+            here = slice(i * 208, (i + 1) * 208)
+            for group in (1, 2):
+                lanes = slice(group * 256, group * 256 + 256)
+                probs = (p1_ref, p2_ref)[group - 1]
+                parts = heads_back(
+                    q_ref[i, :, lanes], k_ref[i, :, lanes], v_ref[i, :, lanes],
+                    attended_grad[here, (group - 1) * 256 : group * 256], lambda h: probs[i, h], lambda *_: None,
+                )
+                for ref, part in zip((dq, dk, dv), parts):
+                    ref[here, lanes] = part
         first_grad = dot_nn(dq[...], wa_ref[0]) + dot_nn(dk[...], wa_ref[1]) + dot_nn(dv[...], wa_ref[2])
-        tg_ref[0] = mg_ref[0] + norm_back(first_grad, normed, inv, first_gain)
+        tg_ref[...] = (middle_grad + norm_back(first_grad, normed, inv, first_gain)).reshape(PAIR, 208, 768)
         late[0:8, :] += fold_rows(first_grad * normed)
         late[8:16, :] += fold_rows(first_grad)
 
-    @pl.when(step == 2 * images - 1)
+    @pl.when(step == 2 * half - 1)
     def _():
         copies = [
             pltpu.make_async_remote_copy(
@@ -702,8 +742,14 @@
         ]
         for copy in copies:
             copy.start()
-        for at in AB_LAST:
-            reduction.run(at)
+        outs = [
+            pltpu.make_async_copy(source, target, local.at[i])
+            for i, (source, target) in enumerate(((total_c, out_c), (total, total_out)))
+        ]
+        for chain, at in AB_LAST:
+            chains[chain].run(at)
+        for copy in outs:
+            copy.start()
         for copy in copies:
             copy.wait()
         summed = late[...]
@@ -720,10 +766,10 @@
             copy.wait()
             summed = late_between[2 * i] + late_between[2 * i + 1]
         late_total[...] = summed
-        copy = pltpu.make_async_copy(total, total_out, local.at[0])
-        copy.start()
-        copy.wait()
-        reduction.drain()
+        for copy in outs:
+            copy.wait()
+        for chain in chains:
+            chain.drain()
 
 
 def make_body(wide_size, narrow_size):
@@ -776,8 +822,8 @@
             return jax.ShapeDtypeStruct(shape, dtype)
 
         params = pltpu.CompilerParams(vmem_limit_bytes=VMEM_LIMIT, dimension_semantics=("arbitrary",))
-        copies = len(CHUNKS) * (narrow_size - 1 + 7)
-        copies = len(CHUNKS) * (narrow_size - 1 + 7)
+        copies = len(chunks_of(narrow_size)) * (narrow_size - 1 + 7)
+        copies = len(chunks_of(narrow_size)) * (narrow_size - 1 + 7)
         me = lax.axis_index("wide") % SLICES
         slices = jnp.stack(
             [lax.dynamic_slice_in_dim(own_a.reshape(4, local, width), me * PART_ROWS, PART_ROWS, 1).reshape(-1, width)]
@@ -840,13 +886,13 @@
 
         ends = pl.BlockSpec((PAIR, slots, width), lambda s, i: (jnp.where((s > 0) & (s < last), pairs - 1, i), 0, 0))
         outs = pl.BlockSpec((PAIR, slots, width), lambda s, i: (jnp.where(s < last, 0, i), 0, 0))
-        layer_out, middle_grad, grad_b, grad_c, sums = pl.pallas_call(
-            functools.partial(feed_forward, beyond=beyond),
+        layer_out, middle_grad, grad_b, grad_c, sums, _ = pl.pallas_call(
+            functools.partial(feed_forward, narrow=narrow_size, beyond=beyond),
             grid=(narrow_size, pairs),
-            in_specs=[smem] + [ends] * 3 + [vmem] * 4 + [anyspace] * 2,
-            out_specs=[outs] * 2 + [anyspace] * 2 + [vmem],
+            in_specs=[smem] + [ends] * 3 + [vmem] * 5 + [anyspace] * 2,
+            out_specs=[outs] * 2 + [anyspace, vmem, vmem, anyspace],
+            input_output_aliases={10: 5},
             scratch_shapes=[
-                pltpu.VMEM((width, width), F32),
                 pltpu.VMEM((width, width), F32),
                 pltpu.VMEM((2, width, width), F32),
                 pltpu.VMEM((2, width, width), BF16),
@@ -856,13 +902,14 @@
                 pltpu.VMEM((pairs, rows, width), F32),
                 pltpu.VMEM((pairs, rows, width), F32),
                 pltpu.VMEM((width, width), F32),
-                pltpu.VMEM((width, width), F32),
             ]
-            + Reduce.scratch(width, width, beyond) * 2
+            + Reduce.scratch(width, width, beyond)
             + [
                 pltpu.SemaphoreType.DMA((2,)),
-                pltpu.SemaphoreType.DMA((2 * (6 + beyond),)),
-                pltpu.SemaphoreType.DMA((2 * (6 + beyond),)),
+                pltpu.SemaphoreType.DMA((6 + beyond,)),
+                pltpu.SemaphoreType.DMA((6 + beyond,)),
+                pltpu.SemaphoreType.DMA((copies,)),
+                pltpu.SemaphoreType.DMA((copies,)),
             ],
             out_shape=[
                 struct(images, slots, width, dtype=BF16),
@@ -870,39 +917,41 @@
                 struct(width, width),
                 struct(width, width),
                 struct(7, 8, width),
+                struct(narrow_size - 1, width, width),
             ],
             compiler_params=remote_params(1),
             name="feed_forward",
-        )(grid_shape, tokens, branch, cotangent, vec, small, up_weight, down_weight, gath_b, gath_c)
+        )(grid_shape, tokens, branch, cotangent, vec, small, up_weight, down_weight, slices, gath_b, gath_c)
 
         def first_pass(*shape):
-            return pl.BlockSpec((1,) + shape, lambda i: (jnp.minimum(i, images - 1),) + (0,) * len(shape))
+            return pl.BlockSpec((PAIR,) + shape, lambda i: (jnp.minimum(i, pairs - 1),) + (0,) * len(shape))
 
         def second_pass(*shape, at=0):
-            return pl.BlockSpec((1,) + shape, lambda i: (jnp.maximum(i - images, 0), at) + (0,) * (len(shape) - 1))
-
-        both_passes = pl.BlockSpec((1, slots, width), lambda i: (i % images, 0, 0))
+            return pl.BlockSpec((PAIR,) + shape, lambda i: (jnp.maximum(i - pairs, 0), at) + (0,) * (len(shape) - 1))
+
+        both_passes = pl.BlockSpec((PAIR, slots, width), lambda i: (i % pairs, 0, 0))
         total_rows = width + SMALL_ROWS
         vec = jnp.concatenate([row(v) for v in (attn_scale, first_gain, first_shift)])
-        tokens_grad, total, late = pl.pallas_call(
+        tokens_grad, total, grad_c, late = pl.pallas_call(
             functools.partial(attention_backward, beyond=beyond),
-            grid=(2 * images,),
+            grid=(2 * pairs,),
             in_specs=[smem, smem, both_passes, both_passes]
             + [first_pass(slots, 256)] * 2
             + [first_pass(256, 256)] * 2
             + [first_pass(4, slots, 256)]
             + [second_pass(slots, width), second_pass(256, width), second_pass(256, width)]
             + [second_pass(4, slots, 256, at=1), second_pass(4, slots, 256, at=2)]
-            + [vmem] * 3,
-            out_specs=[second_pass(slots, width), anyspace, vmem],
+            + [vmem] * 4,
+            out_specs=[second_pass(slots, width), anyspace, anyspace, vmem],
             scratch_shapes=[
                 pltpu.VMEM((total_rows, width), F32),
+                pltpu.VMEM((width, width), F32),
                 pltpu.VMEM((total_rows, width), F32),
-                pltpu.VMEM((images, slots, width), BF16),
-                pltpu.VMEM((3, images, slots, 256), BF16),
-                pltpu.VMEM((slots, width), BF16),
-                pltpu.VMEM((slots, width), BF16),
-                pltpu.VMEM((slots, width), BF16),
+                pltpu.VMEM((pairs, rows, width), BF16),
+                pltpu.VMEM((3, pairs, rows, 256), BF16),
+                pltpu.VMEM((rows, width), BF16),
+                pltpu.VMEM((rows, width), BF16),
+                pltpu.VMEM((rows, width), BF16),
                 pltpu.VMEM((len(GRIDS), 8, DIAG), F32),
                 pltpu.VMEM((9, 8, 256), F32),
                 pltpu.VMEM((2, 8, 256), F32),
@@ -910,20 +959,23 @@
                 pltpu.VMEM((SLICES - 1, 16, width), F32),
                 pltpu.VMEM((2 * max(beyond, 1), 16, width), F32),
             ]
+            + Reduce.scratch(width, width, beyond)
             + Reduce.scratch(total_rows, width, beyond)
             + [
-                pltpu.SemaphoreType.DMA((6 + beyond,)),
-                pltpu.SemaphoreType.DMA((6 + beyond,)),
+                pltpu.SemaphoreType.DMA((2 * (6 + beyond),)),
+                pltpu.SemaphoreType.DMA((2 * (6 + beyond),)),
                 pltpu.SemaphoreType.DMA((SLICES - 1 + beyond,)),
                 pltpu.SemaphoreType.DMA((SLICES - 1 + beyond,)),
-                pltpu.SemaphoreType.DMA((1,)),
+                pltpu.SemaphoreType.DMA((2,)),
             ],
-            out_shape=[struct(images, slots, width), struct(total_rows, width), struct(16, width)],
+            out_shape=[
+                struct(images, slots, width), struct(total_rows, width), struct(width, width), struct(16, width),
+            ],
             compiler_params=remote_params(2),
             name="attention_backward",
         )(
             sid, grid_shape, tokens, middle_grad, attended, queries, keys, values, probs, queries, keys, values, probs,
-            probs, vec, weights_a, sums,
+            probs, vec, weights_a, sums, grad_c,
         )
 
         grad_a = total[:width]

time: 337 us -> 315 us (0.935)
  Pallas kernels: 299 us -> 278 us
    pallas_call x1, Pallas kernels: 136 us -> 110 us  [body(): pl.pallas_call(functools.partial(attention_forward, narrow=narrow_size),...]
    pallas_call x1, Pallas kernels: 76.1 us -> 84.8 us  [body(): pl.pallas_call(functools.partial(attention_backward, beyond=beyond), grid...]
    pallas_call x1, Pallas kernels: 84.7 us -> 81 us  [body(): pl.pallas_call(functools.partial(feed_forward, narrow=narrow_size, beyond...]
where the time goes in v4:
time: 315 us; the launch traced here: 314 us
  Pallas kernels  278 us (88%)
  local copies, waits for them, and re-layouts  28.2 us (9%)
  other arithmetic  7.26 us (2%)
    pallas_call x1, Pallas kernels, body(): pl.pallas_call(functools.partial(attention_forward, narrow=narrow_size),...  110 us
    pallas_call x1, Pallas kernels, body(): pl.pallas_call(functools.partial(attention_backward, beyond=beyond), grid...  84.8 us
    pallas_call x1, Pallas kernels, body(): pl.pallas_call(functools.partial(feed_forward, narrow=narrow_size, beyond...  81 us
    unnamed x50, local copies, waits for them, and re-layouts  11.5 us

profile of v4, /device:TPU:1, one launch (start us, length us, event | category | flops | bytes accessed | tf_op | source)
XLA Modules:
  0.0 314.4 jit_solution(15104265620789579650)
XLA Ops:
  0.8 1.4 pad_maximum_fusion.own_ref
  2.2 1.4 dynamic-slice_bitcast_fusion
  3.5 1.0 maximum_convert_fusion.slices
  5.0 0.6 pad_maximum_fusion.1.small_ref
  5.6 0.7 copy.55.grid_ref
  7.6 0.7 iota_reduce_fusion
  8.6 0.7 pad.43.table_ref
  9.9 109.7 %attention_forward.1 = (bf16[8,12,208,256]{3,2,1,0:T(8,128)(2,1)}, bf16[8,208,768]{2,1,0:T(8,128)(2,1)}, f32[8,208,768]{2,1,0:T(8,128)}, bf16[4,768,768]{2,1,0:T...) custom-call(s32[8]{0:T(128)} %get-tuple-element.38.sid_ref, ...), custom_call_target="tpu_custom_call" | custom-call | tf_op jit(solution)/shard_map/attention_forward/pallas_call | solution.py:832
  119.8 0.6 concatenate.29.vec_ref
  120.4 81.0 %feed_forward.1 = (bf16[8,208,768]{2,1,0:T(8,128)(2,1)}, f32[8,208,768]{2,1,0:T(8,128)}, f32[768,768]{1,0:T(8,128)}, f32[768,768]{1,0:T(8,128)}, f32[7,8,768]{2,1,0:T(8,128)}, /*index=5*/f32[3,768,768]{2,1,0:T(8,128)}) custom-call(s32[8,2]{1,0:T(8,128)} %copy.55.grid_ref, bf16[8,208,768]{2,1,0:T(8,128)(2,1)} %tok_ref.5, ...), custom_call_target="tpu_custom_call", output_to_operand_aliasing={{5}: (10, {})} | custom-call | tf_op jit(solution)/shard_map/feed_forward/pallas_call | solution.py:889
  201.4 0.6 pad_maximum_fusion.3.vec_ref
  202.1 84.8 %attention_backward.1 = (f32[8,208,768]{2,1,0:T(8,128)}, f32[896,768]{1,0:T(8,128)}, f32[768,768]{1,0:T(8,128)}, f32[16,768]{1,0:T(8,128)}) custom-call(s32[8]{0:T(128)} %get-tuple-element.38.sid_ref, s32[8,2]{1,0:T(8,128)} %copy.55.grid_ref, bf16[8,208,768]{2,1,0:T(8,128)(2,1)} %tok_ref.5, f32[8,208,768]{2,1,0:T(8,128)} %get-tuple-element.44.mg_ref, ...), custom_call_target="tpu_custom_call" | custom-call | tf_op jit(solution)/shard_map/attention_backward/pallas_call | solution.py:935
  286.8 0.9 slice_bitcast_fusion
  287.9 0.7 pad.53.diag_ref
  288.6 2.4 undiag.1
  291.0 0.9 slice_bitcast_fusion.1
  292.3 1.0 slice_reduce_fusion
  293.4 0.7 pad_maximum_fusion.2
  294.1 2.8 slice.78
  296.9 1.9 slice.85
  298.8 1.7 slice_reduce_fusion.3
  300.5 0.6 convert_multiply_fusion
  301.1 0.6 convert_multiply_fusion.1
  301.7 0.6 slice_reduce_fusion.1
  302.3 1.3 fusion
  303.7 1.5 copy.67
  305.1 1.9 copy-done.1
  307.1 2.5 copy.68
  309.6 0.8 copy-done.3
  310.4 1.4 copy.69
  311.9 1.1 copy-done.4
  313.0 1.4 copy.70
  (75 shorter events, 3.3 us)
Async XLA Ops:
  0.7 3.9 %copy-start.20 = (bf16[192]{0:T(256)(128)(2,1)S(1)}, bf16[192]{0:T(256)(128)(2,1)}, u32[]{:S(2)}) copy-start(bf16[192]{0:T(256)(128)(2,1)} %param.25) | copy-start | bytes 1156
  0.7 3.9 %copy-start.21 = (bf16[192]{0:T(256)(128)(2,1)S(1)}, bf16[192]{0:T(256)(128)(2,1)}, u32[]{:S(2)}) copy-start(bf16[192]{0:T(256)(128)(2,1)} %param.26) | copy-start | bytes 1156
  0.7 4.0 %copy-start.5 = (bf16[3,2212]{1,0:T(4,128)(2,1)S(1)}, bf16[3,2212]{1,0:T(4,128)(2,1)}, u32[]{:S(2)}) copy-start(bf16[3,2212]{1,0:T(4,128)(2,1)} %param.27) | copy-start | bytes 39820
  0.7 4.1 %copy-start.12 = (bf16[768]{0:T(1024)(128)(2,1)S(1)}, bf16[768]{0:T(1024)(128)(2,1)}, u32[]{:S(2)}) copy-start(bf16[768]{0:T(1024)(128)(2,1)} %param.34) | copy-start | bytes 4612
  0.7 4.9 %copy-start.11 = (s32[8,2]{0,1:T(2,128)S(1)}, s32[8,2]{0,1:T(2,128)}, u32[]{:S(2)}) copy-start(s32[8,2]{0,1:T(2,128)} %param.21) | copy-start | bytes 196
  0.7 5.6 %copy-start.13 = (bf16[768]{0:T(1024)(128)(2,1)S(1)}, bf16[768]{0:T(1024)(128)(2,1)}, u32[]{:S(2)}) copy-start(bf16[768]{0:T(1024)(128)(2,1)} %param.22) | copy-start | bytes 4612
  0.7 6.2 %copy-start.14 = (bf16[768]{0:T(1024)(128)(2,1)S(1)}, bf16[768]{0:T(1024)(128)(2,1)}, u32[]{:S(2)}) copy-start(bf16[768]{0:T(1024)(128)(2,1)} %param.23) | copy-start | bytes 4612
  0.7 6.7 %copy-start.19 = (s32[8,2]{0,1:T(2,128)S(1)}, s32[8,2]{0,1:T(2,128)}, u32[]{:S(2)}) copy-start(s32[8,2]{0,1:T(2,128)} %constant.41.clone) | copy-start | bytes 196
  0.8 8.6 %copy-start.15 = (bf16[768]{0:T(1024)(128)(2,1)S(1)}, bf16[768]{0:T(1024)(128)(2,1)}, u32[]{:S(2)}) copy-start(bf16[768]{0:T(1024)(128)(2,1)} %param.29) | copy-start | bytes 4612
  2.1 7.8 %copy-start = (bf16[768,768]{1,0:T(8,128)(2,1)}, bf16[768,768]{1,0:T(8,128)(2,1)S(1)}, u32[]{:S(2)}) copy-start(bf16[768,768]{1,0:T(8,128)(2,1)S(1)} %pad_maximum_fusion.own_ref) | copy-start | bytes 3538948
  8.6 111.1 %copy-start.10 = (bf16[768]{0:T(1024)(128)(2,1)S(1)}, bf16[768]{0:T(1024)(128)(2,1)}, u32[]{:S(2)}) copy-start(bf16[768]{0:T(1024)(128)(2,1)} %param.30) | copy-start | bytes 4612
  8.6 111.1 %copy-start.9 = (bf16[768]{0:T(1024)(128)(2,1)S(1)}, bf16[768]{0:T(1024)(128)(2,1)}, u32[]{:S(2)}) copy-start(bf16[768]{0:T(1024)(128)(2,1)} %param.37) | copy-start | bytes 4612
  8.6 111.1 %copy-start.16 = (bf16[768]{0:T(1024)(128)(2,1)S(1)}, bf16[768]{0:T(1024)(128)(2,1)}, u32[]{:S(2)}) copy-start(bf16[768]{0:T(1024)(128)(2,1)} %param.31) | copy-start | bytes 4612
  8.6 111.1 %copy-start.17 = (bf16[768]{0:T(1024)(128)(2,1)S(1)}, bf16[768]{0:T(1024)(128)(2,1)}, u32[]{:S(2)}) copy-start(bf16[768]{0:T(1024)(128)(2,1)} %param.32) | copy-start | bytes 4612
  8.6 111.1 %copy-start.18 = (bf16[768]{0:T(1024)(128)(2,1)S(1)}, bf16[768]{0:T(1024)(128)(2,1)}, u32[]{:S(2)}) copy-start(bf16[768]{0:T(1024)(128)(2,1)} %param.36) | copy-start | bytes 4612
  120.4 81.0 %copy-start.7 = (f32[1,768]{1,0:T(1,128)S(1)}, f32[1,768]{1,0:T(1,128)}, u32[]{:S(2)}) copy-start(f32[1,768]{1,0:T(1,128)} %reshape.164.gain_ref) | copy-start | bytes 9220
  120.4 81.0 %copy-start.8 = (f32[1,768]{1,0:T(1,128)S(1)}, f32[1,768]{1,0:T(1,128)}, u32[]{:S(2)}) copy-start(f32[1,768]{1,0:T(1,128)} %reshape.166.shift_ref) | copy-start | bytes 9220
  292.1 9.6 %copy-start.6 = (f32[16,768]{1,0:T(8,128)S(1)}, f32[16,768]{1,0:T(8,128)}, u32[]{:S(2)}) copy-start(f32[16,768]{1,0:T(8,128)} %get-tuple-element.54) | copy-start | bytes 147460
  292.1 11.6 %copy-start.2 = (bf16[8,208,768]{2,1,0:T(8,128)(2,1)S(1)}, bf16[8,208,768]{2,1,0:T(8,128)(2,1)}, u32[]{:S(2)}) copy-start(bf16[8,208,768]{2,1,0:T(8,128)(2,1)} %get-tuple-element.101) | copy-start | bytes 7667716
  303.7 3.4 %copy-start.1 = (f32[8,208,768]{2,1,0:T(8,128)S(1)}, f32[8,208,768]{2,1,0:T(8,128)}, u32[]{:S(2)}) copy-start(f32[8,208,768]{2,1,0:T(8,128)} %get-tuple-element.102) | copy-start | bytes 15335428
  307.0 3.4 %copy-start.3 = (f32[768,768]{1,0:T(8,128)S(1)}, f32[768,768]{1,0:T(8,128)}, u32[]{:S(2)}) copy-start(f32[768,768]{1,0:T(8,128)} %get-tuple-element.114) | copy-start | bytes 7077892
  310.4 2.5 copy-start.4

commit v5 on v4

--- a/solution.py
+++ b/solution.py
@@ -62,13 +62,6 @@
             yield 0, centre + m, centre, at, wide
         if m < high - 1:
             yield 1, centre + 1 + m, centre + 1 - wide, at + 1, wide - 1
-
-
-def undiag_kernel(diag_ref, out_ref):
-    out_ref[...] = jnp.zeros_like(out_ref)
-    for shape_at in range(len(GRIDS)):
-        for which, row, col, at, size in windows(shape_at):
-            out_ref[row, :, col : col + size] += diag_ref[shape_at, which, :, at : at + size]
 
 
 def slot_masks(high, wide, reverse):
@@ -197,8 +190,8 @@
     return tuple((chunk, phase) for chunk, phase in steps if 0 <= chunk < ROW_CHUNKS + 3 * (phase == 0))
 
 
-LATE = {4: 7, 14: 8, 23: 9}
-LAST = ()
+LATE = {6: 7, 17: 8}
+LAST = (9,)
 
 
 def attention_forward(
@@ -576,9 +569,9 @@
 
 
 SMALL_ROWS = 128
-AB_TICKS = {0: ((0, 0),), 2: ((0, 1),), 5: ((0, 2),), 7: ((0, 3),), 8: ((1, 0),), 9: ((1, 1),), 12: ((1, 2),), 14: ((1, 3),), 15: ((0, 4),)}
-
-AB_LAST = ((1, 4), (0, 5), (1, 5), (0, 6), (1, 6))
+AB_TICKS = {0: ((0, 0),), 1: ((0, 1),), 4: ((0, 2),), 6: ((0, 3),)}
+AB_LATE = {0: ((1, 0), (0, 4)), 3: ((1, 1),), 7: ((0, 5),), 9: ((1, 2),), 12: ((1, 3),), 15: ((1, 4),)}
+AB_LAST = ((0, 6), (1, 5), (1, 6))
 
 
 def attention_backward(
@@ -601,9 +594,11 @@
     head_of = lax.broadcasted_iota(jnp.int32, (1, 256), 1) // HD
 
     def advance(i):
-        for when, steps in AB_TICKS.items():
-            if when % PAIR == i:
-                @pl.when(step == when // PAIR)
+        table = [(when % PAIR, when // PAIR, steps) for when, steps in AB_TICKS.items()]
+        table += [(8 + when % 4, half + when // 4, steps) for when, steps in AB_LATE.items()]
+        for part, when, steps in table:
+            if part == i:
+                @pl.when(step == when)
                 def _():
                     for chain, at in steps:
                         chains[chain].run(at)
@@ -715,9 +710,9 @@
         for c, ref in enumerate((dq, dk, dv)):
             ref[:, 0:256] = kept[c, at]
         for i in range(PAIR):
-            advance(i)
             here = slice(i * 208, (i + 1) * 208)
             for group in (1, 2):
+                advance(8 + i * 2 + group - 1)
                 lanes = slice(group * 256, group * 256 + 256)
                 probs = (p1_ref, p2_ref)[group - 1]
                 parts = heads_back(
@@ -770,6 +765,30 @@
             copy.wait()
         for chain in chains:
             chain.drain()
+
+
+def finish(tg_in, out_in, b_in, c_in, total_ref, tg_ref, out_ref, b_ref, c_ref, qkv_ref, proj_ref, table_ref):
+    tg_ref[...] = tg_in[...]
+    out_ref[...] = out_in[...]
+    b_ref[...] = b_in[...]
+    c_ref[...] = c_in[...]
+
+    step, steps = pl.program_id(0), pl.num_programs(0)
+    rows = qkv_ref.shape[0]
+    qkv_ref[...] = total_ref[pl.ds(pl.multiple_of(step * rows, 8), rows), :]
+    rows = proj_ref.shape[0]
+    proj_ref[...] = total_ref[pl.ds(pl.multiple_of(576 + step * rows, 8), rows), :]
+
+    @pl.when(step == 0)
+    def _():
+        table_ref[...] = jnp.zeros_like(table_ref)
+
+    for shape_at in range(len(GRIDS)):
+        @pl.when(step == shape_at)
+        def _():
+            for which, row, col, at, size in windows(shape_at):
+                first = 768 + shape_at * 8 + which * 3
+                table_ref[row, 0:3, col : col + size] += total_ref[first : first + 3, at : at + size]
 
 
 def make_body(wide_size, narrow_size):
@@ -978,19 +997,33 @@
             probs, vec, weights_a, sums, grad_c,
         )
 
-        grad_a = total[:width]
-        lines = total[width : width + 64, :DIAG].reshape(len(GRIDS), 8, DIAG)[:, : 2 * heads]
-        lines = jnp.pad(lines.reshape(len(GRIDS), 2, heads, DIAG), ((0, 0), (0, 0), (0, 8 - heads), (0, 0)))
-        square_grad = pl.pallas_call(
-            undiag_kernel, out_shape=struct(SPAN, 8, 128), name="undiag"
-        )(lines)
+        parts = len(GRIDS)
+
+        def image_block():
+            return pl.BlockSpec((images // parts, slots, width), lambda i: (i, 0, 0))
+
+        def row_block(total_rows=width):
+            return pl.BlockSpec((total_rows // parts, width), lambda i: (i, 0))
+
+        tokens_grad, layer_out, grad_b, grad_c, qkv_grad, proj_grad, square_grad = pl.pallas_call(
+            finish,
+            grid=(parts,),
+            in_specs=[image_block(), image_block(), row_block(), row_block(), vmem],
+            out_specs=[image_block(), image_block(), row_block(), row_block(), row_block(3 * local), row_block(local), vmem],
+            out_shape=[
+                struct(images, slots, width), struct(images, slots, width, dtype=BF16), struct(width, width),
+                struct(width, width), struct(3 * local, width), struct(local, width), struct(SPAN, 8, 128),
+            ],
+            compiler_params=params,
+            name="finish",
+        )(tokens_grad, layer_out, grad_b, grad_c, total)
+        qkv_grad = jnp.transpose(qkv_grad.reshape(3, local, width), (0, 2, 1))
         square_grad = jnp.transpose(square_grad[:, :heads, :SPAN], (1, 0, 2))[:, ::-1, ::-1]
         edges = jnp.sum(total[width + 64 : width + 73, :256], axis=1).reshape(3, heads).T
         table_grad = jnp.concatenate([square_grad.reshape(heads, SPAN * SPAN), edges], axis=1)
         more = total[width + 80 : width + 82, :local]
         sums = total[width + 88 : width + 95]
         late = jnp.sum(late.reshape(2, 8, width), axis=1)
-        qkv_grad = jnp.transpose(grad_a[: 3 * local].reshape(3, local, width), (0, 2, 1))
         return (
             layer_out,
             tokens_grad,
@@ -1000,7 +1033,7 @@
             more[0],
             more[1],
             table_grad,
-            grad_a[3 * local :],
+            proj_grad,
             sums[5] * attn_scale.astype(F32),
             sums[4],
             sums[2],

time: 315 us -> 300 us (0.952)
  local copies, waits for them, and re-layouts: 28.2 us -> 11 us
    pallas_call x1, Pallas kernels: 2.37 us -> 13.3 us  [body(): pl.pallas_call(finish, grid=(parts,), in_specs=[image_block(), image_bloc...]
    unnamed x50 -> x37, local copies, waits for them, and re-layouts: 11.5 us -> 0.76 us
    slice x2 -> x0, local copies, waits for them, and re-layouts: 4.71 us -> none  [the longest x1 2.8 us: body(): grad_a[:3 * local].reshape(3, local, width)]
    pallas_call x1, Pallas kernels: 84.8 us -> 80.2 us  [body(): pl.pallas_call(functools.partial(attention_backward, beyond=beyond), grid...]
    pallas_call x1, Pallas kernels: 110 us -> 106 us  [body(): pl.pallas_call(functools.partial(attention_forward, narrow=narrow_size),...]
where the time goes in v5:
time: 300 us; the launch traced here: 299 us
  Pallas kernels  280 us (93%)
  local copies, waits for them, and re-layouts  11 us (4%)
  other arithmetic  7.11 us (2%)
    pallas_call x1, Pallas kernels, body(): pl.pallas_call(functools.partial(attention_forward, narrow=narrow_size),...  106 us
    pallas_call x1, Pallas kernels, body(): pl.pallas_call(functools.partial(feed_forward, narrow=narrow_size, beyond...  80.3 us
    pallas_call x1, Pallas kernels, body(): pl.pallas_call(functools.partial(attention_backward, beyond=beyond), grid...  80.2 us
    pallas_call x1, Pallas kernels, body(): pl.pallas_call(finish, grid=(parts,), in_specs=[image_block(), image_bloc...  13.3 us

profile of v5, /device:TPU:1, one launch (start us, length us, event | category | flops | bytes accessed | tf_op | source)
XLA Modules:
  0.0 299.3 jit_solution(1428960684599450670)
XLA Ops:
  0.8 1.4 pad_maximum_fusion.own_ref
  2.2 1.4 dynamic-slice_bitcast_fusion
  3.5 1.0 maximum_convert_fusion.slices
  4.5 0.1 fusion.1
  4.7 0.1 reshape_reshape.2
  5.0 0.6 pad_maximum_fusion.1.small_ref
  5.6 0.7 copy.54.grid_ref
  6.3 0.6 reshape.156.gain_ref
  6.9 0.6 reshape.158.shift_ref
  7.6 0.7 iota_reduce_fusion
  8.2 0.1 reshape.136
  8.4 0.2 rev.6
  8.6 0.7 pad.39.table_ref
  9.3 0.6 reshape.160.pb_ref
  9.9 106.3 %attention_forward.1 = (bf16[8,12,208,256]{3,2,1,0:T(8,128)(2,1)}, bf16[8,208,768]{2,1,0:T(8,128)(2,1)}, f32[8,208,768]{2,1,0:T(8,128)}, bf16[4,768,768]{2,1,0:T...) custom-call(s32[8]{0:T(128)} %get-tuple-element.45.sid_ref, ...), custom_call_target="tpu_custom_call" | custom-call | tf_op jit(solution)/shard_map/attention_forward/pallas_call | solution.py:851
  116.3 0.6 concatenate.29.vec_ref
  117.0 80.3 %feed_forward.1 = (bf16[8,208,768]{2,1,0:T(8,128)(2,1)}, f32[8,208,768]{2,1,0:T(8,128)}, f32[768,768]{1,0:T(8,128)}, f32[768,768]{1,0:T(8,128)}, f32[7,8,768]{2,1,0:T(8,128)}, /*index=5*/f32[3,768,768]{2,1,0:T(8,128)}) custom-call(s32[8,2]{1,0:T(8,128)} %copy.54.grid_ref, bf16[8,208,768]{2,1,0:T(8,128)(2,1)} %tok_ref.5, ...), custom_call_target="tpu_custom_call", output_to_operand_aliasing={{5}: (10, {})} | custom-call | tf_op jit(solution)/shard_map/feed_forward/pallas_call | solution.py:908
  197.3 0.6 pad_maximum_fusion.3.vec_ref
  197.9 80.2 %attention_backward.1 = (f32[8,208,768]{2,1,0:T(8,128)}, f32[896,768]{1,0:T(8,128)}, f32[768,768]{1,0:T(8,128)}, f32[16,768]{1,0:T(8,128)}) custom-call(s32[8]{0:T(128)} %get-tuple-element.45.sid_ref, s32[8,2]{1,0:T(8,128)} %copy.54.grid_ref, bf16[8,208,768]{2,1,0:T(8,128)(2,1)} %tok_ref.5, f32[8,208,768]{2,1,0:T(8,128)} %get-tuple-element.50.mg_ref, ...), custom_call_target="tpu_custom_call" | custom-call | tf_op jit(solution)/shard_map/attention_backward/pallas_call | solution.py:954
  278.2 13.3 %finish.1 = (f32[8,208,768]{2,1,0:T(8,128)}, bf16[8,208,768]{2,1,0:T(8,128)(2,1)}, f32[768,768]{1,0:T(8,128)}, f32[768,768]{1,0:T(8,128)}, f32[576,768]{1,0:T(8,...) custom-call(f32[8,208,768]{2,1,0:T(8,128)} %get-tuple-element.59.tg_in, bf16[8,208,768]{2,1,0:T(8,128)(2,1)} %get-tuple-element.60.out_in, ...), custom_call_target="tpu_custom_call" | custom-call | tf_op jit(solution)/shard_map/finish/pallas_call | solution.py:1008
  291.5 0.9 slice_bitcast_fusion
  292.4 0.2 rev.7
  292.6 0.1 reshape.153
  292.8 0.8 slice_reduce_fusion
  293.6 0.1 reshape.154
  293.7 0.1 copy.56
  293.8 0.7 pad_maximum_fusion.2
  294.5 1.7 slice_reduce_fusion.3
  296.1 0.6 convert_multiply_fusion
  296.7 0.6 convert_multiply_fusion.1
  297.3 0.6 slice_reduce_fusion.1
  298.0 1.3 fusion
  (57 shorter events, 0.5 us)
Async XLA Ops:
  0.7 3.9 %copy-start.16 = (bf16[192]{0:T(256)(128)(2,1)S(1)}, bf16[192]{0:T(256)(128)(2,1)}, u32[]{:S(2)}) copy-start(bf16[192]{0:T(256)(128)(2,1)} %param.25) | copy-start | bytes 1156
  0.7 3.9 %copy-start.17 = (bf16[192]{0:T(256)(128)(2,1)S(1)}, bf16[192]{0:T(256)(128)(2,1)}, u32[]{:S(2)}) copy-start(bf16[192]{0:T(256)(128)(2,1)} %param.26) | copy-start | bytes 1156
  0.7 4.0 %copy-start.1 = (bf16[3,2212]{1,0:T(4,128)(2,1)S(1)}, bf16[3,2212]{1,0:T(4,128)(2,1)}, u32[]{:S(2)}) copy-start(bf16[3,2212]{1,0:T(4,128)(2,1)} %param.27) | copy-start | bytes 39820
  0.7 4.1 %copy-start.8 = (bf16[768]{0:T(1024)(128)(2,1)S(1)}, bf16[768]{0:T(1024)(128)(2,1)}, u32[]{:S(2)}) copy-start(bf16[768]{0:T(1024)(128)(2,1)} %param.34) | copy-start | bytes 4612
  0.7 4.9 %copy-start.7 = (s32[8,2]{0,1:T(2,128)S(1)}, s32[8,2]{0,1:T(2,128)}, u32[]{:S(2)}) copy-start(s32[8,2]{0,1:T(2,128)} %param.21) | copy-start | bytes 196
  0.7 5.6 %copy-start.9 = (bf16[768]{0:T(1024)(128)(2,1)S(1)}, bf16[768]{0:T(1024)(128)(2,1)}, u32[]{:S(2)}) copy-start(bf16[768]{0:T(1024)(128)(2,1)} %param.22) | copy-start | bytes 4612
  0.7 6.2 %copy-start.10 = (bf16[768]{0:T(1024)(128)(2,1)S(1)}, bf16[768]{0:T(1024)(128)(2,1)}, u32[]{:S(2)}) copy-start(bf16[768]{0:T(1024)(128)(2,1)} %param.23) | copy-start | bytes 4612
  0.7 6.7 %copy-start.15 = (s32[8,2]{0,1:T(2,128)S(1)}, s32[8,2]{0,1:T(2,128)}, u32[]{:S(2)}) copy-start(s32[8,2]{0,1:T(2,128)} %constant.41.clone) | copy-start | bytes 196
  0.8 8.6 %copy-start.11 = (bf16[768]{0:T(1024)(128)(2,1)S(1)}, bf16[768]{0:T(1024)(128)(2,1)}, u32[]{:S(2)}) copy-start(bf16[768]{0:T(1024)(128)(2,1)} %param.29) | copy-start | bytes 4612
  2.1 7.8 %copy-start = (bf16[768,768]{1,0:T(8,128)(2,1)}, bf16[768,768]{1,0:T(8,128)(2,1)S(1)}, u32[]{:S(2)}) copy-start(bf16[768,768]{1,0:T(8,128)(2,1)S(1)} %pad_maximum_fusion.own_ref) | copy-start | bytes 3538948
  8.6 107.7 %copy-start.6 = (bf16[768]{0:T(1024)(128)(2,1)S(1)}, bf16[768]{0:T(1024)(128)(2,1)}, u32[]{:S(2)}) copy-start(bf16[768]{0:T(1024)(128)(2,1)} %param.30) | copy-start | bytes 4612
  8.6 107.7 %copy-start.5 = (bf16[768]{0:T(1024)(128)(2,1)S(1)}, bf16[768]{0:T(1024)(128)(2,1)}, u32[]{:S(2)}) copy-start(bf16[768]{0:T(1024)(128)(2,1)} %param.37) | copy-start | bytes 4612
  8.6 107.7 %copy-start.12 = (bf16[768]{0:T(1024)(128)(2,1)S(1)}, bf16[768]{0:T(1024)(128)(2,1)}, u32[]{:S(2)}) copy-start(bf16[768]{0:T(1024)(128)(2,1)} %param.31) | copy-start | bytes 4612
  8.6 107.7 %copy-start.13 = (bf16[768]{0:T(1024)(128)(2,1)S(1)}, bf16[768]{0:T(1024)(128)(2,1)}, u32[]{:S(2)}) copy-start(bf16[768]{0:T(1024)(128)(2,1)} %param.32) | copy-start | bytes 4612
  8.6 107.7 %copy-start.14 = (bf16[768]{0:T(1024)(128)(2,1)S(1)}, bf16[768]{0:T(1024)(128)(2,1)}, u32[]{:S(2)}) copy-start(bf16[768]{0:T(1024)(128)(2,1)} %param.36) | copy-start | bytes 4612
  117.0 80.3 %copy-start.3 = (f32[1,768]{1,0:T(1,128)S(1)}, f32[1,768]{1,0:T(1,128)}, u32[]{:S(2)}) copy-start(f32[1,768]{1,0:T(1,128)} %reshape.156.gain_ref) | copy-start | bytes 9220
  117.0 80.3 %copy-start.4 = (f32[1,768]{1,0:T(1,128)S(1)}, f32[1,768]{1,0:T(1,128)}, u32[]{:S(2)}) copy-start(f32[1,768]{1,0:T(1,128)} %reshape.158.shift_ref) | copy-start | bytes 9220
  278.2 19.2 %copy-start.2 = (f32[16,768]{1,0:T(8,128)S(1)}, f32[16,768]{1,0:T(8,128)}, u32[]{:S(2)}) copy-start(f32[16,768]{1,0:T(8,128)} %get-tuple-element.66) | copy-start | bytes 147460

commit v6 on v5

--- a/solution.py
+++ b/solution.py
@@ -62,6 +62,14 @@
             yield 0, centre + m, centre, at, wide
         if m < high - 1:
             yield 1, centre + 1 + m, centre + 1 - wide, at + 1, wide - 1
+
+
+def kind_of(grid_ref, image):
+    high, wide = grid_ref[image, 0], grid_ref[image, 1]
+    kind = jnp.int32(0)
+    for at, (grid_high, grid_wide) in enumerate(GRIDS):
+        kind = jnp.where((high == grid_high) & (wide == grid_wide), at, kind)
+    return kind
 
 
 def slot_masks(high, wide, reverse):
@@ -190,12 +198,12 @@
     return tuple((chunk, phase) for chunk, phase in steps if 0 <= chunk < ROW_CHUNKS + 3 * (phase == 0))
 
 
-LATE = {6: 7, 17: 8}
+LATE = {7: 7, 16: 8}
 LAST = (9,)
 
 
 def attention_forward(
-    sid_ref, grid_ref, tok_ref, gain_ref, shift_ref, pb_ref, own_ref, slices, table_ref, small_ref,
+    grid_ref, tok_ref, gain_ref, shift_ref, pb_ref, own_ref, slices, table_ref, small_ref,
     prob_ref, att_ref, branch_ref, wa_ref, small_out, q_out, k_out, v_out, gath_b, gath_c,
     stage, first_in, queries, k_pad, v_pad, bias, lined, diag, far, smalls, send, recv, extra_send, extra_recv, local,
     narrow,
@@ -224,7 +232,7 @@
             both = p_patch & s_patch
             open_key = s <= limit
             for h in range(3):
-                row = h * 16 + sid_ref[at] * 2
+                row = h * 16 + kind_of(grid_ref, at) * 2
                 toep = [
                     pltpu.roll(
                         jnp.broadcast_to(table(row + which), (208, DIAG)), DIAG - 207, 1, stride=1, stride_axis=0
@@ -443,9 +451,9 @@
 
 
 PAIR = 2
-FF_GATHER = {0: ((8, 1),), 1: ((8, 2), (9, 1)), 3: ((8, 3), (9, 2), (10, 1)), 5: ((9, 3), (10, 2)), 8: ((10, 3),)}
-
-FF_SUM = {4: 0, 7: 1, 10: 2, 11: 3, 13: 4, 15: 5}
+FF_GATHER = {0: ((8, 1),), 1: ((8, 2), (9, 1)), 2: ((10, 1),), 3: ((8, 3), (9, 2)), 5: ((9, 3), (10, 2)), 8: ((10, 3),)}
+
+FF_SUM = {4: 0, 7: 1, 9: 2, 11: 3, 13: 4, 15: 5}
 
 
 def feed_forward(
@@ -575,7 +583,7 @@
 
 
 def attention_backward(
-    sid_ref, grid_ref, tok_ref, mg_ref, att_ref, q0_ref, k0_ref, v0_ref, p0_ref, q_ref, k_ref, v_ref, p1_ref, p2_ref,
+    grid_ref, tok_ref, mg_ref, att_ref, q0_ref, k0_ref, v0_ref, p0_ref, q_ref, k_ref, v_ref, p1_ref, p2_ref,
     vec_ref, wa_ref, ff_sums_ref, grad_c,
     tg_ref, total_out, out_c, late_total,
     total, total_c, grads, attn_lows, kept, dq, dk, dv, lines, edges, sums, late, late_in, late_between,
@@ -658,7 +666,7 @@
             image = step * PAIR + i
             p, s, limit, later, p_patch, s_patch = slot_masks(grid_ref[image, 0], grid_ref[image, 1], True)
             both = p_patch & s_patch
-            kind = sid_ref[image]
+            kind = kind_of(grid_ref, image)
 
             def table_grad(h, score_grad, low):
                 if h == 3:
@@ -821,9 +829,6 @@
         small = jnp.stack([small_for(k) for k in range(narrow_size)])
         all_heads = narrow_size * heads
 
-        kinds = jnp.array(GRIDS, jnp.int32)
-        sid = jnp.argmax(jnp.all(grid_shape[:, None, :] == kinds[None], axis=-1), axis=-1).astype(jnp.int32)
-
         def row(v):
             return v.astype(F32).reshape(1, -1)
 
@@ -851,7 +856,7 @@
         probs, attended, branch, weights_a, small, queries, keys, values, gath_b, gath_c = pl.pallas_call(
             functools.partial(attention_forward, narrow=narrow_size),
             grid=(images,),
-            in_specs=[smem, smem, vmem] + [whole(1, width)] * 3 + [vmem] * 4,
+            in_specs=[smem, vmem] + [whole(1, width)] * 3 + [vmem] * 4,
             out_specs=[per_image(all_heads, slots, 256), per_image(slots, width), per_image(slots, width)]
             + [vmem, vmem] + [anyspace] * 5,
             scratch_shapes=[
@@ -889,7 +894,7 @@
             ),
             name="attention_forward",
         )(
-            sid, grid_shape, tokens, row(first_gain), row(first_shift), row(proj_bias), own_a, slices, square, small,
+            grid_shape, tokens, row(first_gain), row(first_shift), row(proj_bias), own_a, slices, square, small,
         )
 
         vec = jnp.concatenate([row(v) for v in (attn_scale, second_gain, second_shift, mlp_scale, down_bias)])
@@ -954,7 +959,7 @@
         tokens_grad, total, grad_c, late = pl.pallas_call(
             functools.partial(attention_backward, beyond=beyond),
             grid=(2 * pairs,),
-            in_specs=[smem, smem, both_passes, both_passes]
+            in_specs=[smem, both_passes, both_passes]
             + [first_pass(slots, 256)] * 2
             + [first_pass(256, 256)] * 2
             + [first_pass(4, slots, 256)]
@@ -993,7 +998,7 @@
             compiler_params=remote_params(2),
             name="attention_backward",
         )(
-            sid, grid_shape, tokens, middle_grad, attended, queries, keys, values, probs, queries, keys, values, probs,
+            grid_shape, tokens, middle_grad, attended, queries, keys, values, probs, queries, keys, values, probs,
             probs, vec, weights_a, sums, grad_c,
         )
 

time: 300 us -> 299 us (level)
  no operation moved by 1% of the time
where the time goes in v6:
time: 299 us; the launch traced here: 298 us
  Pallas kernels  280 us (94%)
  local copies, waits for them, and re-layouts  11 us (4%)
  other arithmetic  6.36 us (2%)
    pallas_call x1, Pallas kernels, body(): pl.pallas_call(functools.partial(attention_forward, narrow=narrow_size),...  106 us
    pallas_call x1, Pallas kernels, body(): pl.pallas_call(functools.partial(feed_forward, narrow=narrow_size, beyond...  81.2 us
    pallas_call x1, Pallas kernels, body(): pl.pallas_call(functools.partial(attention_backward, beyond=beyond), grid...  79.4 us
    pallas_call x1, Pallas kernels, body(): pl.pallas_call(finish, grid=(parts,), in_specs=[image_block(), image_bloc...  13.3 us

profile of v6, /device:TPU:1, one launch (start us, length us, event | category | flops | bytes accessed | tf_op | source)
XLA Modules:
  0.0 298.3 jit_solution(15157430288975642153)
XLA Ops:
  0.8 1.4 pad_maximum_fusion.own_ref
  2.2 1.4 dynamic-slice_bitcast_fusion
  3.5 1.0 maximum_convert_fusion.slices
  4.5 0.1 fusion.1
  4.6 0.1 slice.75
  4.7 0.1 reshape_reshape.2
  5.0 0.6 pad_maximum_fusion.1.small_ref
  5.6 0.7 copy.45.grid_ref
  6.3 0.6 reshape.154.gain_ref
  6.9 0.6 reshape.156.shift_ref
  7.5 0.1 reshape.134
  7.6 0.2 rev.6
  7.9 0.7 pad.39.table_ref
  8.6 0.6 reshape.158.pb_ref
  9.2 106.1 %attention_forward.1 = (bf16[8,12,208,256]{3,2,1,0:T(8,128)(2,1)}, bf16[8,208,768]{2,1,0:T(8,128)(2,1)}, f32[8,208,768]{2,1,0:T(8,128)}, bf16[4,768,768]{2,1,0:T...) custom-call(s32[8,2]{1,0:T(8,128)} %copy.45.grid_ref, ...), custom_call_target="tpu_custom_call" | custom-call | tf_op jit(solution)/shard_map/attention_forward/pallas_call | solution.py:856
  115.4 0.6 concatenate.29.vec_ref
  116.0 81.2 %feed_forward.1 = (bf16[8,208,768]{2,1,0:T(8,128)(2,1)}, f32[8,208,768]{2,1,0:T(8,128)}, f32[768,768]{1,0:T(8,128)}, f32[768,768]{1,0:T(8,128)}, f32[7,8,768]{2,1,0:T(8,128)}, /*index=5*/f32[3,768,768]{2,1,0:T(8,128)}) custom-call(s32[8,2]{1,0:T(8,128)} %copy.45.grid_ref, bf16[8,208,768]{2,1,0:T(8,128)(2,1)} %tok_ref.5, ...), custom_call_target="tpu_custom_call", output_to_operand_aliasing={{5}: (10, {})} | custom-call | tf_op jit(solution)/shard_map/feed_forward/pallas_call | solution.py:913
  197.2 0.6 pad_maximum_fusion.3.vec_ref
  197.8 79.4 %attention_backward.1 = (f32[8,208,768]{2,1,0:T(8,128)}, f32[896,768]{1,0:T(8,128)}, f32[768,768]{1,0:T(8,128)}, f32[16,768]{1,0:T(8,128)}) custom-call(s32[8,2]{1,0:T(8,128)} %copy.45.grid_ref, bf16[8,208,768]{2,1,0:T(8,128)(2,1)} %tok_ref.5, f32[8,208,768]{2,1,0:T(8,128)} %get-tuple-element.48.mg_ref, bf16[8,208,768]{2,1,0:T(8,128)(2,1)} %get-tuple-element.49.att_ref, ...), custom_call_target="tpu_custom_call" | custom-call | tf_op jit(solution)/shard_map/attention_backward/pallas_call | solution.py:959
  277.2 13.3 %finish.1 = (f32[8,208,768]{2,1,0:T(8,128)}, bf16[8,208,768]{2,1,0:T(8,128)(2,1)}, f32[768,768]{1,0:T(8,128)}, f32[768,768]{1,0:T(8,128)}, f32[576,768]{1,0:T(8,...) custom-call(f32[8,208,768]{2,1,0:T(8,128)} %get-tuple-element.57.tg_in, bf16[8,208,768]{2,1,0:T(8,128)(2,1)} %get-tuple-element.58.out_in, ...), custom_call_target="tpu_custom_call" | custom-call | tf_op jit(solution)/shard_map/finish/pallas_call | solution.py:1013
  290.5 0.9 slice_bitcast_fusion
  291.5 0.2 rev.7
  291.7 0.1 reshape.151
  291.8 0.8 slice_reduce_fusion
  292.6 0.1 reshape.152
  292.7 0.1 copy.47
  292.8 0.7 pad_maximum_fusion.2
  293.5 1.7 slice_reduce_fusion.3
  295.2 0.6 convert_multiply_fusion
  295.8 0.6 convert_multiply_fusion.1
  296.4 0.6 slice_reduce_fusion.1
  297.0 1.3 fusion
  (53 shorter events, 0.4 us)
Async XLA Ops:
  0.7 3.9 %copy-start.15 = (bf16[192]{0:T(256)(128)(2,1)S(1)}, bf16[192]{0:T(256)(128)(2,1)}, u32[]{:S(2)}) copy-start(bf16[192]{0:T(256)(128)(2,1)} %param.24) | copy-start | bytes 1156
  0.7 3.8 %copy-start.16 = (bf16[192]{0:T(256)(128)(2,1)S(1)}, bf16[192]{0:T(256)(128)(2,1)}, u32[]{:S(2)}) copy-start(bf16[192]{0:T(256)(128)(2,1)} %param.25) | copy-start | bytes 1156
  0.7 3.9 %copy-start.1 = (bf16[3,2212]{1,0:T(4,128)(2,1)S(1)}, bf16[3,2212]{1,0:T(4,128)(2,1)}, u32[]{:S(2)}) copy-start(bf16[3,2212]{1,0:T(4,128)(2,1)} %param.26) | copy-start | bytes 39820
  0.7 4.1 %copy-start.7 = (bf16[768]{0:T(1024)(128)(2,1)S(1)}, bf16[768]{0:T(1024)(128)(2,1)}, u32[]{:S(2)}) copy-start(bf16[768]{0:T(1024)(128)(2,1)} %param.33) | copy-start | bytes 4612
  0.7 4.9 %copy-start.14 = (s32[8,2]{0,1:T(2,128)S(1)}, s32[8,2]{0,1:T(2,128)}, u32[]{:S(2)}) copy-start(s32[8,2]{0,1:T(2,128)} %param.20) | copy-start | bytes 196
  0.7 5.6 %copy-start.8 = (bf16[768]{0:T(1024)(128)(2,1)S(1)}, bf16[768]{0:T(1024)(128)(2,1)}, u32[]{:S(2)}) copy-start(bf16[768]{0:T(1024)(128)(2,1)} %param.21) | copy-start | bytes 4612
  0.7 6.2 %copy-start.9 = (bf16[768]{0:T(1024)(128)(2,1)S(1)}, bf16[768]{0:T(1024)(128)(2,1)}, u32[]{:S(2)}) copy-start(bf16[768]{0:T(1024)(128)(2,1)} %param.22) | copy-start | bytes 4612
  0.7 7.8 %copy-start.10 = (bf16[768]{0:T(1024)(128)(2,1)S(1)}, bf16[768]{0:T(1024)(128)(2,1)}, u32[]{:S(2)}) copy-start(bf16[768]{0:T(1024)(128)(2,1)} %param.28) | copy-start | bytes 4612
  2.1 7.0 %copy-start = (bf16[768,768]{1,0:T(8,128)(2,1)}, bf16[768,768]{1,0:T(8,128)(2,1)S(1)}, u32[]{:S(2)}) copy-start(bf16[768,768]{1,0:T(8,128)(2,1)S(1)} %pad_maximum_fusion.own_ref) | copy-start | bytes 3538948
  7.8 107.4 %copy-start.6 = (bf16[768]{0:T(1024)(128)(2,1)S(1)}, bf16[768]{0:T(1024)(128)(2,1)}, u32[]{:S(2)}) copy-start(bf16[768]{0:T(1024)(128)(2,1)} %param.29) | copy-start | bytes 4612
  7.8 107.4 %copy-start.5 = (bf16[768]{0:T(1024)(128)(2,1)S(1)}, bf16[768]{0:T(1024)(128)(2,1)}, u32[]{:S(2)}) copy-start(bf16[768]{0:T(1024)(128)(2,1)} %param.36) | copy-start | bytes 4612
  7.8 107.5 %copy-start.11 = (bf16[768]{0:T(1024)(128)(2,1)S(1)}, bf16[768]{0:T(1024)(128)(2,1)}, u32[]{:S(2)}) copy-start(bf16[768]{0:T(1024)(128)(2,1)} %param.30) | copy-start | bytes 4612
  7.8 107.5 %copy-start.12 = (bf16[768]{0:T(1024)(128)(2,1)S(1)}, bf16[768]{0:T(1024)(128)(2,1)}, u32[]{:S(2)}) copy-start(bf16[768]{0:T(1024)(128)(2,1)} %param.31) | copy-start | bytes 4612
  7.9 107.5 %copy-start.13 = (bf16[768]{0:T(1024)(128)(2,1)S(1)}, bf16[768]{0:T(1024)(128)(2,1)}, u32[]{:S(2)}) copy-start(bf16[768]{0:T(1024)(128)(2,1)} %param.35) | copy-start | bytes 4612
  116.0 81.2 %copy-start.3 = (f32[1,768]{1,0:T(1,128)S(1)}, f32[1,768]{1,0:T(1,128)}, u32[]{:S(2)}) copy-start(f32[1,768]{1,0:T(1,128)} %reshape.154.gain_ref) | copy-start | bytes 9220
  116.0 81.2 %copy-start.4 = (f32[1,768]{1,0:T(1,128)S(1)}, f32[1,768]{1,0:T(1,128)}, u32[]{:S(2)}) copy-start(f32[1,768]{1,0:T(1,128)} %reshape.156.shift_ref) | copy-start | bytes 9220
  277.2 19.2 %copy-start.2 = (f32[16,768]{1,0:T(8,128)S(1)}, f32[16,768]{1,0:T(8,128)}, u32[]{:S(2)}) copy-start(f32[16,768]{1,0:T(8,128)} %get-tuple-element.64) | copy-start | bytes 147460

commit v7 on v6

--- a/solution.py
+++ b/solution.py
@@ -198,7 +198,7 @@
     return tuple((chunk, phase) for chunk, phase in steps if 0 <= chunk < ROW_CHUNKS + 3 * (phase == 0))
 
 
-LATE = {7: 7, 16: 8}
+LATE = {8: 7, 15: 8}
 LAST = (9,)
 
 
@@ -579,7 +579,7 @@
 SMALL_ROWS = 128
 AB_TICKS = {0: ((0, 0),), 1: ((0, 1),), 4: ((0, 2),), 6: ((0, 3),)}
 AB_LATE = {0: ((1, 0), (0, 4)), 3: ((1, 1),), 7: ((0, 5),), 9: ((1, 2),), 12: ((1, 3),), 15: ((1, 4),)}
-AB_LAST = ((0, 6), (1, 5), (1, 6))
+AB_LAST = ((1, 5), (0, 6), (1, 6))
 
 
 def attention_backward(
@@ -775,17 +775,15 @@
             chain.drain()
 
 
-def finish(tg_in, out_in, b_in, c_in, total_ref, tg_ref, out_ref, b_ref, c_ref, qkv_ref, proj_ref, table_ref):
+def finish(tg_in, out_in, b_in, c_in, qkv_in, proj_in, lines_ref, tg_ref, out_ref, b_ref, c_ref, qkv_ref, proj_ref, table_ref):
     tg_ref[...] = tg_in[...]
     out_ref[...] = out_in[...]
     b_ref[...] = b_in[...]
     c_ref[...] = c_in[...]
 
-    step, steps = pl.program_id(0), pl.num_programs(0)
-    rows = qkv_ref.shape[0]
-    qkv_ref[...] = total_ref[pl.ds(pl.multiple_of(step * rows, 8), rows), :]
-    rows = proj_ref.shape[0]
-    proj_ref[...] = total_ref[pl.ds(pl.multiple_of(576 + step * rows, 8), rows), :]
+    step = pl.program_id(0)
+    qkv_ref[...] = qkv_in[...]
+    proj_ref[...] = proj_in[...]
 
     @pl.when(step == 0)
     def _():
@@ -795,8 +793,8 @@
         @pl.when(step == shape_at)
         def _():
             for which, row, col, at, size in windows(shape_at):
-                first = 768 + shape_at * 8 + which * 3
-                table_ref[row, 0:3, col : col + size] += total_ref[first : first + 3, at : at + size]
+                first = shape_at * 8 + which * 3
+                table_ref[row, 0:3, col : col + size] += lines_ref[first : first + 3, at : at + size]
 
 
 def make_body(wide_size, narrow_size):
@@ -1013,7 +1011,11 @@
         tokens_grad, layer_out, grad_b, grad_c, qkv_grad, proj_grad, square_grad = pl.pallas_call(
             finish,
             grid=(parts,),
-            in_specs=[image_block(), image_block(), row_block(), row_block(), vmem],
+            in_specs=[image_block(), image_block(), row_block(), row_block(), row_block(3 * local)]
+            + [
+                pl.BlockSpec((local // parts, width), lambda i: (3 * parts + i, 0)),
+                pl.BlockSpec((SMALL_ROWS, width), lambda i: (width // SMALL_ROWS, 0)),
+            ],
             out_specs=[image_block(), image_block(), row_block(), row_block(), row_block(3 * local), row_block(local), vmem],
             out_shape=[
                 struct(images, slots, width), struct(images, slots, width, dtype=BF16), struct(width, width),
@@ -1021,7 +1023,7 @@
             ],
             compiler_params=params,
             name="finish",
-        )(tokens_grad, layer_out, grad_b, grad_c, total)
+        )(tokens_grad, layer_out, grad_b, grad_c, total, total, total)
         qkv_grad = jnp.transpose(qkv_grad.reshape(3, local, width), (0, 2, 1))
         square_grad = jnp.transpose(square_grad[:, :heads, :SPAN], (1, 0, 2))[:, ::-1, ::-1]
         edges = jnp.sum(total[width + 64 : width + 73, :256], axis=1).reshape(3, heads).T

time: 299 us -> 299 us (level)
  no operation moved by 1% of the time
where the time goes in v7:
time: 299 us; the launch traced here: 298 us
  Pallas kernels  280 us (94%)
  local copies, waits for them, and re-layouts  11 us (4%)
  other arithmetic  6.36 us (2%)
    pallas_call x1, Pallas kernels, body(): pl.pallas_call(functools.partial(attention_forward, narrow=narrow_size),...  107 us
    pallas_call x1, Pallas kernels, body(): pl.pallas_call(functools.partial(feed_forward, narrow=narrow_size, beyond...  80.7 us
    pallas_call x1, Pallas kernels, body(): pl.pallas_call(functools.partial(attention_backward, beyond=beyond), grid...  79.4 us
    pallas_call x1, Pallas kernels, body(): pl.pallas_call(finish, grid=(parts,), in_specs=[image_block(), image_bloc...  13.3 us

profile of v7, /device:TPU:1, one launch (start us, length us, event | category | flops | bytes accessed | tf_op | source)
XLA Modules:
  0.0 298.3 jit_solution(17052935500037361864)
XLA Ops:
  0.8 1.4 pad_maximum_fusion.own_ref
  2.2 1.4 dynamic-slice_bitcast_fusion
  3.5 1.0 maximum_convert_fusion.slices
  4.5 0.1 fusion.1
  4.6 0.1 slice.75
  4.7 0.1 reshape_reshape.2
  5.0 0.6 pad_maximum_fusion.1.small_ref
  5.6 0.7 copy.45.grid_ref
  6.3 0.6 reshape.154.gain_ref
  6.9 0.6 reshape.156.shift_ref
  7.5 0.1 reshape.134
  7.6 0.2 rev.6
  7.9 0.7 pad.39.table_ref
  8.6 0.6 reshape.158.pb_ref
  9.2 106.5 %attention_forward.1 = (bf16[8,12,208,256]{3,2,1,0:T(8,128)(2,1)}, bf16[8,208,768]{2,1,0:T(8,128)(2,1)}, f32[8,208,768]{2,1,0:T(8,128)}, bf16[4,768,768]{2,1,0:T...) custom-call(s32[8,2]{1,0:T(8,128)} %copy.45.grid_ref, ...), custom_call_target="tpu_custom_call" | custom-call | tf_op jit(solution)/shard_map/attention_forward/pallas_call | solution.py:854
  115.8 0.6 concatenate.29.vec_ref
  116.4 80.7 %feed_forward.1 = (bf16[8,208,768]{2,1,0:T(8,128)(2,1)}, f32[8,208,768]{2,1,0:T(8,128)}, f32[768,768]{1,0:T(8,128)}, f32[768,768]{1,0:T(8,128)}, f32[7,8,768]{2,1,0:T(8,128)}, /*index=5*/f32[3,768,768]{2,1,0:T(8,128)}) custom-call(s32[8,2]{1,0:T(8,128)} %copy.45.grid_ref, bf16[8,208,768]{2,1,0:T(8,128)(2,1)} %tok_ref.5, ...), custom_call_target="tpu_custom_call", output_to_operand_aliasing={{5}: (10, {})} | custom-call | tf_op jit(solution)/shard_map/feed_forward/pallas_call | solution.py:911
  197.2 0.6 pad_maximum_fusion.3.vec_ref
  197.8 79.4 %attention_backward.1 = (f32[8,208,768]{2,1,0:T(8,128)}, f32[896,768]{1,0:T(8,128)}, f32[768,768]{1,0:T(8,128)}, f32[16,768]{1,0:T(8,128)}) custom-call(s32[8,2]{1,0:T(8,128)} %copy.45.grid_ref, bf16[8,208,768]{2,1,0:T(8,128)(2,1)} %tok_ref.5, f32[8,208,768]{2,1,0:T(8,128)} %get-tuple-element.48.mg_ref, bf16[8,208,768]{2,1,0:T(8,128)(2,1)} %get-tuple-element.49.att_ref, ...), custom_call_target="tpu_custom_call" | custom-call | tf_op jit(solution)/shard_map/attention_backward/pallas_call | solution.py:957
  277.2 13.3 %finish.1 = (f32[8,208,768]{2,1,0:T(8,128)}, bf16[8,208,768]{2,1,0:T(8,128)(2,1)}, f32[768,768]{1,0:T(8,128)}, f32[768,768]{1,0:T(8,128)}, f32[576,768]{1,0:T(8,...) custom-call(f32[8,208,768]{2,1,0:T(8,128)} %get-tuple-element.57.tg_in, bf16[8,208,768]{2,1,0:T(8,128)(2,1)} %get-tuple-element.58.out_in, ...), custom_call_target="tpu_custom_call" | custom-call | tf_op jit(solution)/shard_map/finish/pallas_call | solution.py:1011
  290.5 0.9 slice_bitcast_fusion
  291.4 0.2 rev.7
  291.6 0.1 reshape.151
  291.7 0.8 slice_reduce_fusion
  292.5 0.1 reshape.152
  292.6 0.1 copy.47
  292.7 0.7 pad_maximum_fusion.2
  293.4 1.7 slice_reduce_fusion.3
  295.1 0.6 convert_multiply_fusion
  295.7 0.6 convert_multiply_fusion.1
  296.3 0.6 slice_reduce_fusion.1
  296.9 1.3 fusion
  (53 shorter events, 0.4 us)
Async XLA Ops:
  0.7 3.9 %copy-start.15 = (bf16[192]{0:T(256)(128)(2,1)S(1)}, bf16[192]{0:T(256)(128)(2,1)}, u32[]{:S(2)}) copy-start(bf16[192]{0:T(256)(128)(2,1)} %param.24) | copy-start | bytes 1156
  0.7 3.8 %copy-start.16 = (bf16[192]{0:T(256)(128)(2,1)S(1)}, bf16[192]{0:T(256)(128)(2,1)}, u32[]{:S(2)}) copy-start(bf16[192]{0:T(256)(128)(2,1)} %param.25) | copy-start | bytes 1156
  0.7 3.9 %copy-start.1 = (bf16[3,2212]{1,0:T(4,128)(2,1)S(1)}, bf16[3,2212]{1,0:T(4,128)(2,1)}, u32[]{:S(2)}) copy-start(bf16[3,2212]{1,0:T(4,128)(2,1)} %param.26) | copy-start | bytes 39820
  0.7 4.1 %copy-start.7 = (bf16[768]{0:T(1024)(128)(2,1)S(1)}, bf16[768]{0:T(1024)(128)(2,1)}, u32[]{:S(2)}) copy-start(bf16[768]{0:T(1024)(128)(2,1)} %param.33) | copy-start | bytes 4612
  0.7 4.9 %copy-start.14 = (s32[8,2]{0,1:T(2,128)S(1)}, s32[8,2]{0,1:T(2,128)}, u32[]{:S(2)}) copy-start(s32[8,2]{0,1:T(2,128)} %param.20) | copy-start | bytes 196
  0.7 5.6 %copy-start.8 = (bf16[768]{0:T(1024)(128)(2,1)S(1)}, bf16[768]{0:T(1024)(128)(2,1)}, u32[]{:S(2)}) copy-start(bf16[768]{0:T(1024)(128)(2,1)} %param.21) | copy-start | bytes 4612
  0.7 6.2 %copy-start.9 = (bf16[768]{0:T(1024)(128)(2,1)S(1)}, bf16[768]{0:T(1024)(128)(2,1)}, u32[]{:S(2)}) copy-start(bf16[768]{0:T(1024)(128)(2,1)} %param.22) | copy-start | bytes 4612
  0.7 7.8 %copy-start.10 = (bf16[768]{0:T(1024)(128)(2,1)S(1)}, bf16[768]{0:T(1024)(128)(2,1)}, u32[]{:S(2)}) copy-start(bf16[768]{0:T(1024)(128)(2,1)} %param.28) | copy-start | bytes 4612
  2.1 7.0 %copy-start = (bf16[768,768]{1,0:T(8,128)(2,1)}, bf16[768,768]{1,0:T(8,128)(2,1)S(1)}, u32[]{:S(2)}) copy-start(bf16[768,768]{1,0:T(8,128)(2,1)S(1)} %pad_maximum_fusion.own_ref) | copy-start | bytes 3538948
  7.8 107.9 %copy-start.6 = (bf16[768]{0:T(1024)(128)(2,1)S(1)}, bf16[768]{0:T(1024)(128)(2,1)}, u32[]{:S(2)}) copy-start(bf16[768]{0:T(1024)(128)(2,1)} %param.29) | copy-start | bytes 4612
  7.8 107.9 %copy-start.5 = (bf16[768]{0:T(1024)(128)(2,1)S(1)}, bf16[768]{0:T(1024)(128)(2,1)}, u32[]{:S(2)}) copy-start(bf16[768]{0:T(1024)(128)(2,1)} %param.36) | copy-start | bytes 4612
  7.8 107.9 %copy-start.11 = (bf16[768]{0:T(1024)(128)(2,1)S(1)}, bf16[768]{0:T(1024)(128)(2,1)}, u32[]{:S(2)}) copy-start(bf16[768]{0:T(1024)(128)(2,1)} %param.30) | copy-start | bytes 4612
  7.8 107.9 %copy-start.12 = (bf16[768]{0:T(1024)(128)(2,1)S(1)}, bf16[768]{0:T(1024)(128)(2,1)}, u32[]{:S(2)}) copy-start(bf16[768]{0:T(1024)(128)(2,1)} %param.31) | copy-start | bytes 4612
  7.9 107.9 %copy-start.13 = (bf16[768]{0:T(1024)(128)(2,1)S(1)}, bf16[768]{0:T(1024)(128)(2,1)}, u32[]{:S(2)}) copy-start(bf16[768]{0:T(1024)(128)(2,1)} %param.35) | copy-start | bytes 4612
  116.4 80.7 %copy-start.3 = (f32[1,768]{1,0:T(1,128)S(1)}, f32[1,768]{1,0:T(1,128)}, u32[]{:S(2)}) copy-start(f32[1,768]{1,0:T(1,128)} %reshape.154.gain_ref) | copy-start | bytes 9220
  116.4 80.7 %copy-start.4 = (f32[1,768]{1,0:T(1,128)S(1)}, f32[1,768]{1,0:T(1,128)}, u32[]{:S(2)}) copy-start(f32[1,768]{1,0:T(1,128)} %reshape.156.shift_ref) | copy-start | bytes 9220
  277.2 19.1 %copy-start.2 = (f32[16,768]{1,0:T(8,128)S(1)}, f32[16,768]{1,0:T(8,128)}, u32[]{:S(2)}) copy-start(f32[16,768]{1,0:T(8,128)} %get-tuple-element.64) | copy-start | bytes 147460
